TPU v7x, 768 devices: a whole 4x8x12 slice. The times are simulated.
768 devices in a mesh: space: 48 (over z, x_hi, core), vel: 16 (over x_lo, y).
Axes of the slice: x: 4 (x_hi: 2, x_lo: 2; x = x_hi * 2 + x_lo), y: 8, z: 12, core: 2. Of those that a mesh axis runs over, the one named last changes fastest.
Arguments:
- distribution: float32 [384, 4, 4, 2, 16384], P('space', None, None, None, 'vel'), may hold values from 0 to 15, as said below
Outputs:
- evolved: float32 [384, 4, 4, 2, 16384], P('space', None, None, None, 'vel')
Inputs may be any that keep to these rules, and one draw needn't show every extreme that they name: `distribution`: every entry is non-negative.
All inputs are finite; a program needn't handle non-finite values.
Results may differ from a plain program's by a relative error of at most 0.0001.
Values sent between devices are 32-bit elements; how exact they have to be, the bound alone decides.
No kernel may reach another device: no remote copies, remote signals or barrier semaphores. Data moves between devices by JAX's collectives and lax.ppermute only.
A program may use at most 32 MiB of HBM per device.

v0:
```python
import math

import jax
import jax.numpy as jnp
from jax import lax
from jax.sharding import PartitionSpec as P

NV = 32
STEPS = 3


speed_limit = 8.0
courant = 1.9
diffusivity_ratio = 2.0 / 3.0
encounter_rate = 0.7
shear_power_index = 0.75


def extended(cells, sides, width):
    for axis, dim in sides:
        count = lax.axis_size(axis)
        ends = count - 1
        head = lax.slice_in_dim(cells, 0, width, axis=dim)
        tail = lax.slice_in_dim(cells, cells.shape[dim] - width, cells.shape[dim], axis=dim)
        cells = jnp.concatenate(
            [
                lax.ppermute(tail, axis, [(i, (i + 1) % count) for i in range(ends)]),
                cells,
                lax.ppermute(head, axis, [((i + 1) % count, i) for i in range(ends)]),
            ],
            axis=dim,
        )
    return cells


def velocity_table(offset, velocities):
    spacing = 2.0 * speed_limit / NV
    flat_index = offset + jnp.arange(velocities, dtype=jnp.int32)
    xlevel = (flat_index // (NV * NV)).astype(jnp.float32)
    ylevel = (flat_index // NV % NV).astype(jnp.float32)
    zlevel = (flat_index % NV).astype(jnp.float32)
    direction = (2 * jnp.arange(2, dtype=jnp.int32) - 1).astype(jnp.float32)[:, None]
    xspeed = direction * ((xlevel + 0.5) * spacing)[None, :]
    yspeed = jnp.broadcast_to((-speed_limit + (ylevel + 0.5) * spacing)[None, :], xspeed.shape)
    zspeed = jnp.broadcast_to((-speed_limit + (zlevel + 0.5) * spacing)[None, :], xspeed.shape)
    return (xspeed, yspeed, zspeed)


def moment_weights(xspeed, yspeed, zspeed):
    spacing = 2.0 * speed_limit / NV
    quadrature = spacing**3 / (2.0 * math.pi) ** 1.5
    square = xspeed * xspeed + yspeed * yspeed + zspeed * zspeed
    rows = [
        jnp.ones_like(xspeed),
        xspeed,
        yspeed,
        zspeed,
        xspeed * xspeed,
        yspeed * yspeed,
        zspeed * zspeed,
        xspeed * yspeed,
        xspeed * zspeed,
        yspeed * zspeed,
        xspeed * square,
        yspeed * square,
        zspeed * square,
    ]
    return quadrature * jnp.stack(rows)


def moments_of(current, weights):
    flat = current.reshape(-1, weights.shape[1] * weights.shape[2])
    table = weights.reshape(weights.shape[0], -1)
    return lax.dot_general(
        table,
        flat,
        (((1,), (1,)), ((), ())),
        precision=lax.Precision.HIGHEST,
        preferred_element_type=jnp.float32,
    )


def cell_fields(moments):
    matter_concentration = moments[0]
    impulse_first_axis = moments[1] / matter_concentration
    impulse_second_axis = moments[2] / matter_concentration
    impulse_third_axis = moments[3] / matter_concentration
    whole_internal_work = moments[4] + moments[5] + moments[6]
    velocity_norm_power = (
        impulse_first_axis * impulse_first_axis
        + impulse_second_axis * impulse_second_axis
        + impulse_third_axis * impulse_third_axis
    )
    thermal_state = (whole_internal_work / matter_concentration - velocity_norm_power) / 3.0
    along_flow = (
        impulse_first_axis * moments[1]
        + impulse_second_axis * moments[2]
        + impulse_third_axis * moments[3]
    )
    xheating = 0.5 * (
        moments[10]
        - 2.0
        * (
            impulse_first_axis * moments[4]
            + impulse_second_axis * moments[7]
            + impulse_third_axis * moments[8]
        )
        - impulse_first_axis * whole_internal_work
        + velocity_norm_power * moments[1]
        + 2.0 * impulse_first_axis * along_flow
        - impulse_first_axis * velocity_norm_power * matter_concentration
    )
    yheating = 0.5 * (
        moments[11]
        - 2.0
        * (
            impulse_first_axis * moments[7]
            + impulse_second_axis * moments[5]
            + impulse_third_axis * moments[9]
        )
        - impulse_second_axis * whole_internal_work
        + velocity_norm_power * moments[2]
        + 2.0 * impulse_second_axis * along_flow
        - impulse_second_axis * velocity_norm_power * matter_concentration
    )
    zheating = 0.5 * (
        moments[12]
        - 2.0
        * (
            impulse_first_axis * moments[8]
            + impulse_second_axis * moments[9]
            + impulse_third_axis * moments[6]
        )
        - impulse_third_axis * whole_internal_work
        + velocity_norm_power * moments[3]
        + 2.0 * impulse_third_axis * along_flow
        - impulse_third_axis * velocity_norm_power * matter_concentration
    )
    normal_stress_level = matter_concentration * thermal_state
    conduction_factor = (1.0 - diffusivity_ratio) / (5.0 * normal_stress_level * thermal_state)
    perturbation_height = matter_concentration * thermal_state ** (-1.5)
    surviving_share = jnp.exp(
        -encounter_rate * matter_concentration * thermal_state ** (1.0 - shear_power_index)
    )
    return jnp.stack(
        [
            perturbation_height,
            impulse_first_axis,
            impulse_second_axis,
            impulse_third_axis,
            1.0 / thermal_state,
            conduction_factor * xheating,
            conduction_factor * yheating,
            conduction_factor * zheating,
            surviving_share,
        ]
    )


def collide(current, fields, xspeed, yspeed, zspeed):

    def field(which):
        return fields[which][..., None, None]

    xdrift = xspeed - field(1)
    ydrift = yspeed - field(2)
    zdrift = zspeed - field(3)
    energy = (xdrift * xdrift + ydrift * ydrift + zdrift * zdrift) * field(4)
    heat_term = xdrift * field(5) + ydrift * field(6) + zdrift * field(7)
    target = field(0) * jnp.exp(-0.5 * energy) * (1.0 + heat_term * (energy - 5.0))
    return target + (current - target) * field(8)


def sweep_shares(speed):
    courant_ratio = courant / ((NV - 1) * speed_limit / NV)
    fraction = courant_ratio * jnp.abs(speed)
    own_share = (1.0 - fraction) * (1.0 - 0.5 * fraction)
    near_share = fraction * (2.0 - fraction)
    far_share = 0.5 * fraction * (fraction - 1.0)
    forward = speed > 0.0
    nothing = jnp.zeros_like(speed)
    return (
        own_share,
        jnp.where(forward, near_share, nothing),
        jnp.where(forward, far_share, nothing),
        jnp.where(forward, nothing, near_share),
        jnp.where(forward, nothing, far_share),
    )


def periodic_sweep(current, shares, along):
    own_share, near_back, far_back, near_front, far_front = shares
    return (
        own_share * current
        + near_back * jnp.roll(current, 1, along)
        + far_back * jnp.roll(current, 2, along)
        + near_front * jnp.roll(current, -1, along)
        + far_front * jnp.roll(current, -2, along)
    )


def local(distribution):
    layers, breadth, height, halves, velocities = distribution.shape
    offset = lax.axis_index("vel") * velocities
    xspeed, yspeed, zspeed = velocity_table(offset, velocities)
    weights = moment_weights(xspeed, yspeed, zspeed)
    xshares = sweep_shares(xspeed)
    yshares = sweep_shares(yspeed)
    zshares = sweep_shares(zspeed)
    own_share, near_back, far_back, near_front, far_front = xshares
    current = distribution
    for repeat in range(STEPS):
        partial_value = moments_of(current, weights)
        owned_moments = lax.psum_scatter(partial_value, "vel", scatter_dimension=1, tiled=True)
        fields = lax.all_gather(cell_fields(owned_moments), "vel", axis=1, tiled=True)
        fields = fields.reshape(9, layers, breadth, height)
        relaxed = collide(current, fields, xspeed, yspeed, zspeed)
        padded = extended(relaxed, (("space", 0),), 2)
        moved = (
            own_share * padded[2 : layers + 2]
            + near_back * padded[1 : layers + 1]
            + far_back * padded[0:layers]
            + near_front * padded[3 : layers + 3]
            + far_front * padded[4 : layers + 4]
        )
        moved = periodic_sweep(moved, yshares, 1)
        current = periodic_sweep(moved, zshares, 2)
    return current


def solution(mesh):
    return jax.shard_map(
        local,
        mesh=mesh,
        in_specs=(P("space", None, None, None, "vel"),),
        out_specs=P("space", None, None, None, "vel"),
        check_vma=False,
    )
```

profile of v0, /device:TPU:205, one launch (start us, length us, event | category | flops | bytes accessed | tf_op | source)
XLA Modules:
  0.0 374.5 jit_solution(9416813949199954724)
XLA Ops:
  0.5 1.6 copy.9
  2.1 0.2 stack.26
  2.3 1.0 fusion.82
  3.3 46.4 %all-reduce = f32[13,128]{0,1:T(8,128)S(1)} all-reduce(f32[13,128]{0,1:T(8,128)S(1)} %fusion.82), channel_id=2, replica_groups=mesh['space'=48,'vel'=16] {'vel'}, use_global_device_ids=true, to_apply=%region_0.1.clone | all-reduce | flops 1664 | bytes 13312
  49.7 1.3 dynamic-slice
  52.0 26.9 %all_gather.9 = f32[9,128]{0,1:T(8,128)S(1)} all-gather(f32[9,8]{0,1:T(8,128)S(1)} %stack.27), channel_id=1, replica_groups=mesh['space'=48,'vel'=16] {'vel'}, dimensions={1}, use_global_device_ids=true | all-gather | bytes 4896 | tf_op jit(solution)/shard_map/all_gather | solution.py:215
  78.9 0.4 slice_reduce_fusion.26
  79.5 0.1 mul.1625
  80.5 4.0 %multiply_add_fusion.2 = f32[8,4,4,2,1024]{4,3,2,1,0:T(2,128)S(1)} fusion(f32[8,4,4,2,1024]{4,3,2,1,0:T(2,128)S(1)} %copy-done, f32[8,4,4]{2,1,0:T(4,128)S(1)} %mul.1625, f32[8,4,4]{2,1,0:T(4,128)S(1)} %mul.1620, f32[8,4,4]{2,1,0:T(4,128)S(1)} %mul.1617, f32[8,4,4]{2,1,0:T(4,128)S(1)} %mul.1614, f32[8,4,4]{2,1,0:T(4,128)S(1)} %mul.1609, ...), kind=kLoop, calls=%fused_computation.134 | loop fusion | flops 6029312 | bytes 2118144 | tf_op jit(solution)/shard_map/add | solution.py:171
  84.5 26.9 %collective-permute-start = (f32[2,4,4,2,1024]{4,3,2,1,0:T(2,128)S(1)}, f32[2,4,4,2,1024]{4,3,2,1,0:T(2,128)S(1)}, u32[]{:S(2)}, u32[]{:S(2)}) collective-permute-start(f32[2,4,4,2,1024]{4,3,2,1,0:T(2,128)S(1)} %get-tuple-element.93), channel_id=1, source_target_pairs={{0,16},{16,32},{32,48},{48,64},{64,80},{80,96},{96,112},{112,128},... | collective-permute-start | bytes 786440 | tf_op jit(solution)/shard_map/ppermute | solution.py:27
  111.4 1.9 collective-permute-start.1
  113.5 1.2 collective-permute-done
  114.7 8.0 %collective-permute-done.1 = f32[2,4,4,2,1024]{4,3,2,1,0:T(2,128)S(1)} collective-permute-done((f32[2,4,4,2,1024]{4,3,2,1,0:T(2,128)S(1)}, f32[2,4,4,2,1024]{4,3,2,1,0:T(2,128)S(1)}, u32[]{:S(2)}, u32[]{:S(2)}) %collective-permute-start.1) | collective-permute-done | bytes 262176 | tf_op jit(solution)/shard_map/ppermute | solution.py:29
  122.7 2.9 fusion.19
  125.8 1.0 fusion.138
  126.8 2.1 fusion.57
  129.1 0.6 fusion.135
  129.7 1.9 fusion.61
  131.6 0.3 copy.10
  132.0 1.0 fusion.80
  132.9 44.3 %all-reduce.1 = f32[13,128]{0,1:T(8,128)S(1)} all-reduce(f32[13,128]{0,1:T(8,128)S(1)} %fusion.80), channel_id=3, replica_groups=mesh['space'=48,'vel'=16] {'vel'}, use_global_device_ids=true, to_apply=%region_1.2.clone | all-reduce | flops 1664 | bytes 13312
  177.7 26.7 %all_gather.10 = f32[9,128]{0,1:T(8,128)S(1)} all-gather(f32[9,8]{0,1:T(8,128)S(1)} %stack.28), channel_id=1, replica_groups=mesh['space'=48,'vel'=16] {'vel'}, dimensions={1}, use_global_device_ids=true | all-gather | bytes 4896 | tf_op jit(solution)/shard_map/all_gather | solution.py:215
  204.4 0.4 slice_reduce_fusion.17
  205.9 4.0 %multiply_add_fusion.1 = f32[8,4,4,2,1024]{4,3,2,1,0:T(2,128)S(1)} fusion(f32[8,4,4,2,1024]{4,3,2,1,0:T(2,128)S(1)} %fusion.61, f32[8,4,4]{2,1,0:T(4,128)S(1)} %mul.1730, f32[8,4,4]{2,1,0:T(4,128)S(1)} %mul.1725, f32[8,4,4]{2,1,0:T(4,128)S(1)} %mul.1722, f32[8,4,4]{2,1,0:T(4,128)S(1)} %mul.1719, f32[8,4,4]{2,1,0:T(4,128)S(1)} %mul.1714, ...), kind=kLoop, calls=%fused_computation.133 | loop fusion | flops 6029312 | bytes 2118144 | tf_op jit(solution)/shard_map/add | solution.py:171
  210.0 22.4 %collective-permute-start.2 = (f32[2,4,4,2,1024]{4,3,2,1,0:T(2,128)S(1)}, f32[2,4,4,2,1024]{4,3,2,1,0:T(2,128)S(1)}, u32[]{:S(2)}, u32[]{:S(2)}) collective-permute-start(f32[2,4,4,2,1024]{4,3,2,1,0:T(2,128)S(1)} %get-tuple-element.79), channel_id=1, source_target_pairs={{0,16},{16,32},{32,48},{48,64},{64,80},{80,96},{96,112},{112,128},... | collective-permute-start | bytes 786440 | tf_op jit(solution)/shard_map/ppermute | solution.py:27
  232.4 2.1 collective-permute-start.3
  234.5 1.2 collective-permute-done.2
  235.7 8.2 %collective-permute-done.3 = f32[2,4,4,2,1024]{4,3,2,1,0:T(2,128)S(1)} collective-permute-done((f32[2,4,4,2,1024]{4,3,2,1,0:T(2,128)S(1)}, f32[2,4,4,2,1024]{4,3,2,1,0:T(2,128)S(1)}, u32[]{:S(2)}, u32[]{:S(2)}) %collective-permute-start.3) | collective-permute-done | bytes 262176 | tf_op jit(solution)/shard_map/ppermute | solution.py:29
  243.8 2.9 fusion.11
  246.9 1.0 fusion.131
  248.0 2.1 fusion.65
  250.2 0.6 fusion.128
  250.8 1.9 fusion.69
  252.7 0.3 copy.11
  253.1 1.0 fusion.78
  254.0 44.6 %all-reduce.2 = f32[13,128]{0,1:T(8,128)S(1)} all-reduce(f32[13,128]{0,1:T(8,128)S(1)} %fusion.78), channel_id=4, replica_groups=mesh['space'=48,'vel'=16] {'vel'}, use_global_device_ids=true, to_apply=%region_2.3.clone | all-reduce | flops 1664 | bytes 13312
  299.1 26.6 %all_gather.11 = f32[9,128]{0,1:T(8,128)S(1)} all-gather(f32[9,8]{0,1:T(8,128)S(1)} %stack.29), channel_id=1, replica_groups=mesh['space'=48,'vel'=16] {'vel'}, dimensions={1}, use_global_device_ids=true | all-gather | bytes 4896 | tf_op jit(solution)/shard_map/all_gather | solution.py:215
  325.7 0.4 slice_reduce_fusion.8
  327.2 4.0 %multiply_add_fusion = f32[8,4,4,2,1024]{4,3,2,1,0:T(2,128)S(1)} fusion(f32[8,4,4,2,1024]{4,3,2,1,0:T(2,128)S(1)} %fusion.69, f32[8,4,4]{2,1,0:T(4,128)S(1)} %mul.1817, f32[8,4,4]{2,1,0:T(4,128)S(1)} %mul.1812, f32[8,4,4]{2,1,0:T(4,128)S(1)} %mul.1809, f32[8,4,4]{2,1,0:T(4,128)S(1)} %mul.1806, f32[8,4,4]{2,1,0:T(4,128)S(1)} %mul.1801, ...), kind=kLoop, calls=%fused_computation.132 | loop fusion | flops 6029312 | bytes 2118144 | tf_op jit(solution)/shard_map/add | solution.py:171
  331.3 22.2 %collective-permute-start.4 = (f32[2,4,4,2,1024]{4,3,2,1,0:T(2,128)S(1)}, f32[2,4,4,2,1024]{4,3,2,1,0:T(2,128)S(1)}, u32[]{:S(2)}, u32[]{:S(2)}) collective-permute-start(f32[2,4,4,2,1024]{4,3,2,1,0:T(2,128)S(1)} %get-tuple-element.65), channel_id=1, source_target_pairs={{0,16},{16,32},{32,48},{48,64},{64,80},{80,96},{96,112},{112,128},... | collective-permute-start | bytes 786440 | tf_op jit(solution)/shard_map/ppermute | solution.py:27
  353.5 1.9 collective-permute-start.5
  355.4 1.4 collective-permute-done.4
  356.8 8.0 %collective-permute-done.5 = f32[2,4,4,2,1024]{4,3,2,1,0:T(2,128)S(1)} collective-permute-done((f32[2,4,4,2,1024]{4,3,2,1,0:T(2,128)S(1)}, f32[2,4,4,2,1024]{4,3,2,1,0:T(2,128)S(1)}, u32[]{:S(2)}, u32[]{:S(2)}) %collective-permute-start.5) | collective-permute-done | bytes 262176 | tf_op jit(solution)/shard_map/ppermute | solution.py:29
  364.8 2.9 fusion.3
  367.9 1.0 fusion.124
  368.9 2.1 fusion.73
  371.2 0.6 fusion.121
  371.8 2.7 fusion.77
  (88 shorter events, 5.8 us)
Async XLA Ops:
  2.3 78.2 %copy-start = (f32[8,4,4,2,1024]{4,3,2,1,0:T(2,128)S(1)}, f32[8,4,4,2,1024]{4,3,2,1,0:T(2,128)}, u32[]{:S(2)}) copy-start(f32[8,4,4,2,1024]{4,3,2,1,0:T(2,128)} %param.1) | copy-start | bytes 3145732
  84.5 30.2 %collective-permute-start = (f32[2,4,4,2,1024]{4,3,2,1,0:T(2,128)S(1)}, f32[2,4,4,2,1024]{4,3,2,1,0:T(2,128)S(1)}, u32[]{:S(2)}, u32[]{:S(2)}) collective-permute-start(f32[2,4,4,2,1024]{4,3,2,1,0:T(2,128)S(1)} %get-tuple-element.93), channel_id=1, source_target_pairs={{0,16},{16,32},{32,48},{48,64},{64,80},{80,96},{96,112},{112,128},... | collective-permute-start | bytes 786440 | tf_op jit(solution)/shard_map/ppermute | solution.py:27
  111.4 11.3 %collective-permute-start.1 = (f32[2,4,4,2,1024]{4,3,2,1,0:T(2,128)S(1)}, f32[2,4,4,2,1024]{4,3,2,1,0:T(2,128)S(1)}, u32[]{:S(2)}, u32[]{:S(2)}) collective-permute-start(f32[2,4,4,2,1024]{4,3,2,1,0:T(2,128)S(1)} %get-tuple-element.94), channel_id=1, source_target_pairs={{16,0},{32,16},{48,32},{64,48},{80,64},{96,80},{112,96},{128,112},... | collective-permute-start | bytes 786440 | tf_op jit(solution)/shard_map/ppermute | solution.py:29
  210.0 25.7 %collective-permute-start.2 = (f32[2,4,4,2,1024]{4,3,2,1,0:T(2,128)S(1)}, f32[2,4,4,2,1024]{4,3,2,1,0:T(2,128)S(1)}, u32[]{:S(2)}, u32[]{:S(2)}) collective-permute-start(f32[2,4,4,2,1024]{4,3,2,1,0:T(2,128)S(1)} %get-tuple-element.79), channel_id=1, source_target_pairs={{0,16},{16,32},{32,48},{48,64},{64,80},{80,96},{96,112},{112,128},... | collective-permute-start | bytes 786440 | tf_op jit(solution)/shard_map/ppermute | solution.py:27
  232.4 11.5 %collective-permute-start.3 = (f32[2,4,4,2,1024]{4,3,2,1,0:T(2,128)S(1)}, f32[2,4,4,2,1024]{4,3,2,1,0:T(2,128)S(1)}, u32[]{:S(2)}, u32[]{:S(2)}) collective-permute-start(f32[2,4,4,2,1024]{4,3,2,1,0:T(2,128)S(1)} %get-tuple-element.80), channel_id=1, source_target_pairs={{16,0},{32,16},{48,32},{64,48},{80,64},{96,80},{112,96},{128,112},... | collective-permute-start | bytes 786440 | tf_op jit(solution)/shard_map/ppermute | solution.py:29
  331.3 25.5 %collective-permute-start.4 = (f32[2,4,4,2,1024]{4,3,2,1,0:T(2,128)S(1)}, f32[2,4,4,2,1024]{4,3,2,1,0:T(2,128)S(1)}, u32[]{:S(2)}, u32[]{:S(2)}) collective-permute-start(f32[2,4,4,2,1024]{4,3,2,1,0:T(2,128)S(1)} %get-tuple-element.65), channel_id=1, source_target_pairs={{0,16},{16,32},{32,48},{48,64},{64,80},{80,96},{96,112},{112,128},... | collective-permute-start | bytes 786440 | tf_op jit(solution)/shard_map/ppermute | solution.py:27
  353.5 11.3 %collective-permute-start.5 = (f32[2,4,4,2,1024]{4,3,2,1,0:T(2,128)S(1)}, f32[2,4,4,2,1024]{4,3,2,1,0:T(2,128)S(1)}, u32[]{:S(2)}, u32[]{:S(2)}) collective-permute-start(f32[2,4,4,2,1024]{4,3,2,1,0:T(2,128)S(1)} %get-tuple-element.66), channel_id=1, source_target_pairs={{16,0},{32,16},{48,32},{64,48},{80,64},{96,80},{112,96},{128,112},... | collective-permute-start | bytes 786440 | tf_op jit(solution)/shard_map/ppermute | solution.py:29
where the time goes:
time: 375 us; the launch traced here: 374 us
  blocking collectives  216 us (58%)
  starting transfers between devices  77.4 us (21%)
  other arithmetic  35 us (9%)
  waiting for transfers between devices  28 us (7%)
  local copies, waits for them, and re-layouts  14.4 us (4%)
    unnamed x3, blocking collectives  135 us
    all_gather x3, blocking collectives, local(): lax.all_gather(cell_fields(owned_moments), 'vel', axis=1, tiled=True)  80.2 us
    ppermute x3, starting transfers between devices, extended(): lax.ppermute(tail, axis, [(i, (i + 1) % count) for i in range(ends)])  71.5 us
    ppermute x3, waiting for transfers between devices, extended(): lax.ppermute(head, axis, [((i + 1) % count, i) for i in range(ends)])  24.2 us
    add x6, other arithmetic, periodic_sweep(): own_share * current + near_back * jnp.roll(current, 1, along)  12.8 us
    add x3, other arithmetic, collide(): return target + (current - target) * field(8)  12 us
    add x3, other arithmetic, local(): own_share * padded[2:layers + 2] + near_back * padded[1:layers + 1]  8.83 us
  transfers between devices with their start and end apart: 6, of which 6 were waited for; matrix products, arithmetic and copies ran while one was open for 0% of the time, Pallas kernels for 0%

commit v1 on v0

v1 whole, which is shorter than its diff:
```python
import math

import jax
import jax.numpy as jnp
from jax import lax
from jax.experimental import pallas as pl
from jax.experimental.pallas import tpu as pltpu
from jax.sharding import PartitionSpec as P


NV = 32
STEPS = 3
SPEED_LIMIT = 8.0
SPACING = 2.0 * SPEED_LIMIT / NV
LAM = 1.9 / ((NV - 1) * SPEED_LIMIT / NV)
QUAD = SPACING**3 / (2.0 * math.pi) ** 1.5
LOG2E = math.log2(math.e)
NYZ, CELLS = 16, 128
HIGHEST = lax.Precision.HIGHEST
VMEM = pl.BlockSpec(memory_space=pltpu.VMEM)
TILE = (8, 128)


def iota(axis):
    return lax.broadcasted_iota(jnp.int32, TILE, axis)


def shares(speed):
    n = LAM * jnp.abs(speed)
    return (1.0 - n) * (1.0 - 0.5 * n), n * (2.0 - n), 0.5 * n * (n - 1.0)


def yspeed(block):
    return -SPEED_LIMIT + ((4 * block + iota(1) // 32).astype(jnp.float32) + 0.5) * SPACING


def zspeed():
    return -SPEED_LIMIT + ((iota(1) % 32).astype(jnp.float32) + 0.5) * SPACING


def sweep_yz(cells, ycoef, zcoef, zforward, yforward):
    step = -1 if yforward else 1
    ya, yb, yc = ycoef
    za, zb, zc = zcoef
    mid = [
        [
            ya * cells[y][z] + yb * cells[(y + step) % 4][z] + yc * cells[(y + 2) % 4][z]
            for z in range(4)
        ]
        for y in range(4)
    ]
    return [
        [
            za * mid[y][z]
            + zb * jnp.where(zforward, mid[y][(z - 1) % 4], mid[y][(z + 1) % 4])
            + zc * mid[y][(z + 2) % 4]
            for z in range(4)
        ]
        for y in range(4)
    ]


def moments_into(g_ref, w_ref, m_ref):
    m_ref[...] = lax.dot_general(
        w_ref[...],
        g_ref[...],
        (((1,), (1,)), ((), ())),
        precision=HIGHEST,
        preferred_element_type=jnp.float32,
    )


def xabs_here():
    index = jnp.full(TILE, lax.axis_index("vel"), jnp.int32)
    return (index.astype(jnp.float32) + 0.5) * SPACING


def even_here():
    return lax.axis_index("space") % 2 == 0


def first_kernel(d_ref, g_ref, w_ref, m_ref):
    for block in range(8):
        for half in range(2):
            lanes = pl.ds(half * 1024 + block * 128, 128)
            for yz in range(NYZ):
                rows = pl.ds(yz * 16 + block * 2 + half, 8, stride=256)
                g_ref[pl.ds(yz * 8, 8), lanes] = d_ref[rows, :]
    xabs = xabs_here()
    zs = zspeed()
    row = iota(0)
    for half in range(2):
        xs = xabs if half else -xabs
        for block in range(8):
            ys = yspeed(block)
            square = xs * xs + ys * ys + zs * zs
            lanes = pl.ds(half * 1024 + block * 128, 128)
            low = [jnp.ones_like(xs), xs, ys, zs, xs * xs, ys * ys, zs * zs, xs * ys]
            high = [xs * zs, ys * zs, xs * square, ys * square, zs * square]
            for base, rows in ((0, low), (8, high)):
                tile = jnp.zeros(TILE, jnp.float32)
                for i, r in enumerate(rows):
                    tile = jnp.where(row == i, r, tile)
                w_ref[pl.ds(base, 8), lanes] = QUAD * tile
    moments_into(g_ref, w_ref, m_ref)


def cell_fields(m):
    rho = m[0]
    inv_rho = 1.0 / rho
    ux, uy, uz = m[1] * inv_rho, m[2] * inv_rho, m[3] * inv_rho
    energy = m[4] + m[5] + m[6]
    norm = ux * ux + uy * uy + uz * uz
    temp = (energy * inv_rho - norm) / 3.0
    along = ux * m[1] + uy * m[2] + uz * m[3]

    def heating(third, u, first, r0, r1, r2):
        return 0.5 * (
            third
            - 2.0 * (ux * r0 + uy * r1 + uz * r2)
            - u * energy
            + norm * first
            + 2.0 * u * along
            - u * norm * rho
        )

    xq = heating(m[10], ux, m[1], m[4], m[7], m[8])
    yq = heating(m[11], uy, m[2], m[7], m[5], m[9])
    zq = heating(m[12], uz, m[3], m[8], m[9], m[6])
    root = jnp.sqrt(temp)
    conduction = (1.0 / 3.0) / (5.0 * rho * temp * temp)
    amp = rho / (temp * root)
    retain = jnp.exp(-0.7 * rho * jnp.sqrt(root))
    k = -0.5 * LOG2E
    fold = conduction / k
    return [ux, uy, uz, k / temp, fold * xq, fold * yq, fold * zq, amp * (1.0 - retain), retain]


class Cell:
    def __init__(self, tile, xabs, zs):
        (self.ux, self.uy, uz, self.scale, self.qx, self.qy, qz, self.amp, self.retain) = [
            jnp.broadcast_to(tile[:, k : k + 1], TILE) for k in range(9)
        ]
        zd = zs - uz
        self.ez, self.hz = zd * zd * self.scale, zd * qz
        self.x = []
        for xs in (-xabs, xabs):
            xd = xs - self.ux
            self.x.append((xd * xd * self.scale, xd * self.qx))

    def yz(self, block):
        yd = yspeed(block) - self.uy
        return yd * yd * self.scale + self.ez, yd * self.qy + self.hz

    def relax(self, half, yz, current):
        e = self.x[half][0] + yz[0]
        h = self.x[half][1] + yz[1]
        return self.amp * (jnp.exp2(e) * (1.0 + h * (e + 2.5 * LOG2E))) + self.retain * current


def xmask(half, far):
    row = iota(0)
    return (row < 1 + far) if half else (row > 6 - far)


def rotated(relaxed, half):
    return pltpu.roll(relaxed, 1 if half else 7, 0), pltpu.roll(relaxed, 2 if half else 6, 0)


def placed(out, half, z):
    shift = (2 * z if half else 2 * z + 2) % 8
    return pltpu.roll(out, shift, 0) if shift else out


def outer_kernel(a_ref, g_ref, f_ref, mb_ref):
    total = a_ref[0]
    for peer in range(1, a_ref.shape[0]):
        total = total + a_ref[peer]
    fields = cell_fields([total[k : k + 1, :] for k in range(13)])
    for k, value in enumerate(fields):
        f_ref[k : k + 1, :] = value
    f_ref[...] = jnp.transpose(f_ref[...])
    xabs = xabs_here()
    _, near, far = shares(xabs)
    zero = jnp.zeros(TILE, jnp.float32)
    zs = zspeed()

    def message(half):
        n_out = jnp.where(xmask(half, 0), near, zero)
        f_out = jnp.where(xmask(half, 1), far, zero)

        def per_y(y, carry):
            packed = [zero] * 8
            for z in range(4):
                rows = pl.ds(pl.multiple_of(y * 32 + z * 8, 8), 8)
                cell = Cell(f_ref[rows, :], xabs, zs)
                for block in range(8):
                    relaxed = cell.relax(half, cell.yz(block), g_ref[rows, pl.ds(half * 1024 + block * 128, 128)])
                    r1, r2 = rotated(relaxed, half)
                    packed[block] = packed[block] + placed(n_out * r1 + f_out * r2, half, z)
            for block in range(8):
                mb_ref[pl.ds(pl.multiple_of(y * 8, 8), 8), pl.ds(block * 128, 128)] = packed[block]
            return carry

        lax.fori_loop(0, 4, per_y, 0)

    even = even_here()
    pl.when(even)(lambda: message(0))
    pl.when(jnp.logical_not(even))(lambda: message(1))


def inner_kernel(f_ref, g_ref, l_ref, ma_ref):
    xabs = xabs_here()
    own, near, far = shares(xabs)
    zero = jnp.zeros(TILE, jnp.float32)
    zs = zspeed()
    inside = [
        (jnp.where(xmask(half, 0), zero, near), jnp.where(xmask(half, 1), zero, far)) for half in range(2)
    ]

    def slab(sent):
        n_out = jnp.where(xmask(sent, 0), near, zero)
        f_out = jnp.where(xmask(sent, 1), far, zero)

        def per_y(y, carry):
            packed = [zero] * 8
            for z in range(4):
                rows = pl.ds(pl.multiple_of(y * 32 + z * 8, 8), 8)
                cell = Cell(f_ref[rows, :], xabs, zs)
                for block in range(8):
                    yz = cell.yz(block)
                    for half in range(2):
                        lanes = pl.ds(half * 1024 + block * 128, 128)
                        relaxed = cell.relax(half, yz, g_ref[rows, lanes])
                        r1, r2 = rotated(relaxed, half)
                        n_in, f_in = inside[half]
                        l_ref[rows, lanes] = own * relaxed + n_in * r1 + f_in * r2
                        if half == sent:
                            packed[block] = packed[block] + placed(n_out * r1 + f_out * r2, half, z)
            for block in range(8):
                ma_ref[pl.ds(pl.multiple_of(y * 8, 8), 8), pl.ds(block * 128, 128)] = packed[block]
            return carry

        lax.fori_loop(0, 4, per_y, 0)

    even = even_here()
    pl.when(even)(lambda: slab(1))
    pl.when(jnp.logical_not(even))(lambda: slab(0))


def sweep_kernel(l_ref, g_ref):
    zs = zspeed()
    zcoef = shares(zs)
    zforward = zs > 0.0
    for block in range(8):
        ycoef = shares(yspeed(block))
        for half in range(2):
            lanes = pl.ds(half * 1024 + block * 128, 128)
            cells = [[l_ref[pl.ds((4 * y + z) * 8, 8), lanes] for z in range(4)] for y in range(4)]
            done = sweep_yz(cells, ycoef, zcoef, zforward, block >= 4)
            for y in range(4):
                for z in range(4):
                    g_ref[pl.ds((4 * y + z) * 8, 8), lanes] = done[y][z]


def edges(g_ref, ra_ref, rb_ref, store):
    even = jnp.full(TILE, (lax.axis_index("space") + 1) % 2, jnp.int32) > 0
    zero = jnp.zeros(TILE, jnp.float32)
    zs = zspeed()
    za, zb, zc = shares(zs)
    zforward = zs > 0.0
    for block in range(8):
        ya, yb, yc = shares(yspeed(block))
        step = -1 if block >= 4 else 1
        for half in range(2):
            cells = []
            for y in range(4):
                a, b = [r[pl.ds(y * 8, 8), pl.ds(block * 128, 128)] for r in (ra_ref, rb_ref)]
                cells.append(jnp.where(even, b, a) if half else jnp.where(even, a, b))
            for y in range(4):
                mid = ya * cells[y] + yb * cells[(y + step) % 4] + yc * cells[(y + 2) % 4]
                near = jnp.where(zforward, pltpu.roll(mid, 2, 0), pltpu.roll(mid, 6, 0))
                done = za * mid + zb * near + zc * pltpu.roll(mid, 4, 0)
                for z in range(4):
                    shift = (-2 * z if half else 6 - 2 * z) % 8
                    part = pltpu.roll(done, shift, 0) if shift else done
                    rows = pl.ds((4 * y + z) * 8, 8)
                    lanes = pl.ds(half * 1024 + block * 128, 128)
                    value = g_ref[rows, lanes] + jnp.where(xmask(half, 1), part, zero)
                    store(4 * y + z, half, block, value)


def edge_kernel(g_ref, ra_ref, rb_ref, w_ref, o_ref, m_ref):
    def store(yz, half, block, value):
        o_ref[pl.ds(yz * 8, 8), pl.ds(half * 1024 + block * 128, 128)] = value

    edges(g_ref, ra_ref, rb_ref, store)
    moments_into(o_ref, w_ref, m_ref)


def last_kernel(g_ref, ra_ref, rb_ref, o_ref):
    def store(yz, half, block, value):
        o_ref[pl.ds(yz * 16 + block * 2 + half, 8, stride=256), :] = value

    edges(g_ref, ra_ref, rb_ref, store)


def call(kernel, outs, **kw):
    shapes = [pltpu.VMEM(s, jnp.float32) for s in outs]
    return lambda *args: pl.pallas_call(
        kernel, out_shape=shapes, in_specs=[VMEM] * len(args), out_specs=[VMEM] * len(outs), **kw
    )(*(pltpu.with_memory_space_constraint(a, pltpu.VMEM) for a in args))


def local(distribution):
    layers, breadth, height, halves, velocities = distribution.shape
    vel_count = lax.axis_size("vel")
    space_count = lax.axis_size("space")
    grid = (CELLS, halves * velocities)
    message = (2 * NYZ, velocities)
    stored = distribution.reshape(layers, breadth, height, halves, 8, 128).transpose(0, 1, 2, 4, 3, 5)
    stored = stored.reshape(2048, 128)
    pairs_a = [(i, i ^ 1) for i in range(space_count)]
    pairs_b = [(i, i + 1) for i in range(1, space_count - 1, 2)]
    pairs_b = pairs_b + [(j, i) for i, j in pairs_b]
    g, weights, partial_moments = call(first_kernel, [grid, (16, grid[1]), (16, CELLS)])(stored)
    for step in range(STEPS):
        everywhere = jnp.broadcast_to(partial_moments[None], (vel_count, 16, CELLS))
        gathered = lax.all_to_all(everywhere, "vel", 0, 0)
        fields, msg_b = call(outer_kernel, [(128, 128), message])(gathered, g)
        got_b = lax.ppermute(msg_b, "space", pairs_b)
        moved, msg_a = call(inner_kernel, [grid, message])(fields, g)
        got_a = lax.ppermute(msg_a, "space", pairs_a)
        (swept,) = call(sweep_kernel, [grid])(moved)
        if step + 1 < STEPS:
            g, partial_moments = call(edge_kernel, [grid, (16, CELLS)], input_output_aliases={0: 0})(
                swept, got_a, got_b, weights
            )
        else:
            (out,) = call(last_kernel, [(2048, 128)])(swept, got_a, got_b)
    out = out.reshape(layers, breadth, height, 8, halves, 128).transpose(0, 1, 2, 4, 3, 5)
    return out.reshape(distribution.shape)


def solution(mesh):
    return jax.shard_map(
        local,
        mesh=mesh,
        in_specs=(P("space", None, None, None, "vel"),),
        out_specs=P("space", None, None, None, "vel"),
        check_vma=False,
    )
```

time: 375 us -> 88.8 us (0.24)
  the two profiles are of different devices: /device:TPU:205 before, /device:TPU:512 now
where the time goes in v1:
time: 88.8 us; the launch traced here: 88.4 us
  blocking collectives  39.8 us (45%)
  starting transfers between devices  19.7 us (22%)
  waiting for transfers between devices  14.4 us (16%)
  Pallas kernels  12 us (14%)
  local copies, waits for them, and re-layouts  2.27 us (3%)
    all_to_all x3, blocking collectives, local(): gathered = lax.all_to_all(everywhere, 'vel', 0, 0)  39.8 us
    ppermute x3, waiting for transfers between devices, local(): got_b = lax.ppermute(msg_b, 'space', pairs_b)  14.4 us
    ppermute x3, starting transfers between devices, local(): got_b = lax.ppermute(msg_b, 'space', pairs_b)  14 us
    pallas_call x13, Pallas kernels, call(): pl.pallas_call(kernel, out_shape=shapes, in_specs=[VMEM] * len(args), out...  12 us
    ppermute x3, starting transfers between devices, local(): got_a = lax.ppermute(msg_a, 'space', pairs_a)  5.76 us
    unnamed x3, local copies, waits for them, and re-layouts  2.2 us
  transfers between devices with their start and end apart: 6, of which 3 were waited for; matrix products, arithmetic and copies ran while one was open for 0% of the time, Pallas kernels for 1%

profile of v1, /device:TPU:512, one launch (start us, length us, event | category | flops | bytes accessed | tf_op | source)
XLA Modules:
  0.0 88.4 jit_solution(12350857361380718195)
XLA Ops:
  0.0 0.0 copy-start
  0.0 1.2 %copy-done = f32[8,4,4,2,1024]{4,3,2,1,0:T(2,128)S(1)} copy-done((f32[8,4,4,2,1024]{4,3,2,1,0:T(2,128)S(1)}, f32[8,4,4,2,1024]{4,3,2,1,0:T(2,128)}, u32[]{:S(2)}) %copy-start) | copy-done | bytes 1048600
  1.2 1.3 %shard_map.17 = (f32[128,2048]{1,0:T(8,128)S(1)}, f32[16,2048]{1,0:T(8,128)S(1)}, f32[16,128]{1,0:T(8,128)S(1)}) custom-call(f32[2048,128]{1,0:T(8,128)S(1)} %bitcast.11), custom_call_target="tpu_custom_call" | custom-call | tf_op jit(solution)/shard_map/pallas_call | solution.py:310
  2.6 16.5 %all_to_all.15.a_ref = f32[16,16,128]{2,1,0:T(8,128)S(1)} all-to-all(f32[16,16,128]{2,1,0:T(8,128)S(1)} %broadcast_in_dim.6), channel_id=1, replica_groups=mesh['space'=48,'vel'=16] {'vel'}, dimensions={0} | all-to-all | bytes 262144 | tf_op jit(solution)/shard_map/all_to_all | solution.py:329
  19.1 0.9 %shard_map.18 = (f32[128,128]{1,0:T(8,128)S(1)}, f32[32,1024]{1,0:T(8,128)S(1)}) custom-call(f32[16,16,128]{2,1,0:T(8,128)S(1)} %all_to_all.15.a_ref, f32[128,2048]{1,0:T(8,128)S(1)} %get-tuple-element.25.g_ref), custom_call_target="tpu_custom_call" | custom-call | tf_op jit(solution)/shard_map/pallas_call | solution.py:310
  20.0 1.1 %shard_map.19 = (f32[128,2048]{1,0:T(8,128)S(1)}, f32[32,1024]{1,0:T(8,128)S(1)}) custom-call(f32[128,128]{1,0:T(8,128)S(1)} %get-tuple-element.26.f_ref, f32[128,2048]{1,0:T(8,128)S(1)} %get-tuple-element.25.g_ref), custom_call_target="tpu_custom_call" | custom-call | tf_op jit(solution)/shard_map/pallas_call | solution.py:310
  21.1 1.9 %collective-permute-start = (f32[32,1024]{1,0:T(8,128)S(1)}, f32[32,1024]{1,0:T(8,128)S(1)}, u32[]{:S(2)}, u32[]{:S(2)}) collective-permute-start(f32[32,1024]{1,0:T(8,128)S(1)} %get-tuple-element.28), channel_id=1, source_target_pairs={{0,16},{16,0},{32,48},{48,32},{64,80},{80,64},{96,112},{112,96},{1... | collective-permute-start | bytes 393224 | tf_op jit(solution)/shard_map/ppermute | solution.py:333
  23.0 5.9 %collective-permute-start.1 = (f32[32,1024]{1,0:T(8,128)S(1)}, f32[32,1024]{1,0:T(8,128)S(1)}, u32[]{:S(2)}, u32[]{:S(2)}) collective-permute-start(f32[32,1024]{1,0:T(8,128)S(1)} %get-tuple-element.29), channel_id=1, source_target_pairs={{16,32},{48,64},{80,96},{112,128},{144,160},{176,192},{208,224},{2... | collective-permute-start | bytes 393224 | tf_op jit(solution)/shard_map/ppermute | solution.py:331
  29.0 0.4 shard_map.20.g_ref
  29.4 0.0 collective-permute-done.ra_ref
  29.4 3.5 %collective-permute-done.1.rb_ref = f32[32,1024]{1,0:T(8,128)S(1)} collective-permute-done((f32[32,1024]{1,0:T(8,128)S(1)}, f32[32,1024]{1,0:T(8,128)S(1)}, u32[]{:S(2)}, u32[]{:S(2)}) %collective-permute-start.1) | collective-permute-done | bytes 131104 | tf_op jit(solution)/shard_map/ppermute | solution.py:331
  32.9 1.3 %shard_map.21 = (f32[128,2048]{1,0:T(8,128)S(1)}, f32[16,128]{1,0:T(8,128)S(1)}) custom-call(f32[128,2048]{1,0:T(8,128)S(1)} %shard_map.20.g_ref, f32[32,1024]{1,0:T(8,128)S(1)} %collective-permute-done.ra_ref, f32[32,1024]{1,0:T(8,128)S(1)} %collective-permute-done.1.rb_ref, f32[16,2048]{1,0:T(8,128)S(1)} %get-tuple-element.30.w_ref), custom_call_target="tpu_custom_call", output_to_operand_aliasing={{0}: (0, {})} | custom-call | tf_op jit(solution)/shard_map/pallas_call | solution.py:310
  34.2 11.6 %all_to_all.16.a_ref = f32[16,16,128]{2,1,0:T(8,128)S(1)} all-to-all(f32[16,16,128]{2,1,0:T(8,128)S(1)} %broadcast_in_dim.7), channel_id=1, replica_groups=mesh['space'=48,'vel'=16] {'vel'}, dimensions={0} | all-to-all | bytes 262144 | tf_op jit(solution)/shard_map/all_to_all | solution.py:329
  45.9 0.9 %shard_map.22 = (f32[128,128]{1,0:T(8,128)S(1)}, f32[32,1024]{1,0:T(8,128)S(1)}) custom-call(f32[16,16,128]{2,1,0:T(8,128)S(1)} %all_to_all.16.a_ref, f32[128,2048]{1,0:T(8,128)S(1)} %get-tuple-element.32.g_ref), custom_call_target="tpu_custom_call" | custom-call | tf_op jit(solution)/shard_map/pallas_call | solution.py:310
  46.8 1.1 %shard_map.23 = (f32[128,2048]{1,0:T(8,128)S(1)}, f32[32,1024]{1,0:T(8,128)S(1)}) custom-call(f32[128,128]{1,0:T(8,128)S(1)} %get-tuple-element.33.f_ref, f32[128,2048]{1,0:T(8,128)S(1)} %get-tuple-element.32.g_ref), custom_call_target="tpu_custom_call" | custom-call | tf_op jit(solution)/shard_map/pallas_call | solution.py:310
  47.9 1.9 %collective-permute-start.2 = (f32[32,1024]{1,0:T(8,128)S(1)}, f32[32,1024]{1,0:T(8,128)S(1)}, u32[]{:S(2)}, u32[]{:S(2)}) collective-permute-start(f32[32,1024]{1,0:T(8,128)S(1)} %get-tuple-element.35), channel_id=1, source_target_pairs={{0,16},{16,0},{32,48},{48,32},{64,80},{80,64},{96,112},{112,96},{1... | collective-permute-start | bytes 393224 | tf_op jit(solution)/shard_map/ppermute | solution.py:333
  49.8 4.6 %collective-permute-start.3 = (f32[32,1024]{1,0:T(8,128)S(1)}, f32[32,1024]{1,0:T(8,128)S(1)}, u32[]{:S(2)}, u32[]{:S(2)}) collective-permute-start(f32[32,1024]{1,0:T(8,128)S(1)} %get-tuple-element.36), channel_id=1, source_target_pairs={{16,32},{48,64},{80,96},{112,128},{144,160},{176,192},{208,224},{2... | collective-permute-start | bytes 393224 | tf_op jit(solution)/shard_map/ppermute | solution.py:331
  54.4 0.4 shard_map.24.g_ref
  54.9 0.0 collective-permute-done.2.ra_ref
  54.9 4.9 %collective-permute-done.3.rb_ref = f32[32,1024]{1,0:T(8,128)S(1)} collective-permute-done((f32[32,1024]{1,0:T(8,128)S(1)}, f32[32,1024]{1,0:T(8,128)S(1)}, u32[]{:S(2)}, u32[]{:S(2)}) %collective-permute-start.3) | collective-permute-done | bytes 131104 | tf_op jit(solution)/shard_map/ppermute | solution.py:331
  59.7 1.3 %shard_map.25 = (f32[128,2048]{1,0:T(8,128)S(1)}, f32[16,128]{1,0:T(8,128)S(1)}) custom-call(f32[128,2048]{1,0:T(8,128)S(1)} %shard_map.24.g_ref, f32[32,1024]{1,0:T(8,128)S(1)} %collective-permute-done.2.ra_ref, f32[32,1024]{1,0:T(8,128)S(1)} %collective-permute-done.3.rb_ref, f32[16,2048]{1,0:T(8,128)S(1)} %get-tuple-element.30.w_ref), custom_call_target="tpu_custom_call", output_to_operand_aliasing={{0}: (0, {})} | custom-call | tf_op jit(solution)/shard_map/pallas_call | solution.py:310
  61.1 11.6 %all_to_all.17.a_ref = f32[16,16,128]{2,1,0:T(8,128)S(1)} all-to-all(f32[16,16,128]{2,1,0:T(8,128)S(1)} %broadcast_in_dim.8), channel_id=1, replica_groups=mesh['space'=48,'vel'=16] {'vel'}, dimensions={0} | all-to-all | bytes 262144 | tf_op jit(solution)/shard_map/all_to_all | solution.py:329
  72.7 0.9 %shard_map.26 = (f32[128,128]{1,0:T(8,128)S(1)}, f32[32,1024]{1,0:T(8,128)S(1)}) custom-call(f32[16,16,128]{2,1,0:T(8,128)S(1)} %all_to_all.17.a_ref, f32[128,2048]{1,0:T(8,128)S(1)} %get-tuple-element.38.g_ref), custom_call_target="tpu_custom_call" | custom-call | tf_op jit(solution)/shard_map/pallas_call | solution.py:310
  73.6 1.1 %shard_map.27 = (f32[128,2048]{1,0:T(8,128)S(1)}, f32[32,1024]{1,0:T(8,128)S(1)}) custom-call(f32[128,128]{1,0:T(8,128)S(1)} %get-tuple-element.39.f_ref, f32[128,2048]{1,0:T(8,128)S(1)} %get-tuple-element.38.g_ref), custom_call_target="tpu_custom_call" | custom-call | tf_op jit(solution)/shard_map/pallas_call | solution.py:310
  74.7 1.9 %collective-permute-start.4 = (f32[32,1024]{1,0:T(8,128)S(1)}, f32[32,1024]{1,0:T(8,128)S(1)}, u32[]{:S(2)}, u32[]{:S(2)}) collective-permute-start(f32[32,1024]{1,0:T(8,128)S(1)} %get-tuple-element.41), channel_id=1, source_target_pairs={{0,16},{16,0},{32,48},{48,32},{64,80},{80,64},{96,112},{112,96},{1... | collective-permute-start | bytes 393224 | tf_op jit(solution)/shard_map/ppermute | solution.py:333
  76.7 3.4 %collective-permute-start.5 = (f32[32,1024]{1,0:T(8,128)S(1)}, f32[32,1024]{1,0:T(8,128)S(1)}, u32[]{:S(2)}, u32[]{:S(2)}) collective-permute-start(f32[32,1024]{1,0:T(8,128)S(1)} %get-tuple-element.42), channel_id=1, source_target_pairs={{16,32},{48,64},{80,96},{112,128},{144,160},{176,192},{208,224},{2... | collective-permute-start | bytes 393224 | tf_op jit(solution)/shard_map/ppermute | solution.py:331
  80.1 0.4 shard_map.28.g_ref
  80.5 0.0 collective-permute-done.4.ra_ref
  80.5 6.0 %collective-permute-done.5.rb_ref = f32[32,1024]{1,0:T(8,128)S(1)} collective-permute-done((f32[32,1024]{1,0:T(8,128)S(1)}, f32[32,1024]{1,0:T(8,128)S(1)}, u32[]{:S(2)}, u32[]{:S(2)}) %collective-permute-start.5) | collective-permute-done | bytes 131104 | tf_op jit(solution)/shard_map/ppermute | solution.py:331
  86.6 0.9 shard_map.29
  87.4 1.0 %copy.8 = f32[8,4,4,2,1024]{4,3,2,1,0:T(2,128)} copy(f32[8,4,4,2,1024]{4,3,2,1,0:T(2,128)S(1)} %bitcast.10) | data formatting | bytes 2097152
  (3 shorter events, 0.1 us)
Async XLA Ops:
  0.0 1.2 %copy-start = (f32[8,4,4,2,1024]{4,3,2,1,0:T(2,128)S(1)}, f32[8,4,4,2,1024]{4,3,2,1,0:T(2,128)}, u32[]{:S(2)}) copy-start(f32[8,4,4,2,1024]{4,3,2,1,0:T(2,128)} %param.1) | copy-start | bytes 3145732
  21.1 8.3 %collective-permute-start = (f32[32,1024]{1,0:T(8,128)S(1)}, f32[32,1024]{1,0:T(8,128)S(1)}, u32[]{:S(2)}, u32[]{:S(2)}) collective-permute-start(f32[32,1024]{1,0:T(8,128)S(1)} %get-tuple-element.28), channel_id=1, source_target_pairs={{0,16},{16,0},{32,48},{48,32},{64,80},{80,64},{96,112},{112,96},{1... | collective-permute-start | bytes 393224 | tf_op jit(solution)/shard_map/ppermute | solution.py:333
  23.0 9.9 %collective-permute-start.1 = (f32[32,1024]{1,0:T(8,128)S(1)}, f32[32,1024]{1,0:T(8,128)S(1)}, u32[]{:S(2)}, u32[]{:S(2)}) collective-permute-start(f32[32,1024]{1,0:T(8,128)S(1)} %get-tuple-element.29), channel_id=1, source_target_pairs={{16,32},{48,64},{80,96},{112,128},{144,160},{176,192},{208,224},{2... | collective-permute-start | bytes 393224 | tf_op jit(solution)/shard_map/ppermute | solution.py:331
  47.9 7.0 %collective-permute-start.2 = (f32[32,1024]{1,0:T(8,128)S(1)}, f32[32,1024]{1,0:T(8,128)S(1)}, u32[]{:S(2)}, u32[]{:S(2)}) collective-permute-start(f32[32,1024]{1,0:T(8,128)S(1)} %get-tuple-element.35), channel_id=1, source_target_pairs={{0,16},{16,0},{32,48},{48,32},{64,80},{80,64},{96,112},{112,96},{1... | collective-permute-start | bytes 393224 | tf_op jit(solution)/shard_map/ppermute | solution.py:333
  49.8 9.9 %collective-permute-start.3 = (f32[32,1024]{1,0:T(8,128)S(1)}, f32[32,1024]{1,0:T(8,128)S(1)}, u32[]{:S(2)}, u32[]{:S(2)}) collective-permute-start(f32[32,1024]{1,0:T(8,128)S(1)} %get-tuple-element.36), channel_id=1, source_target_pairs={{16,32},{48,64},{80,96},{112,128},{144,160},{176,192},{208,224},{2... | collective-permute-start | bytes 393224 | tf_op jit(solution)/shard_map/ppermute | solution.py:331
  74.7 5.8 %collective-permute-start.4 = (f32[32,1024]{1,0:T(8,128)S(1)}, f32[32,1024]{1,0:T(8,128)S(1)}, u32[]{:S(2)}, u32[]{:S(2)}) collective-permute-start(f32[32,1024]{1,0:T(8,128)S(1)} %get-tuple-element.41), channel_id=1, source_target_pairs={{0,16},{16,0},{32,48},{48,32},{64,80},{80,64},{96,112},{112,96},{1... | collective-permute-start | bytes 393224 | tf_op jit(solution)/shard_map/ppermute | solution.py:333
  76.7 9.9 %collective-permute-start.5 = (f32[32,1024]{1,0:T(8,128)S(1)}, f32[32,1024]{1,0:T(8,128)S(1)}, u32[]{:S(2)}, u32[]{:S(2)}) collective-permute-start(f32[32,1024]{1,0:T(8,128)S(1)} %get-tuple-element.42), channel_id=1, source_target_pairs={{16,32},{48,64},{80,96},{112,128},{144,160},{176,192},{208,224},{2... | collective-permute-start | bytes 393224 | tf_op jit(solution)/shard_map/ppermute | solution.py:331

commit v2 on v1

--- a/solution.py
+++ b/solution.py
@@ -15,8 +15,7 @@
 LAM = 1.9 / ((NV - 1) * SPEED_LIMIT / NV)
 QUAD = SPACING**3 / (2.0 * math.pi) ** 1.5
 LOG2E = math.log2(math.e)
-NYZ, CELLS = 16, 128
-HIGHEST = lax.Precision.HIGHEST
+LAYERS, CELLS = 8, 128
 VMEM = pl.BlockSpec(memory_space=pltpu.VMEM)
 TILE = (8, 128)
 
@@ -60,14 +59,24 @@
     ]
 
 
-def moments_into(g_ref, w_ref, m_ref):
-    m_ref[...] = lax.dot_general(
-        w_ref[...],
-        g_ref[...],
-        (((1,), (1,)), ((), ())),
-        precision=HIGHEST,
-        preferred_element_type=jnp.float32,
-    )
+def split(x):
+    high = x.astype(jnp.bfloat16)
+    rest = x - high.astype(jnp.float32)
+    mid = rest.astype(jnp.bfloat16)
+    return high, mid, (rest - mid.astype(jnp.float32)).astype(jnp.bfloat16)
+
+
+def weighed(w_ref, x):
+    n = w_ref.shape[0] // 3
+    total = None
+    for k, part in enumerate(split(x)):
+        product = lax.dot_general(
+            w_ref[0 : (3 - k) * n, :], part, (((1,), (1,)), ((), ())), preferred_element_type=jnp.float32
+        )
+        for j in range(3 - k):
+            piece = product[j * n : (j + 1) * n, :]
+            total = piece if total is None else total + piece
+    return total
 
 
 def xabs_here():
@@ -79,13 +88,14 @@
     return lax.axis_index("space") % 2 == 0
 
 
-def first_kernel(d_ref, g_ref, w_ref, m_ref):
-    for block in range(8):
-        for half in range(2):
-            lanes = pl.ds(half * 1024 + block * 128, 128)
-            for yz in range(NYZ):
-                rows = pl.ds(yz * 16 + block * 2 + half, 8, stride=256)
-                g_ref[pl.ds(yz * 8, 8), lanes] = d_ref[rows, :]
+def plane(y):
+    return (slice(None), pl.ds(y * 64, 64), slice(None))
+
+
+def first_kernel(d_hbm, g_ref, w_ref, we_ref, m_ref, d_ref, sems):
+    copies = [pltpu.make_async_copy(d_hbm.at[plane(y)], d_ref.at[plane(y)], sems.at[y]) for y in range(4)]
+    for copy in copies:
+        copy.start()
     xabs = xabs_here()
     zs = zspeed()
     row = iota(0)
@@ -94,15 +104,26 @@
         for block in range(8):
             ys = yspeed(block)
             square = xs * xs + ys * ys + zs * zs
-            lanes = pl.ds(half * 1024 + block * 128, 128)
             low = [jnp.ones_like(xs), xs, ys, zs, xs * xs, ys * ys, zs * zs, xs * ys]
             high = [xs * zs, ys * zs, xs * square, ys * square, zs * square]
-            for base, rows in ((0, low), (8, high)):
+            tiles = []
+            for rows in (low, high):
                 tile = jnp.zeros(TILE, jnp.float32)
                 for i, r in enumerate(rows):
                     tile = jnp.where(row == i, r, tile)
-                w_ref[pl.ds(base, 8), lanes] = QUAD * tile
-    moments_into(g_ref, w_ref, m_ref)
+                tiles.append(QUAD * tile)
+            for k, part in enumerate(split(jnp.concatenate(tiles))):
+                w_ref[pl.ds(k * 16, 16), pl.ds(half * 1024 + block * 128, 128)] = part
+                we_ref[pl.ds(k * 32 + (1 - half) * 16, 16), pl.ds(block * 128, 128)] = part
+    for y in range(4):
+        copies[y].wait()
+        for z in range(4):
+            yz = 4 * y + z
+            for block in range(8):
+                for half in range(2):
+                    lanes = pl.ds(half * 1024 + block * 128, 128)
+                    g_ref[pl.ds(yz * 8, 8), lanes] = d_ref[:, yz * 16 + block * 2 + half, :]
+    m_ref[...] = weighed(w_ref, g_ref[...])
 
 
 def cell_fields(m):
@@ -248,7 +269,7 @@
     pl.when(jnp.logical_not(even))(lambda: slab(0))
 
 
-def sweep_kernel(l_ref, g_ref):
+def sweep_kernel(l_ref, w_ref, g_ref, m_ref):
     zs = zspeed()
     zcoef = shares(zs)
     zforward = zs > 0.0
@@ -261,83 +282,131 @@
             for y in range(4):
                 for z in range(4):
                     g_ref[pl.ds((4 * y + z) * 8, 8), lanes] = done[y][z]
-
-
-def edges(g_ref, ra_ref, rb_ref, store):
+    if m_ref is not None:
+        m_ref[...] = weighed(w_ref, g_ref[...])
+
+
+def last_sweep_kernel(l_ref, g_ref):
+    sweep_kernel(l_ref, None, g_ref, None)
+
+
+def sweep_edges(ra_ref, rb_ref, x_refs):
     even = jnp.full(TILE, (lax.axis_index("space") + 1) % 2, jnp.int32) > 0
-    zero = jnp.zeros(TILE, jnp.float32)
     zs = zspeed()
     za, zb, zc = shares(zs)
     zforward = zs > 0.0
     for block in range(8):
         ya, yb, yc = shares(yspeed(block))
         step = -1 if block >= 4 else 1
+        lanes = pl.ds(block * 128, 128)
         for half in range(2):
             cells = []
             for y in range(4):
-                a, b = [r[pl.ds(y * 8, 8), pl.ds(block * 128, 128)] for r in (ra_ref, rb_ref)]
+                a, b = [r[pl.ds(y * 8, 8), lanes] for r in (ra_ref, rb_ref)]
                 cells.append(jnp.where(even, b, a) if half else jnp.where(even, a, b))
             for y in range(4):
                 mid = ya * cells[y] + yb * cells[(y + step) % 4] + yc * cells[(y + 2) % 4]
                 near = jnp.where(zforward, pltpu.roll(mid, 2, 0), pltpu.roll(mid, 6, 0))
-                done = za * mid + zb * near + zc * pltpu.roll(mid, 4, 0)
-                for z in range(4):
-                    shift = (-2 * z if half else 6 - 2 * z) % 8
-                    part = pltpu.roll(done, shift, 0) if shift else done
-                    rows = pl.ds((4 * y + z) * 8, 8)
+                x_refs[half][pl.ds(y * 8, 8), lanes] = za * mid + zb * near + zc * pltpu.roll(mid, 4, 0)
+
+
+def unpacked(x_refs, y, z, half, block):
+    shift = (-2 * z if half else 6 - 2 * z) % 8
+    part = x_refs[half][pl.ds(y * 8, 8), pl.ds(block * 128, 128)]
+    part = pltpu.roll(part, shift, 0) if shift else part
+    return jnp.where(xmask(half, 1), part, jnp.zeros(TILE, jnp.float32))
+
+
+def edge_kernel(g_ref, ml_ref, ra_ref, rb_ref, we_ref, o_ref, m_ref, x0_ref, x1_ref, e_ref):
+    x_refs = (x0_ref, x1_ref)
+    sweep_edges(ra_ref, rb_ref, x_refs)
+    for y in range(4):
+        for z in range(4):
+            rows = pl.ds((4 * y + z) * 8, 8)
+            for block in range(8):
+                parts = [unpacked(x_refs, y, z, half, block) for half in range(2)]
+                for half in range(2):
                     lanes = pl.ds(half * 1024 + block * 128, 128)
-                    value = g_ref[rows, lanes] + jnp.where(xmask(half, 1), part, zero)
-                    store(4 * y + z, half, block, value)
-
-
-def edge_kernel(g_ref, ra_ref, rb_ref, w_ref, o_ref, m_ref):
-    def store(yz, half, block, value):
-        o_ref[pl.ds(yz * 8, 8), pl.ds(half * 1024 + block * 128, 128)] = value
-
-    edges(g_ref, ra_ref, rb_ref, store)
-    moments_into(o_ref, w_ref, m_ref)
-
-
-def last_kernel(g_ref, ra_ref, rb_ref, o_ref):
-    def store(yz, half, block, value):
-        o_ref[pl.ds(yz * 16 + block * 2 + half, 8, stride=256), :] = value
-
-    edges(g_ref, ra_ref, rb_ref, store)
-
-
-def call(kernel, outs, **kw):
-    shapes = [pltpu.VMEM(s, jnp.float32) for s in outs]
-    return lambda *args: pl.pallas_call(
-        kernel, out_shape=shapes, in_specs=[VMEM] * len(args), out_specs=[VMEM] * len(outs), **kw
-    )(*(pltpu.with_memory_space_constraint(a, pltpu.VMEM) for a in args))
+                    o_ref[rows, lanes] = g_ref[rows, lanes] + parts[half]
+                e_ref[rows, pl.ds(block * 128, 128)] = parts[0] + parts[1]
+    both = weighed(we_ref, e_ref[...])
+    front = lax.broadcasted_iota(jnp.int32, (16, CELLS), 1) % LAYERS < 2
+    m_ref[...] = ml_ref[...] + jnp.where(front, both[0:16, :], both[16:32, :])
+
+
+def last_kernel(g_ref, ra_ref, rb_ref, o_hbm, x0_ref, x1_ref, o_ref, sems):
+    x_refs = (x0_ref, x1_ref)
+    sweep_edges(ra_ref, rb_ref, x_refs)
+    copies = [pltpu.make_async_copy(o_ref.at[plane(y)], o_hbm.at[plane(y)], sems.at[y]) for y in range(4)]
+    for y in range(4):
+        for z in range(4):
+            yz = 4 * y + z
+            for block in range(8):
+                for half in range(2):
+                    value = g_ref[pl.ds(yz * 8, 8), pl.ds(half * 1024 + block * 128, 128)]
+                    o_ref[:, yz * 16 + block * 2 + half, :] = value + unpacked(x_refs, y, z, half, block)
+        copies[y].start()
+    for copy in copies:
+        copy.wait()
+
+
+F32, BF16 = jnp.float32, jnp.bfloat16
+HBM = pl.BlockSpec(memory_space=pl.ANY)
+GRID, MESSAGE, STORED = (CELLS, 2048), (32, 1024), (LAYERS, 256, 128)
+IO = [pltpu.VMEM(STORED, F32), pltpu.SemaphoreType.DMA((4,))]
+
+
+def call(kernel, outs, scratch=(), hbm_in=False, hbm_out=False, **kw):
+    if hbm_out:
+        shapes = [jax.ShapeDtypeStruct(s, t) for s, t in outs]
+    else:
+        shapes = [pltpu.VMEM(s, t) for s, t in outs]
+
+    def run(*args):
+        if not hbm_in:
+            args = [pltpu.with_memory_space_constraint(a, pltpu.VMEM) for a in args]
+        return pl.pallas_call(
+            kernel,
+            out_shape=shapes,
+            in_specs=[HBM if hbm_in else VMEM] * len(args),
+            out_specs=[HBM if hbm_out else VMEM] * len(outs),
+            scratch_shapes=list(scratch),
+            **kw,
+        )(*args)
+
+    return run
 
 
 def local(distribution):
-    layers, breadth, height, halves, velocities = distribution.shape
+    layers, breadth, height, halves, _ = distribution.shape
     vel_count = lax.axis_size("vel")
     space_count = lax.axis_size("space")
-    grid = (CELLS, halves * velocities)
-    message = (2 * NYZ, velocities)
     stored = distribution.reshape(layers, breadth, height, halves, 8, 128).transpose(0, 1, 2, 4, 3, 5)
-    stored = stored.reshape(2048, 128)
     pairs_a = [(i, i ^ 1) for i in range(space_count)]
     pairs_b = [(i, i + 1) for i in range(1, space_count - 1, 2)]
     pairs_b = pairs_b + [(j, i) for i, j in pairs_b]
-    g, weights, partial_moments = call(first_kernel, [grid, (16, grid[1]), (16, CELLS)])(stored)
+    g, weights, edge_weights, partial_moments = call(
+        first_kernel, [(GRID, F32), ((48, 2048), BF16), ((96, 1024), BF16), ((16, CELLS), F32)], IO, hbm_in=True
+    )(stored.reshape(STORED))
+    edge_scratch = [pltpu.VMEM(MESSAGE, F32), pltpu.VMEM(MESSAGE, F32)]
     for step in range(STEPS):
         everywhere = jnp.broadcast_to(partial_moments[None], (vel_count, 16, CELLS))
         gathered = lax.all_to_all(everywhere, "vel", 0, 0)
-        fields, msg_b = call(outer_kernel, [(128, 128), message])(gathered, g)
+        fields, msg_b = call(outer_kernel, [((128, 128), F32), (MESSAGE, F32)])(gathered, g)
         got_b = lax.ppermute(msg_b, "space", pairs_b)
-        moved, msg_a = call(inner_kernel, [grid, message])(fields, g)
+        moved, msg_a = call(inner_kernel, [(GRID, F32), (MESSAGE, F32)])(fields, g)
         got_a = lax.ppermute(msg_a, "space", pairs_a)
-        (swept,) = call(sweep_kernel, [grid])(moved)
         if step + 1 < STEPS:
-            g, partial_moments = call(edge_kernel, [grid, (16, CELLS)], input_output_aliases={0: 0})(
-                swept, got_a, got_b, weights
-            )
+            swept, inside = call(sweep_kernel, [(GRID, F32), ((16, CELLS), F32)])(moved, weights)
+            g, partial_moments = call(
+                edge_kernel,
+                [(GRID, F32), ((16, CELLS), F32)],
+                edge_scratch + [pltpu.VMEM((CELLS, 1024), F32)],
+                input_output_aliases={0: 0},
+            )(swept, inside, got_a, got_b, edge_weights)
         else:
-            (out,) = call(last_kernel, [(2048, 128)])(swept, got_a, got_b)
+            (swept,) = call(last_sweep_kernel, [(GRID, F32)])(moved)
+            (out,) = call(last_kernel, [(STORED, F32)], edge_scratch + IO, hbm_out=True)(swept, got_a, got_b)
     out = out.reshape(layers, breadth, height, 8, halves, 128).transpose(0, 1, 2, 4, 3, 5)
     return out.reshape(distribution.shape)
 

time: 88.8 us -> 87 us (0.980)
  local copies, waits for them, and re-layouts: 2.27 us -> 0.04 us
  Pallas kernels: 12 us -> 13.4 us
  waiting for transfers between devices: 14.4 us -> 13.5 us
    unnamed x3 -> x0, local copies, waits for them, and re-layouts: 2.2 us -> none
    pallas_call x13, Pallas kernels: 12 us -> 13.4 us  [run(): pl.pallas_call(kernel, out_shape=shapes, in_specs=[HBM if hbm_in else VME...]
    ppermute x3, waiting for transfers between devices: 14.4 us -> 13.5 us  [local(): got_b = lax.ppermute(msg_b, 'space', pairs_b)]
  transfers between devices with their start and end apart: 6 -> 6, of which waited for: 3 -> 3; matrix products, arithmetic and copies ran while one was open for 0% -> 0% of each run, Pallas kernels for 1% -> 3%
where the time goes in v2:
time: 87 us; the launch traced here: 86.6 us
  blocking collectives  39.8 us (46%)
  starting transfers between devices  19.7 us (23%)
  waiting for transfers between devices  13.5 us (16%)
  Pallas kernels  13.4 us (15%)
    all_to_all x3, blocking collectives, local(): gathered = lax.all_to_all(everywhere, 'vel', 0, 0)  39.8 us
    ppermute x3, starting transfers between devices, local(): got_b = lax.ppermute(msg_b, 'space', pairs_b)  14 us
    ppermute x3, waiting for transfers between devices, local(): got_b = lax.ppermute(msg_b, 'space', pairs_b)  13.5 us
    pallas_call x13, Pallas kernels, run(): pl.pallas_call(kernel, out_shape=shapes, in_specs=[HBM if hbm_in else VME...  13.4 us
    ppermute x3, starting transfers between devices, local(): got_a = lax.ppermute(msg_a, 'space', pairs_a)  5.76 us
  transfers between devices with their start and end apart: 6, of which 3 were waited for; matrix products, arithmetic and copies ran while one was open for 0% of the time, Pallas kernels for 3%

profile of v2, /device:TPU:512, one launch (start us, length us, event | category | flops | bytes accessed | tf_op | source)
XLA Modules:
  0.0 86.6 jit_solution(9571454685949820628)
XLA Ops:
  0.0 2.0 %shard_map.17 = (f32[128,2048]{1,0:T(8,128)S(1)}, bf16[48,2048]{1,0:T(8,128)(2,1)S(1)}, bf16[96,1024]{1,0:T(8,128)(2,1)S(1)}, f32[16,128]{1,0:T(8,128)S(1)}) custom-call(f32[8,256,128]{2,1,0:T(8,128)} %bitcast.10), custom_call_target="tpu_custom_call" | custom-call | tf_op jit(solution)/shard_map/pallas_call | solution.py:368
  2.1 16.5 %all_to_all.15.a_ref = f32[16,16,128]{2,1,0:T(8,128)S(1)} all-to-all(f32[16,16,128]{2,1,0:T(8,128)S(1)} %broadcast_in_dim.6), channel_id=1, replica_groups=mesh['space'=48,'vel'=16] {'vel'}, dimensions={0} | all-to-all | bytes 262144 | tf_op jit(solution)/shard_map/all_to_all | solution.py:394
  18.6 0.9 %shard_map.18 = (f32[128,128]{1,0:T(8,128)S(1)}, f32[32,1024]{1,0:T(8,128)S(1)}) custom-call(f32[16,16,128]{2,1,0:T(8,128)S(1)} %all_to_all.15.a_ref, f32[128,2048]{1,0:T(8,128)S(1)} %get-tuple-element.30.g_ref), custom_call_target="tpu_custom_call" | custom-call | tf_op jit(solution)/shard_map/pallas_call | solution.py:368
  19.5 1.1 %shard_map.19 = (f32[128,2048]{1,0:T(8,128)S(1)}, f32[32,1024]{1,0:T(8,128)S(1)}) custom-call(f32[128,128]{1,0:T(8,128)S(1)} %get-tuple-element.31.f_ref, f32[128,2048]{1,0:T(8,128)S(1)} %get-tuple-element.30.g_ref), custom_call_target="tpu_custom_call" | custom-call | tf_op jit(solution)/shard_map/pallas_call | solution.py:368
  20.6 1.9 %collective-permute-start = (f32[32,1024]{1,0:T(8,128)S(1)}, f32[32,1024]{1,0:T(8,128)S(1)}, u32[]{:S(2)}, u32[]{:S(2)}) collective-permute-start(f32[32,1024]{1,0:T(8,128)S(1)} %get-tuple-element.36), channel_id=1, source_target_pairs={{0,16},{16,0},{32,48},{48,32},{64,80},{80,64},{96,112},{112,96},{1... | collective-permute-start | bytes 393224 | tf_op jit(solution)/shard_map/ppermute | solution.py:398
  22.5 5.9 %collective-permute-start.1 = (f32[32,1024]{1,0:T(8,128)S(1)}, f32[32,1024]{1,0:T(8,128)S(1)}, u32[]{:S(2)}, u32[]{:S(2)}) collective-permute-start(f32[32,1024]{1,0:T(8,128)S(1)} %get-tuple-element.37), channel_id=1, source_target_pairs={{16,32},{48,64},{80,96},{112,128},{144,160},{176,192},{208,224},{2... | collective-permute-start | bytes 393224 | tf_op jit(solution)/shard_map/ppermute | solution.py:396
  28.5 0.9 %shard_map.20 = (f32[128,2048]{1,0:T(8,128)S(1)}, f32[16,128]{1,0:T(8,128)S(1)}) custom-call(f32[128,2048]{1,0:T(8,128)S(1)} %get-tuple-element.32.l_ref, bf16[48,2048]{1,0:T(8,128)(2,1)S(1)} %get-tuple-element.33.w_ref), custom_call_target="tpu_custom_call" | custom-call | tf_op jit(solution)/shard_map/pallas_call | solution.py:368
  29.4 0.0 collective-permute-done.ra_ref
  29.4 3.1 %collective-permute-done.1.rb_ref = f32[32,1024]{1,0:T(8,128)S(1)} collective-permute-done((f32[32,1024]{1,0:T(8,128)S(1)}, f32[32,1024]{1,0:T(8,128)S(1)}, u32[]{:S(2)}, u32[]{:S(2)}) %collective-permute-start.1) | collective-permute-done | bytes 131104 | tf_op jit(solution)/shard_map/ppermute | solution.py:396
  32.4 0.8 shard_map.21
  33.2 11.6 %all_to_all.16.a_ref = f32[16,16,128]{2,1,0:T(8,128)S(1)} all-to-all(f32[16,16,128]{2,1,0:T(8,128)S(1)} %broadcast_in_dim.7), channel_id=1, replica_groups=mesh['space'=48,'vel'=16] {'vel'}, dimensions={0} | all-to-all | bytes 262144 | tf_op jit(solution)/shard_map/all_to_all | solution.py:394
  44.9 0.9 %shard_map.22 = (f32[128,128]{1,0:T(8,128)S(1)}, f32[32,1024]{1,0:T(8,128)S(1)}) custom-call(f32[16,16,128]{2,1,0:T(8,128)S(1)} %all_to_all.16.a_ref, f32[128,2048]{1,0:T(8,128)S(1)} %get-tuple-element.40.g_ref), custom_call_target="tpu_custom_call" | custom-call | tf_op jit(solution)/shard_map/pallas_call | solution.py:368
  45.8 1.1 %shard_map.23 = (f32[128,2048]{1,0:T(8,128)S(1)}, f32[32,1024]{1,0:T(8,128)S(1)}) custom-call(f32[128,128]{1,0:T(8,128)S(1)} %get-tuple-element.41.f_ref, f32[128,2048]{1,0:T(8,128)S(1)} %get-tuple-element.40.g_ref), custom_call_target="tpu_custom_call" | custom-call | tf_op jit(solution)/shard_map/pallas_call | solution.py:368
  46.9 1.9 %collective-permute-start.2 = (f32[32,1024]{1,0:T(8,128)S(1)}, f32[32,1024]{1,0:T(8,128)S(1)}, u32[]{:S(2)}, u32[]{:S(2)}) collective-permute-start(f32[32,1024]{1,0:T(8,128)S(1)} %get-tuple-element.45), channel_id=1, source_target_pairs={{0,16},{16,0},{32,48},{48,32},{64,80},{80,64},{96,112},{112,96},{1... | collective-permute-start | bytes 393224 | tf_op jit(solution)/shard_map/ppermute | solution.py:398
  48.9 4.6 %collective-permute-start.3 = (f32[32,1024]{1,0:T(8,128)S(1)}, f32[32,1024]{1,0:T(8,128)S(1)}, u32[]{:S(2)}, u32[]{:S(2)}) collective-permute-start(f32[32,1024]{1,0:T(8,128)S(1)} %get-tuple-element.46), channel_id=1, source_target_pairs={{16,32},{48,64},{80,96},{112,128},{144,160},{176,192},{208,224},{2... | collective-permute-start | bytes 393224 | tf_op jit(solution)/shard_map/ppermute | solution.py:396
  53.5 0.9 %shard_map.24 = (f32[128,2048]{1,0:T(8,128)S(1)}, f32[16,128]{1,0:T(8,128)S(1)}) custom-call(f32[128,2048]{1,0:T(8,128)S(1)} %get-tuple-element.42.l_ref, bf16[48,2048]{1,0:T(8,128)(2,1)S(1)} %get-tuple-element.33.w_ref), custom_call_target="tpu_custom_call" | custom-call | tf_op jit(solution)/shard_map/pallas_call | solution.py:368
  54.4 0.0 collective-permute-done.2.ra_ref
  54.4 4.4 %collective-permute-done.3.rb_ref = f32[32,1024]{1,0:T(8,128)S(1)} collective-permute-done((f32[32,1024]{1,0:T(8,128)S(1)}, f32[32,1024]{1,0:T(8,128)S(1)}, u32[]{:S(2)}, u32[]{:S(2)}) %collective-permute-start.3) | collective-permute-done | bytes 131104 | tf_op jit(solution)/shard_map/ppermute | solution.py:396
  58.8 0.8 shard_map.25
  59.6 11.6 %all_to_all.17.a_ref = f32[16,16,128]{2,1,0:T(8,128)S(1)} all-to-all(f32[16,16,128]{2,1,0:T(8,128)S(1)} %broadcast_in_dim.8), channel_id=1, replica_groups=mesh['space'=48,'vel'=16] {'vel'}, dimensions={0} | all-to-all | bytes 262144 | tf_op jit(solution)/shard_map/all_to_all | solution.py:394
  71.2 0.9 %shard_map.26 = (f32[128,128]{1,0:T(8,128)S(1)}, f32[32,1024]{1,0:T(8,128)S(1)}) custom-call(f32[16,16,128]{2,1,0:T(8,128)S(1)} %all_to_all.17.a_ref, f32[128,2048]{1,0:T(8,128)S(1)} %get-tuple-element.48.g_ref), custom_call_target="tpu_custom_call" | custom-call | tf_op jit(solution)/shard_map/pallas_call | solution.py:368
  72.1 1.1 %shard_map.27 = (f32[128,2048]{1,0:T(8,128)S(1)}, f32[32,1024]{1,0:T(8,128)S(1)}) custom-call(f32[128,128]{1,0:T(8,128)S(1)} %get-tuple-element.49.f_ref, f32[128,2048]{1,0:T(8,128)S(1)} %get-tuple-element.48.g_ref), custom_call_target="tpu_custom_call" | custom-call | tf_op jit(solution)/shard_map/pallas_call | solution.py:368
  73.3 1.9 %collective-permute-start.4 = (f32[32,1024]{1,0:T(8,128)S(1)}, f32[32,1024]{1,0:T(8,128)S(1)}, u32[]{:S(2)}, u32[]{:S(2)}) collective-permute-start(f32[32,1024]{1,0:T(8,128)S(1)} %get-tuple-element.51), channel_id=1, source_target_pairs={{0,16},{16,0},{32,48},{48,32},{64,80},{80,64},{96,112},{112,96},{1... | collective-permute-start | bytes 393224 | tf_op jit(solution)/shard_map/ppermute | solution.py:398
  75.2 3.4 %collective-permute-start.5 = (f32[32,1024]{1,0:T(8,128)S(1)}, f32[32,1024]{1,0:T(8,128)S(1)}, u32[]{:S(2)}, u32[]{:S(2)}) collective-permute-start(f32[32,1024]{1,0:T(8,128)S(1)} %get-tuple-element.52), channel_id=1, source_target_pairs={{16,32},{48,64},{80,96},{112,128},{144,160},{176,192},{208,224},{2... | collective-permute-start | bytes 393224 | tf_op jit(solution)/shard_map/ppermute | solution.py:396
  78.6 0.4 shard_map.28.g_ref
  79.1 0.0 collective-permute-done.4.ra_ref
  79.1 6.0 %collective-permute-done.5.rb_ref = f32[32,1024]{1,0:T(8,128)S(1)} collective-permute-done((f32[32,1024]{1,0:T(8,128)S(1)}, f32[32,1024]{1,0:T(8,128)S(1)}, u32[]{:S(2)}, u32[]{:S(2)}) %collective-permute-start.5) | collective-permute-done | bytes 131104 | tf_op jit(solution)/shard_map/ppermute | solution.py:396
  85.1 1.5 %shard_map.29 = f32[8,256,128]{2,1,0:T(8,128)} custom-call(f32[128,2048]{1,0:T(8,128)S(1)} %shard_map.28.g_ref, f32[32,1024]{1,0:T(8,128)S(1)} %collective-permute-done.4.ra_ref, f32[32,1024]{1,0:T(8,128)S(1)} %collective-permute-done.5.rb_ref), custom_call_target="tpu_custom_call" | custom-call | tf_op jit(solution)/shard_map/pallas_call | solution.py:368
  (3 shorter events, 0.0 us)
Async XLA Ops:
  20.6 8.8 %collective-permute-start = (f32[32,1024]{1,0:T(8,128)S(1)}, f32[32,1024]{1,0:T(8,128)S(1)}, u32[]{:S(2)}, u32[]{:S(2)}) collective-permute-start(f32[32,1024]{1,0:T(8,128)S(1)} %get-tuple-element.36), channel_id=1, source_target_pairs={{0,16},{16,0},{32,48},{48,32},{64,80},{80,64},{96,112},{112,96},{1... | collective-permute-start | bytes 393224 | tf_op jit(solution)/shard_map/ppermute | solution.py:398
  22.5 9.9 %collective-permute-start.1 = (f32[32,1024]{1,0:T(8,128)S(1)}, f32[32,1024]{1,0:T(8,128)S(1)}, u32[]{:S(2)}, u32[]{:S(2)}) collective-permute-start(f32[32,1024]{1,0:T(8,128)S(1)} %get-tuple-element.37), channel_id=1, source_target_pairs={{16,32},{48,64},{80,96},{112,128},{144,160},{176,192},{208,224},{2... | collective-permute-start | bytes 393224 | tf_op jit(solution)/shard_map/ppermute | solution.py:396
  46.9 7.4 %collective-permute-start.2 = (f32[32,1024]{1,0:T(8,128)S(1)}, f32[32,1024]{1,0:T(8,128)S(1)}, u32[]{:S(2)}, u32[]{:S(2)}) collective-permute-start(f32[32,1024]{1,0:T(8,128)S(1)} %get-tuple-element.45), channel_id=1, source_target_pairs={{0,16},{16,0},{32,48},{48,32},{64,80},{80,64},{96,112},{112,96},{1... | collective-permute-start | bytes 393224 | tf_op jit(solution)/shard_map/ppermute | solution.py:398
  48.9 9.9 %collective-permute-start.3 = (f32[32,1024]{1,0:T(8,128)S(1)}, f32[32,1024]{1,0:T(8,128)S(1)}, u32[]{:S(2)}, u32[]{:S(2)}) collective-permute-start(f32[32,1024]{1,0:T(8,128)S(1)} %get-tuple-element.46), channel_id=1, source_target_pairs={{16,32},{48,64},{80,96},{112,128},{144,160},{176,192},{208,224},{2... | collective-permute-start | bytes 393224 | tf_op jit(solution)/shard_map/ppermute | solution.py:396
  73.3 5.8 %collective-permute-start.4 = (f32[32,1024]{1,0:T(8,128)S(1)}, f32[32,1024]{1,0:T(8,128)S(1)}, u32[]{:S(2)}, u32[]{:S(2)}) collective-permute-start(f32[32,1024]{1,0:T(8,128)S(1)} %get-tuple-element.51), channel_id=1, source_target_pairs={{0,16},{16,0},{32,48},{48,32},{64,80},{80,64},{96,112},{112,96},{1... | collective-permute-start | bytes 393224 | tf_op jit(solution)/shard_map/ppermute | solution.py:398
  75.2 9.9 %collective-permute-start.5 = (f32[32,1024]{1,0:T(8,128)S(1)}, f32[32,1024]{1,0:T(8,128)S(1)}, u32[]{:S(2)}, u32[]{:S(2)}) collective-permute-start(f32[32,1024]{1,0:T(8,128)S(1)} %get-tuple-element.52), channel_id=1, source_target_pairs={{16,32},{48,64},{80,96},{112,128},{144,160},{176,192},{208,224},{2... | collective-permute-start | bytes 393224 | tf_op jit(solution)/shard_map/ppermute | solution.py:396

commit v3 on v2

--- a/solution.py
+++ b/solution.py
@@ -66,6 +66,10 @@
     return high, mid, (rest - mid.astype(jnp.float32)).astype(jnp.bfloat16)
 
 
+def wide(ref, rows):
+    return jnp.concatenate([ref[k, rows, :] for k in range(ref.shape[0])], axis=1)
+
+
 def weighed(w_ref, x):
     n = w_ref.shape[0] // 3
     total = None
@@ -92,7 +96,7 @@
     return (slice(None), pl.ds(y * 64, 64), slice(None))
 
 
-def first_kernel(d_hbm, g_ref, w_ref, we_ref, m_ref, d_ref, sems):
+def first_kernel(d_hbm, g_ref, w_ref, m_ref, d_ref, sems):
     copies = [pltpu.make_async_copy(d_hbm.at[plane(y)], d_ref.at[plane(y)], sems.at[y]) for y in range(4)]
     for copy in copies:
         copy.start()
@@ -114,16 +118,14 @@
                 tiles.append(QUAD * tile)
             for k, part in enumerate(split(jnp.concatenate(tiles))):
                 w_ref[pl.ds(k * 16, 16), pl.ds(half * 1024 + block * 128, 128)] = part
-                we_ref[pl.ds(k * 32 + (1 - half) * 16, 16), pl.ds(block * 128, 128)] = part
     for y in range(4):
         copies[y].wait()
         for z in range(4):
             yz = 4 * y + z
             for block in range(8):
                 for half in range(2):
-                    lanes = pl.ds(half * 1024 + block * 128, 128)
-                    g_ref[pl.ds(yz * 8, 8), lanes] = d_ref[:, yz * 16 + block * 2 + half, :]
-    m_ref[...] = weighed(w_ref, g_ref[...])
+                    g_ref[half * 8 + block, pl.ds(yz * 8, 8), :] = d_ref[:, yz * 16 + block * 2 + half, :]
+        m_ref[:, y * 32 : (y + 1) * 32] = weighed(w_ref, wide(g_ref, pl.ds(y * 32, 32)))
 
 
 def cell_fields(m):
@@ -132,7 +134,7 @@
     ux, uy, uz = m[1] * inv_rho, m[2] * inv_rho, m[3] * inv_rho
     energy = m[4] + m[5] + m[6]
     norm = ux * ux + uy * uy + uz * uz
-    temp = (energy * inv_rho - norm) / 3.0
+    temp = (energy * inv_rho - norm) * (1.0 / 3.0)
     along = ux * m[1] + uy * m[2] + uz * m[3]
 
     def heating(third, u, first, r0, r1, r2):
@@ -149,12 +151,13 @@
     yq = heating(m[11], uy, m[2], m[7], m[5], m[9])
     zq = heating(m[12], uz, m[3], m[8], m[9], m[6])
     root = jnp.sqrt(temp)
-    conduction = (1.0 / 3.0) / (5.0 * rho * temp * temp)
-    amp = rho / (temp * root)
+    inv_temp = 1.0 / temp
+    conduction = (1.0 / 15.0) * (inv_rho * inv_temp) * inv_temp
+    amp = (rho * inv_temp) * (root * inv_temp)
     retain = jnp.exp(-0.7 * rho * jnp.sqrt(root))
     k = -0.5 * LOG2E
     fold = conduction / k
-    return [ux, uy, uz, k / temp, fold * xq, fold * yq, fold * zq, amp * (1.0 - retain), retain]
+    return [ux, uy, uz, k * inv_temp, fold * xq, fold * yq, fold * zq, amp * (1.0 - retain), retain]
 
 
 class Cell:
@@ -203,34 +206,33 @@
     f_ref[...] = jnp.transpose(f_ref[...])
     xabs = xabs_here()
     _, near, far = shares(xabs)
-    zero = jnp.zeros(TILE, jnp.float32)
     zs = zspeed()
 
     def message(half):
-        n_out = jnp.where(xmask(half, 0), near, zero)
-        f_out = jnp.where(xmask(half, 1), far, zero)
-
-        def per_y(y, carry):
-            packed = [zero] * 8
-            for z in range(4):
-                rows = pl.ds(pl.multiple_of(y * 32 + z * 8, 8), 8)
-                cell = Cell(f_ref[rows, :], xabs, zs)
-                for block in range(8):
-                    relaxed = cell.relax(half, cell.yz(block), g_ref[rows, pl.ds(half * 1024 + block * 128, 128)])
-                    r1, r2 = rotated(relaxed, half)
-                    packed[block] = packed[block] + placed(n_out * r1 + f_out * r2, half, z)
+        lower = 6 if half else 0
+        near_rows = jnp.where((iota(0) < 4) if half else (iota(0) > 3), near, jnp.zeros(TILE, jnp.float32))
+
+        def gathered(ref, y):
+            return jnp.concatenate([ref[pl.ds(y * 32 + lower + layer, 4, stride=8), :] for layer in range(2)])
+
+        for y in range(4):
+            cell = Cell(gathered(f_ref, y), xabs, zs)
             for block in range(8):
-                mb_ref[pl.ds(pl.multiple_of(y * 8, 8), 8), pl.ds(block * 128, 128)] = packed[block]
-            return carry
-
-        lax.fori_loop(0, 4, per_y, 0)
+                current = gathered(g_ref.at[half * 8 + block], y)
+                relaxed = cell.relax(half, cell.yz(block), current)
+                out = far * relaxed + near_rows * pltpu.roll(relaxed, 4, 0)
+                for layer in range(2):
+                    mb_ref[block, pl.ds(y * 8 + layer, 4, stride=2), :] = out[
+                        layer * 4 : layer * 4 + 4, :
+                    ]
 
     even = even_here()
     pl.when(even)(lambda: message(0))
     pl.when(jnp.logical_not(even))(lambda: message(1))
 
 
-def inner_kernel(f_ref, g_ref, l_ref, ma_ref):
+def inner_kernel(f_ref, g_ref, *refs):
+    x_refs, (l_ref, ma_ref) = refs[:-2], refs[-2:]
     xabs = xabs_here()
     own, near, far = shares(xabs)
     zero = jnp.zeros(TILE, jnp.float32)
@@ -251,15 +253,18 @@
                 for block in range(8):
                     yz = cell.yz(block)
                     for half in range(2):
-                        lanes = pl.ds(half * 1024 + block * 128, 128)
-                        relaxed = cell.relax(half, yz, g_ref[rows, lanes])
+                        at = half * 8 + block
+                        current = g_ref[at, rows, :]
+                        if x_refs:
+                            current = current + unpacked(x_refs, y, z, half, block)
+                        relaxed = cell.relax(half, yz, current)
                         r1, r2 = rotated(relaxed, half)
                         n_in, f_in = inside[half]
-                        l_ref[rows, lanes] = own * relaxed + n_in * r1 + f_in * r2
+                        l_ref[at, rows, :] = own * relaxed + n_in * r1 + f_in * r2
                         if half == sent:
                             packed[block] = packed[block] + placed(n_out * r1 + f_out * r2, half, z)
             for block in range(8):
-                ma_ref[pl.ds(pl.multiple_of(y * 8, 8), 8), pl.ds(block * 128, 128)] = packed[block]
+                ma_ref[block, pl.ds(pl.multiple_of(y * 8, 8), 8), :] = packed[block]
             return carry
 
         lax.fori_loop(0, 4, per_y, 0)
@@ -269,25 +274,33 @@
     pl.when(jnp.logical_not(even))(lambda: slab(0))
 
 
-def sweep_kernel(l_ref, w_ref, g_ref, m_ref):
+def sweep_cells(l_ref, store):
     zs = zspeed()
     zcoef = shares(zs)
     zforward = zs > 0.0
     for block in range(8):
         ycoef = shares(yspeed(block))
         for half in range(2):
-            lanes = pl.ds(half * 1024 + block * 128, 128)
-            cells = [[l_ref[pl.ds((4 * y + z) * 8, 8), lanes] for z in range(4)] for y in range(4)]
+            cells = [[l_ref[half * 8 + block, pl.ds((4 * y + z) * 8, 8), :] for z in range(4)] for y in range(4)]
             done = sweep_yz(cells, ycoef, zcoef, zforward, block >= 4)
             for y in range(4):
                 for z in range(4):
-                    g_ref[pl.ds((4 * y + z) * 8, 8), lanes] = done[y][z]
-    if m_ref is not None:
-        m_ref[...] = weighed(w_ref, g_ref[...])
-
-
-def last_sweep_kernel(l_ref, g_ref):
-    sweep_kernel(l_ref, None, g_ref, None)
+                    store(4 * y + z, half, block, done[y][z])
+
+
+def sweep_kernel(l_ref, w_ref, g_ref, m_ref):
+    def store(yz, half, block, value):
+        g_ref[half * 8 + block, pl.ds(yz * 8, 8), :] = value
+
+    sweep_cells(l_ref, store)
+    m_ref[...] = weighed(w_ref, wide(g_ref, slice(None)))
+
+
+def last_sweep_kernel(l_ref, o_ref):
+    def store(yz, half, block, value):
+        o_ref[:, yz * 16 + block * 2 + half, :] = value
+
+    sweep_cells(l_ref, store)
 
 
 def sweep_edges(ra_ref, rb_ref, x_refs):
@@ -298,62 +311,65 @@
     for block in range(8):
         ya, yb, yc = shares(yspeed(block))
         step = -1 if block >= 4 else 1
-        lanes = pl.ds(block * 128, 128)
         for half in range(2):
             cells = []
             for y in range(4):
-                a, b = [r[pl.ds(y * 8, 8), lanes] for r in (ra_ref, rb_ref)]
+                a, b = [r[block, pl.ds(y * 8, 8), :] for r in (ra_ref, rb_ref)]
                 cells.append(jnp.where(even, b, a) if half else jnp.where(even, a, b))
             for y in range(4):
                 mid = ya * cells[y] + yb * cells[(y + step) % 4] + yc * cells[(y + 2) % 4]
                 near = jnp.where(zforward, pltpu.roll(mid, 2, 0), pltpu.roll(mid, 6, 0))
-                x_refs[half][pl.ds(y * 8, 8), lanes] = za * mid + zb * near + zc * pltpu.roll(mid, 4, 0)
+                x_refs[half][block, pl.ds(y * 8, 8), :] = za * mid + zb * near + zc * pltpu.roll(mid, 4, 0)
 
 
 def unpacked(x_refs, y, z, half, block):
     shift = (-2 * z if half else 6 - 2 * z) % 8
-    part = x_refs[half][pl.ds(y * 8, 8), pl.ds(block * 128, 128)]
+    part = x_refs[half][block, pl.ds(pl.multiple_of(y * 8, 8), 8), :]
     part = pltpu.roll(part, shift, 0) if shift else part
     return jnp.where(xmask(half, 1), part, jnp.zeros(TILE, jnp.float32))
 
 
-def edge_kernel(g_ref, ml_ref, ra_ref, rb_ref, we_ref, o_ref, m_ref, x0_ref, x1_ref, e_ref):
+def edge_kernel(ml_ref, ra_ref, rb_ref, w_ref, x0_ref, x1_ref, m_ref):
     x_refs = (x0_ref, x1_ref)
     sweep_edges(ra_ref, rb_ref, x_refs)
-    for y in range(4):
-        for z in range(4):
-            rows = pl.ds((4 * y + z) * 8, 8)
-            for block in range(8):
-                parts = [unpacked(x_refs, y, z, half, block) for half in range(2)]
-                for half in range(2):
-                    lanes = pl.ds(half * 1024 + block * 128, 128)
-                    o_ref[rows, lanes] = g_ref[rows, lanes] + parts[half]
-                e_ref[rows, pl.ds(block * 128, 128)] = parts[0] + parts[1]
-    both = weighed(we_ref, e_ref[...])
-    front = lax.broadcasted_iota(jnp.int32, (16, CELLS), 1) % LAYERS < 2
-    m_ref[...] = ml_ref[...] + jnp.where(front, both[0:16, :], both[16:32, :])
-
-
-def last_kernel(g_ref, ra_ref, rb_ref, o_hbm, x0_ref, x1_ref, o_ref, sems):
+    total = ml_ref[...]
+    source = lax.broadcasted_iota(jnp.int32, (32, CELLS), 0)
+    cell = lax.broadcasted_iota(jnp.int32, (32, CELLS), 1)
+    for half in range(2):
+        sums = weighed(w_ref.at[:, pl.ds(half * 1024, 1024)], wide(x_refs[half], slice(None)))
+        target = source // 2 * 8 + source % 2 + (0 if half else 6)
+        spread = (target == cell).astype(jnp.bfloat16)
+        for part in split(sums):
+            total = total + jnp.dot(part, spread, preferred_element_type=jnp.float32)
+    m_ref[...] = total
+
+
+def last_kernel(s_ref, ra_ref, rb_ref, o_hbm, x0_ref, x1_ref, e_ref, sems):
+    inside = pltpu.make_async_copy(s_ref.at[pl.ds(2, 4)], o_hbm.at[pl.ds(2, 4)], sems.at[4])
+    inside.start()
     x_refs = (x0_ref, x1_ref)
     sweep_edges(ra_ref, rb_ref, x_refs)
-    copies = [pltpu.make_async_copy(o_ref.at[plane(y)], o_hbm.at[plane(y)], sems.at[y]) for y in range(4)]
-    for y in range(4):
-        for z in range(4):
-            yz = 4 * y + z
-            for block in range(8):
-                for half in range(2):
-                    value = g_ref[pl.ds(yz * 8, 8), pl.ds(half * 1024 + block * 128, 128)]
-                    o_ref[:, yz * 16 + block * 2 + half, :] = value + unpacked(x_refs, y, z, half, block)
-        copies[y].start()
-    for copy in copies:
+    copies = []
+    for half in (1, 0):
+        for layer in range(2):
+            at = layer if half else 2 + layer
+            outer = layer if half else 6 + layer
+            e_ref[at] = s_ref[outer]
+            for y in range(4):
+                for block in range(8):
+                    rows = pl.ds(y * 64 + block * 2 + half, 4, stride=16)
+                    part = x_refs[half][block, pl.ds(y * 8 + layer, 4, stride=2), :]
+                    e_ref[at, rows, :] = e_ref[at, rows, :] + part
+            copies.append(pltpu.make_async_copy(e_ref.at[at], o_hbm.at[outer], sems.at[at]))
+            copies[-1].start()
+    for copy in [inside] + copies:
         copy.wait()
 
 
 F32, BF16 = jnp.float32, jnp.bfloat16
-HBM = pl.BlockSpec(memory_space=pl.ANY)
-GRID, MESSAGE, STORED = (CELLS, 2048), (32, 1024), (LAYERS, 256, 128)
-IO = [pltpu.VMEM(STORED, F32), pltpu.SemaphoreType.DMA((4,))]
+HBM = pl.BlockSpec(memory_space=pltpu.HBM)
+GRID, MESSAGE, STORED = (16, CELLS, 128), (8, 32, 128), (LAYERS, 256, 128)
+EDGES = [pltpu.VMEM(MESSAGE, F32), pltpu.VMEM(MESSAGE, F32)]
 
 
 def call(kernel, outs, scratch=(), hbm_in=False, hbm_out=False, **kw):
@@ -363,14 +379,15 @@
         shapes = [pltpu.VMEM(s, t) for s, t in outs]
 
     def run(*args):
-        if not hbm_in:
-            args = [pltpu.with_memory_space_constraint(a, pltpu.VMEM) for a in args]
+        space = pltpu.HBM if hbm_in else pltpu.VMEM
+        args = [pltpu.with_memory_space_constraint(a, space) for a in args]
         return pl.pallas_call(
             kernel,
             out_shape=shapes,
             in_specs=[HBM if hbm_in else VMEM] * len(args),
             out_specs=[HBM if hbm_out else VMEM] * len(outs),
             scratch_shapes=list(scratch),
+            compiler_params=pltpu.CompilerParams(vmem_limit_bytes=8 << 20),
             **kw,
         )(*args)
 
@@ -385,28 +402,35 @@
     pairs_a = [(i, i ^ 1) for i in range(space_count)]
     pairs_b = [(i, i + 1) for i in range(1, space_count - 1, 2)]
     pairs_b = pairs_b + [(j, i) for i, j in pairs_b]
-    g, weights, edge_weights, partial_moments = call(
-        first_kernel, [(GRID, F32), ((48, 2048), BF16), ((96, 1024), BF16), ((16, CELLS), F32)], IO, hbm_in=True
+    g, weights, partial_moments = call(
+        first_kernel,
+        [(GRID, F32), ((48, 2048), BF16), ((16, CELLS), F32)],
+        [pltpu.VMEM(STORED, F32), pltpu.SemaphoreType.DMA((4,))],
+        hbm_in=True,
     )(stored.reshape(STORED))
-    edge_scratch = [pltpu.VMEM(MESSAGE, F32), pltpu.VMEM(MESSAGE, F32)]
+    sides = ()
     for step in range(STEPS):
         everywhere = jnp.broadcast_to(partial_moments[None], (vel_count, 16, CELLS))
         gathered = lax.all_to_all(everywhere, "vel", 0, 0)
         fields, msg_b = call(outer_kernel, [((128, 128), F32), (MESSAGE, F32)])(gathered, g)
         got_b = lax.ppermute(msg_b, "space", pairs_b)
-        moved, msg_a = call(inner_kernel, [(GRID, F32), (MESSAGE, F32)])(fields, g)
+        moved, msg_a = call(inner_kernel, [(GRID, F32), (MESSAGE, F32)])(fields, g, *sides)
         got_a = lax.ppermute(msg_a, "space", pairs_a)
         if step + 1 < STEPS:
-            swept, inside = call(sweep_kernel, [(GRID, F32), ((16, CELLS), F32)])(moved, weights)
-            g, partial_moments = call(
-                edge_kernel,
-                [(GRID, F32), ((16, CELLS), F32)],
-                edge_scratch + [pltpu.VMEM((CELLS, 1024), F32)],
-                input_output_aliases={0: 0},
-            )(swept, inside, got_a, got_b, edge_weights)
+            g, inside = call(sweep_kernel, [(GRID, F32), ((16, CELLS), F32)])(
+                moved, weights
+            )
+            *sides, partial_moments = call(
+                edge_kernel, [(MESSAGE, F32), (MESSAGE, F32), ((16, CELLS), F32)]
+            )(inside, got_a, got_b, weights)
         else:
-            (swept,) = call(last_sweep_kernel, [(GRID, F32)])(moved)
-            (out,) = call(last_kernel, [(STORED, F32)], edge_scratch + IO, hbm_out=True)(swept, got_a, got_b)
+            (swept,) = call(last_sweep_kernel, [(STORED, F32)])(moved)
+            (out,) = call(
+                last_kernel,
+                [(STORED, F32)],
+                EDGES + [pltpu.VMEM((4, 256, 128), F32), pltpu.SemaphoreType.DMA((5,))],
+                hbm_out=True,
+            )(swept, got_a, got_b)
     out = out.reshape(layers, breadth, height, 8, halves, 128).transpose(0, 1, 2, 4, 3, 5)
     return out.reshape(distribution.shape)
 

time: 87 us -> 86 us (0.989)
  no operation moved by 1% of the time
where the time goes in v3:
time: 86 us; the launch traced here: 85.6 us
  blocking collectives  39.8 us (46%)
  starting transfers between devices  19.8 us (23%)
  Pallas kernels  13 us (15%)
  waiting for transfers between devices  12.8 us (15%)
    all_to_all x3, blocking collectives, local(): gathered = lax.all_to_all(everywhere, 'vel', 0, 0)  39.8 us
    ppermute x3, starting transfers between devices, local(): got_b = lax.ppermute(msg_b, 'space', pairs_b)  14.1 us
    pallas_call x13, Pallas kernels, run(): pl.pallas_call(kernel, out_shape=shapes, in_specs=[HBM if hbm_in else VME...  13 us
    ppermute x3, waiting for transfers between devices, local(): got_b = lax.ppermute(msg_b, 'space', pairs_b)  12.8 us
    ppermute x3, starting transfers between devices, local(): got_a = lax.ppermute(msg_a, 'space', pairs_a)  5.76 us
  transfers between devices with their start and end apart: 6, of which 3 were waited for; matrix products, arithmetic and copies ran while one was open for 0% of the time, Pallas kernels for 3%

profile of v3, /device:TPU:512, one launch (start us, length us, event | category | flops | bytes accessed | tf_op | source)
XLA Modules:
  0.0 85.6 jit_solution(4561573341148201603)
XLA Ops:
  0.0 3.1 %shard_map.17 = (f32[16,128,128]{2,1,0:T(8,128)S(1)}, bf16[48,2048]{1,0:T(8,128)(2,1)S(1)}, f32[16,128]{1,0:T(8,128)S(1)}) custom-call(f32[8,256,128]{2,1,0:T(8,128)} %bitcast.10), custom_call_target="tpu_custom_call" | custom-call | tf_op jit(solution)/shard_map/pallas_call | solution.py:384
  3.1 16.5 %all_to_all.15.a_ref = f32[16,16,128]{2,1,0:T(8,128)S(1)} all-to-all(f32[16,16,128]{2,1,0:T(8,128)S(1)} %broadcast_in_dim.6), channel_id=1, replica_groups=mesh['space'=48,'vel'=16] {'vel'}, dimensions={0} | all-to-all | bytes 262144 | tf_op jit(solution)/shard_map/all_to_all | solution.py:414
  19.6 0.3 shard_map.18
  20.0 1.1 %shard_map.19 = (f32[16,128,128]{2,1,0:T(8,128)S(1)}, f32[8,32,128]{2,1,0:T(8,128)S(1)}) custom-call(f32[128,128]{1,0:T(8,128)S(1)} %get-tuple-element.32.f_ref, f32[16,128,128]{2,1,0:T(8,128)S(1)} %get-tuple-element.31.g_ref), custom_call_target="tpu_custom_call" | custom-call | tf_op jit(solution)/shard_map/pallas_call | solution.py:384
  21.1 1.9 %collective-permute-start = (f32[8,32,128]{2,1,0:T(8,128)S(1)}, f32[8,32,128]{2,1,0:T(8,128)S(1)}, u32[]{:S(2)}, u32[]{:S(2)}) collective-permute-start(f32[8,32,128]{2,1,0:T(8,128)S(1)} %get-tuple-element.36), channel_id=1, source_target_pairs={{0,16},{16,0},{32,48},{48,32},{64,80},{80,64},{96,112},{112,96},{1... | collective-permute-start | bytes 393224 | tf_op jit(solution)/shard_map/ppermute | solution.py:418
  23.1 5.9 %collective-permute-start.1 = (f32[8,32,128]{2,1,0:T(8,128)S(1)}, f32[8,32,128]{2,1,0:T(8,128)S(1)}, u32[]{:S(2)}, u32[]{:S(2)}) collective-permute-start(f32[8,32,128]{2,1,0:T(8,128)S(1)} %get-tuple-element.37), channel_id=1, source_target_pairs={{16,32},{48,64},{80,96},{112,128},{144,160},{176,192},{208,224},{2... | collective-permute-start | bytes 393224 | tf_op jit(solution)/shard_map/ppermute | solution.py:416
  29.0 0.9 %shard_map.20 = (f32[16,128,128]{2,1,0:T(8,128)S(1)}, f32[16,128]{1,0:T(8,128)S(1)}) custom-call(f32[16,128,128]{2,1,0:T(8,128)S(1)} %get-tuple-element.33.l_ref, bf16[48,2048]{1,0:T(8,128)(2,1)S(1)} %get-tuple-element.34.w_ref), custom_call_target="tpu_custom_call" | custom-call | tf_op jit(solution)/shard_map/pallas_call | solution.py:384
  29.9 0.0 collective-permute-done.ra_ref
  29.9 3.1 %collective-permute-done.1.rb_ref = f32[8,32,128]{2,1,0:T(8,128)S(1)} collective-permute-done((f32[8,32,128]{2,1,0:T(8,128)S(1)}, f32[8,32,128]{2,1,0:T(8,128)S(1)}, u32[]{:S(2)}, u32[]{:S(2)}) %collective-permute-start.1) | collective-permute-done | bytes 131104 | tf_op jit(solution)/shard_map/ppermute | solution.py:416
  33.0 0.7 shard_map.21
  33.7 11.6 %all_to_all.16.a_ref = f32[16,16,128]{2,1,0:T(8,128)S(1)} all-to-all(f32[16,16,128]{2,1,0:T(8,128)S(1)} %broadcast_in_dim.7), channel_id=1, replica_groups=mesh['space'=48,'vel'=16] {'vel'}, dimensions={0} | all-to-all | bytes 262144 | tf_op jit(solution)/shard_map/all_to_all | solution.py:414
  45.4 0.3 shard_map.22
  45.7 1.2 %shard_map.23 = (f32[16,128,128]{2,1,0:T(8,128)S(1)}, f32[8,32,128]{2,1,0:T(8,128)S(1)}) custom-call(f32[128,128]{1,0:T(8,128)S(1)} %get-tuple-element.40.f_ref, f32[16,128,128]{2,1,0:T(8,128)S(1)} %get-tuple-element.39.g_ref, f32[8,32,128]{2,1,0:T(8,128)S(1)} %get-tuple-element.41.refs_0_, f32[8,32,128]{2,1,0:T(8,128)S(1)} %get-tuple-element.42.refs_1_), custom_call_target="tpu_custom_call" | custom-call | tf_op jit(solution)/shard_map/pallas_call | solution.py:384
  46.9 1.9 %collective-permute-start.2 = (f32[8,32,128]{2,1,0:T(8,128)S(1)}, f32[8,32,128]{2,1,0:T(8,128)S(1)}, u32[]{:S(2)}, u32[]{:S(2)}) collective-permute-start(f32[8,32,128]{2,1,0:T(8,128)S(1)} %get-tuple-element.45), channel_id=1, source_target_pairs={{0,16},{16,0},{32,48},{48,32},{64,80},{80,64},{96,112},{112,96},{1... | collective-permute-start | bytes 393224 | tf_op jit(solution)/shard_map/ppermute | solution.py:418
  48.9 4.6 %collective-permute-start.3 = (f32[8,32,128]{2,1,0:T(8,128)S(1)}, f32[8,32,128]{2,1,0:T(8,128)S(1)}, u32[]{:S(2)}, u32[]{:S(2)}) collective-permute-start(f32[8,32,128]{2,1,0:T(8,128)S(1)} %get-tuple-element.46), channel_id=1, source_target_pairs={{16,32},{48,64},{80,96},{112,128},{144,160},{176,192},{208,224},{2... | collective-permute-start | bytes 393224 | tf_op jit(solution)/shard_map/ppermute | solution.py:416
  53.5 0.9 %shard_map.24 = (f32[16,128,128]{2,1,0:T(8,128)S(1)}, f32[16,128]{1,0:T(8,128)S(1)}) custom-call(f32[16,128,128]{2,1,0:T(8,128)S(1)} %get-tuple-element.43.l_ref, bf16[48,2048]{1,0:T(8,128)(2,1)S(1)} %get-tuple-element.34.w_ref), custom_call_target="tpu_custom_call" | custom-call | tf_op jit(solution)/shard_map/pallas_call | solution.py:384
  54.4 0.0 collective-permute-done.2.ra_ref
  54.4 4.4 %collective-permute-done.3.rb_ref = f32[8,32,128]{2,1,0:T(8,128)S(1)} collective-permute-done((f32[8,32,128]{2,1,0:T(8,128)S(1)}, f32[8,32,128]{2,1,0:T(8,128)S(1)}, u32[]{:S(2)}, u32[]{:S(2)}) %collective-permute-start.3) | collective-permute-done | bytes 131104 | tf_op jit(solution)/shard_map/ppermute | solution.py:416
  58.8 0.7 shard_map.25
  59.5 11.6 %all_to_all.17.a_ref = f32[16,16,128]{2,1,0:T(8,128)S(1)} all-to-all(f32[16,16,128]{2,1,0:T(8,128)S(1)} %broadcast_in_dim.8), channel_id=1, replica_groups=mesh['space'=48,'vel'=16] {'vel'}, dimensions={0} | all-to-all | bytes 262144 | tf_op jit(solution)/shard_map/all_to_all | solution.py:414
  71.2 0.3 shard_map.26
  71.5 1.2 %shard_map.27 = (f32[16,128,128]{2,1,0:T(8,128)S(1)}, f32[8,32,128]{2,1,0:T(8,128)S(1)}) custom-call(f32[128,128]{1,0:T(8,128)S(1)} %get-tuple-element.49.f_ref, f32[16,128,128]{2,1,0:T(8,128)S(1)} %get-tuple-element.48.g_ref, f32[8,32,128]{2,1,0:T(8,128)S(1)} %get-tuple-element.50.refs_0_, f32[8,32,128]{2,1,0:T(8,128)S(1)} %get-tuple-element.51.refs_1_), custom_call_target="tpu_custom_call" | custom-call | tf_op jit(solution)/shard_map/pallas_call | solution.py:384
  72.7 1.9 %collective-permute-start.4 = (f32[8,32,128]{2,1,0:T(8,128)S(1)}, f32[8,32,128]{2,1,0:T(8,128)S(1)}, u32[]{:S(2)}, u32[]{:S(2)}) collective-permute-start(f32[8,32,128]{2,1,0:T(8,128)S(1)} %get-tuple-element.53), channel_id=1, source_target_pairs={{0,16},{16,0},{32,48},{48,32},{64,80},{80,64},{96,112},{112,96},{1... | collective-permute-start | bytes 393224 | tf_op jit(solution)/shard_map/ppermute | solution.py:418
  74.7 3.5 %collective-permute-start.5 = (f32[8,32,128]{2,1,0:T(8,128)S(1)}, f32[8,32,128]{2,1,0:T(8,128)S(1)}, u32[]{:S(2)}, u32[]{:S(2)}) collective-permute-start(f32[8,32,128]{2,1,0:T(8,128)S(1)} %get-tuple-element.54), channel_id=1, source_target_pairs={{16,32},{48,64},{80,96},{112,128},{144,160},{176,192},{208,224},{2... | collective-permute-start | bytes 393224 | tf_op jit(solution)/shard_map/ppermute | solution.py:416
  78.2 1.1 %shard_map.28.s_ref = f32[8,256,128]{2,1,0:T(8,128)S(1)} custom-call(f32[16,128,128]{2,1,0:T(8,128)S(1)} %get-tuple-element.52.l_ref), custom_call_target="tpu_custom_call" | custom-call | tf_op jit(solution)/shard_map/pallas_call | solution.py:384
  79.2 0.0 collective-permute-done.4.ra_ref
  79.3 5.3 %collective-permute-done.5.rb_ref = f32[8,32,128]{2,1,0:T(8,128)S(1)} collective-permute-done((f32[8,32,128]{2,1,0:T(8,128)S(1)}, f32[8,32,128]{2,1,0:T(8,128)S(1)}, u32[]{:S(2)}, u32[]{:S(2)}) %collective-permute-start.5) | collective-permute-done | bytes 131104 | tf_op jit(solution)/shard_map/ppermute | solution.py:416
  84.6 1.0 %shard_map.29 = f32[8,256,128]{2,1,0:T(8,128)} custom-call(f32[8,256,128]{2,1,0:T(8,128)S(1)} %shard_map.28.s_ref, f32[8,32,128]{2,1,0:T(8,128)S(1)} %collective-permute-done.4.ra_ref, f32[8,32,128]{2,1,0:T(8,128)S(1)} %collective-permute-done.5.rb_ref), custom_call_target="tpu_custom_call" | custom-call | tf_op jit(solution)/shard_map/pallas_call | solution.py:384
  (3 shorter events, 0.1 us)
Async XLA Ops:
  21.1 8.8 %collective-permute-start = (f32[8,32,128]{2,1,0:T(8,128)S(1)}, f32[8,32,128]{2,1,0:T(8,128)S(1)}, u32[]{:S(2)}, u32[]{:S(2)}) collective-permute-start(f32[8,32,128]{2,1,0:T(8,128)S(1)} %get-tuple-element.36), channel_id=1, source_target_pairs={{0,16},{16,0},{32,48},{48,32},{64,80},{80,64},{96,112},{112,96},{1... | collective-permute-start | bytes 393224 | tf_op jit(solution)/shard_map/ppermute | solution.py:418
  23.1 9.9 %collective-permute-start.1 = (f32[8,32,128]{2,1,0:T(8,128)S(1)}, f32[8,32,128]{2,1,0:T(8,128)S(1)}, u32[]{:S(2)}, u32[]{:S(2)}) collective-permute-start(f32[8,32,128]{2,1,0:T(8,128)S(1)} %get-tuple-element.37), channel_id=1, source_target_pairs={{16,32},{48,64},{80,96},{112,128},{144,160},{176,192},{208,224},{2... | collective-permute-start | bytes 393224 | tf_op jit(solution)/shard_map/ppermute | solution.py:416
  46.9 7.5 %collective-permute-start.2 = (f32[8,32,128]{2,1,0:T(8,128)S(1)}, f32[8,32,128]{2,1,0:T(8,128)S(1)}, u32[]{:S(2)}, u32[]{:S(2)}) collective-permute-start(f32[8,32,128]{2,1,0:T(8,128)S(1)} %get-tuple-element.45), channel_id=1, source_target_pairs={{0,16},{16,0},{32,48},{48,32},{64,80},{80,64},{96,112},{112,96},{1... | collective-permute-start | bytes 393224 | tf_op jit(solution)/shard_map/ppermute | solution.py:418
  48.9 9.9 %collective-permute-start.3 = (f32[8,32,128]{2,1,0:T(8,128)S(1)}, f32[8,32,128]{2,1,0:T(8,128)S(1)}, u32[]{:S(2)}, u32[]{:S(2)}) collective-permute-start(f32[8,32,128]{2,1,0:T(8,128)S(1)} %get-tuple-element.46), channel_id=1, source_target_pairs={{16,32},{48,64},{80,96},{112,128},{144,160},{176,192},{208,224},{2... | collective-permute-start | bytes 393224 | tf_op jit(solution)/shard_map/ppermute | solution.py:416
  72.7 6.5 %collective-permute-start.4 = (f32[8,32,128]{2,1,0:T(8,128)S(1)}, f32[8,32,128]{2,1,0:T(8,128)S(1)}, u32[]{:S(2)}, u32[]{:S(2)}) collective-permute-start(f32[8,32,128]{2,1,0:T(8,128)S(1)} %get-tuple-element.53), channel_id=1, source_target_pairs={{0,16},{16,0},{32,48},{48,32},{64,80},{80,64},{96,112},{112,96},{1... | collective-permute-start | bytes 393224 | tf_op jit(solution)/shard_map/ppermute | solution.py:418
  74.7 9.9 %collective-permute-start.5 = (f32[8,32,128]{2,1,0:T(8,128)S(1)}, f32[8,32,128]{2,1,0:T(8,128)S(1)}, u32[]{:S(2)}, u32[]{:S(2)}) collective-permute-start(f32[8,32,128]{2,1,0:T(8,128)S(1)} %get-tuple-element.54), channel_id=1, source_target_pairs={{16,32},{48,64},{80,96},{112,128},{144,160},{176,192},{208,224},{2... | collective-permute-start | bytes 393224 | tf_op jit(solution)/shard_map/ppermute | solution.py:416

commit v4 on v3

--- a/solution.py
+++ b/solution.py
@@ -92,12 +92,11 @@
     return lax.axis_index("space") % 2 == 0
 
 
-def plane(y):
-    return (slice(None), pl.ds(y * 64, 64), slice(None))
-
-
 def first_kernel(d_hbm, g_ref, w_ref, m_ref, d_ref, sems):
-    copies = [pltpu.make_async_copy(d_hbm.at[plane(y)], d_ref.at[plane(y)], sems.at[y]) for y in range(4)]
+    copies = []
+    for k in range(8):
+        part = (slice(None), pl.ds(k * 32, 32), slice(None))
+        copies.append(pltpu.make_async_copy(d_hbm.at[part], d_ref.at[part], sems.at[k]))
     for copy in copies:
         copy.start()
     xabs = xabs_here()
@@ -118,14 +117,13 @@
                 tiles.append(QUAD * tile)
             for k, part in enumerate(split(jnp.concatenate(tiles))):
                 w_ref[pl.ds(k * 16, 16), pl.ds(half * 1024 + block * 128, 128)] = part
-    for y in range(4):
-        copies[y].wait()
-        for z in range(4):
-            yz = 4 * y + z
+    for k in range(8):
+        copies[k].wait()
+        for yz in (2 * k, 2 * k + 1):
             for block in range(8):
                 for half in range(2):
                     g_ref[half * 8 + block, pl.ds(yz * 8, 8), :] = d_ref[:, yz * 16 + block * 2 + half, :]
-        m_ref[:, y * 32 : (y + 1) * 32] = weighed(w_ref, wide(g_ref, pl.ds(y * 32, 32)))
+    m_ref[...] = weighed(w_ref, wide(g_ref, slice(None)))
 
 
 def cell_fields(m):
@@ -232,7 +230,7 @@
 
 
 def inner_kernel(f_ref, g_ref, *refs):
-    x_refs, (l_ref, ma_ref) = refs[:-2], refs[-2:]
+    sides, (l_ref, ma_ref) = refs[:-2], refs[-2:]
     xabs = xabs_here()
     own, near, far = shares(xabs)
     zero = jnp.zeros(TILE, jnp.float32)
@@ -242,6 +240,7 @@
     ]
 
     def slab(sent):
+        x_refs = sides if sent else sides[::-1]
         n_out = jnp.where(xmask(sent, 0), near, zero)
         f_out = jnp.where(xmask(sent, 1), far, zero)
 
@@ -329,23 +328,37 @@
     return jnp.where(xmask(half, 1), part, jnp.zeros(TILE, jnp.float32))
 
 
-def edge_kernel(ml_ref, ra_ref, rb_ref, w_ref, x0_ref, x1_ref, m_ref):
-    x_refs = (x0_ref, x1_ref)
-    sweep_edges(ra_ref, rb_ref, x_refs)
-    total = ml_ref[...]
+def edge_kernel(half, mi_ref, r_ref, w_ref, x_ref, m_ref):
+    zs = zspeed()
+    za, zb, zc = shares(zs)
+    zforward = zs > 0.0
+    for block in range(8):
+        ya, yb, yc = shares(yspeed(block))
+        step = -1 if block >= 4 else 1
+        cells = [r_ref[block, pl.ds(y * 8, 8), :] for y in range(4)]
+        for y in range(4):
+            mid = ya * cells[y] + yb * cells[(y + step) % 4] + yc * cells[(y + 2) % 4]
+            near = jnp.where(zforward, pltpu.roll(mid, 2, 0), pltpu.roll(mid, 6, 0))
+            x_ref[block, pl.ds(y * 8, 8), :] = za * mid + zb * near + zc * pltpu.roll(mid, 4, 0)
+    at = pl.ds(pl.multiple_of(half * 1024, 1024), 1024)
+    sums = weighed(w_ref.at[:, at], wide(x_ref, slice(None)))
     source = lax.broadcasted_iota(jnp.int32, (32, CELLS), 0)
     cell = lax.broadcasted_iota(jnp.int32, (32, CELLS), 1)
-    for half in range(2):
-        sums = weighed(w_ref.at[:, pl.ds(half * 1024, 1024)], wide(x_refs[half], slice(None)))
-        target = source // 2 * 8 + source % 2 + (0 if half else 6)
-        spread = (target == cell).astype(jnp.bfloat16)
-        for part in split(sums):
-            total = total + jnp.dot(part, spread, preferred_element_type=jnp.float32)
-    m_ref[...] = total
+    spread = (source // 2 * 8 + source % 2 + 6 * (1 - half) == cell).astype(jnp.bfloat16)
+    thirds = jnp.dot(jnp.concatenate(split(sums)), spread, preferred_element_type=jnp.float32)
+    m_ref[...] = mi_ref[...] + ((thirds[32:48, :] + thirds[16:32, :]) + thirds[0:16, :])
+
+
+def chip_edge_kernel(*refs):
+    edge_kernel(lax.axis_index("space") % 2, *refs)
+
+
+def far_edge_kernel(*refs):
+    edge_kernel(1 - lax.axis_index("space") % 2, *refs)
 
 
 def last_kernel(s_ref, ra_ref, rb_ref, o_hbm, x0_ref, x1_ref, e_ref, sems):
-    inside = pltpu.make_async_copy(s_ref.at[pl.ds(2, 4)], o_hbm.at[pl.ds(2, 4)], sems.at[4])
+    inside = pltpu.make_async_copy(s_ref.at[pl.ds(2, 4), pl.ds(0, 256)], o_hbm.at[pl.ds(2, 4)], sems.at[4])
     inside.start()
     x_refs = (x0_ref, x1_ref)
     sweep_edges(ra_ref, rb_ref, x_refs)
@@ -354,7 +367,7 @@
         for layer in range(2):
             at = layer if half else 2 + layer
             outer = layer if half else 6 + layer
-            e_ref[at] = s_ref[outer]
+            e_ref[at] = s_ref[outer, 0:256, :]
             for y in range(4):
                 for block in range(8):
                     rows = pl.ds(y * 64 + block * 2 + half, 4, stride=16)
@@ -369,6 +382,7 @@
 F32, BF16 = jnp.float32, jnp.bfloat16
 HBM = pl.BlockSpec(memory_space=pltpu.HBM)
 GRID, MESSAGE, STORED = (16, CELLS, 128), (8, 32, 128), (LAYERS, 256, 128)
+PADDED = (LAYERS, 264, 128)
 EDGES = [pltpu.VMEM(MESSAGE, F32), pltpu.VMEM(MESSAGE, F32)]
 
 
@@ -405,7 +419,7 @@
     g, weights, partial_moments = call(
         first_kernel,
         [(GRID, F32), ((48, 2048), BF16), ((16, CELLS), F32)],
-        [pltpu.VMEM(STORED, F32), pltpu.SemaphoreType.DMA((4,))],
+        [pltpu.VMEM(PADDED, F32), pltpu.SemaphoreType.DMA((8,))],
         hbm_in=True,
     )(stored.reshape(STORED))
     sides = ()
@@ -420,11 +434,12 @@
             g, inside = call(sweep_kernel, [(GRID, F32), ((16, CELLS), F32)])(
                 moved, weights
             )
-            *sides, partial_moments = call(
-                edge_kernel, [(MESSAGE, F32), (MESSAGE, F32), ((16, CELLS), F32)]
-            )(inside, got_a, got_b, weights)
+            outs = [(MESSAGE, F32), ((16, CELLS), F32)]
+            near, inside = call(chip_edge_kernel, outs)(inside, got_a, weights)
+            distant, partial_moments = call(far_edge_kernel, outs)(inside, got_b, weights)
+            sides = (near, distant)
         else:
-            (swept,) = call(last_sweep_kernel, [(STORED, F32)])(moved)
+            (swept,) = call(last_sweep_kernel, [(PADDED, F32)])(moved)
             (out,) = call(
                 last_kernel,
                 [(STORED, F32)],

time: 86 us -> 84.3 us (0.980)
  Pallas kernels: 13 us -> 11.8 us
    pallas_call x13 -> x15, Pallas kernels: 13 us -> 11.8 us  [run(): pl.pallas_call(kernel, out_shape=shapes, in_specs=[HBM if hbm_in else VME...]
  transfers between devices with their start and end apart: 6 -> 6, of which waited for: 3 -> 3; matrix products, arithmetic and copies ran while one was open for 0% -> 0% of each run, Pallas kernels for 3% -> 4%
where the time goes in v4:
time: 84.3 us; the launch traced here: 83.9 us
  blocking collectives  39.8 us (47%)
  starting transfers between devices  19.8 us (23%)
  waiting for transfers between devices  12.2 us (14%)
  Pallas kernels  11.8 us (14%)
    all_to_all x3, blocking collectives, local(): gathered = lax.all_to_all(everywhere, 'vel', 0, 0)  39.8 us
    ppermute x3, starting transfers between devices, local(): got_b = lax.ppermute(msg_b, 'space', pairs_b)  14.1 us
    ppermute x3, waiting for transfers between devices, local(): got_b = lax.ppermute(msg_b, 'space', pairs_b)  12.2 us
    pallas_call x15, Pallas kernels, run(): pl.pallas_call(kernel, out_shape=shapes, in_specs=[HBM if hbm_in else VME...  11.8 us
    ppermute x3, starting transfers between devices, local(): got_a = lax.ppermute(msg_a, 'space', pairs_a)  5.76 us
  transfers between devices with their start and end apart: 6, of which 3 were waited for; matrix products, arithmetic and copies ran while one was open for 0% of the time, Pallas kernels for 4%

profile of v4, /device:TPU:512, one launch (start us, length us, event | category | flops | bytes accessed | tf_op | source)
XLA Modules:
  0.0 83.9 jit_solution(10713112157060220764)
XLA Ops:
  0.0 2.1 %shard_map.17 = (f32[16,128,128]{2,1,0:T(8,128)S(1)}, bf16[48,2048]{1,0:T(8,128)(2,1)S(1)}, f32[16,128]{1,0:T(8,128)S(1)}) custom-call(f32[8,256,128]{2,1,0:T(8,128)} %bitcast.10), custom_call_target="tpu_custom_call" | custom-call | tf_op jit(solution)/shard_map/pallas_call | solution.py:398
  2.1 16.5 %all_to_all.15.a_ref = f32[16,16,128]{2,1,0:T(8,128)S(1)} all-to-all(f32[16,16,128]{2,1,0:T(8,128)S(1)} %broadcast_in_dim.6), channel_id=1, replica_groups=mesh['space'=48,'vel'=16] {'vel'}, dimensions={0} | all-to-all | bytes 262144 | tf_op jit(solution)/shard_map/all_to_all | solution.py:428
  18.6 0.3 shard_map.18
  19.0 1.1 %shard_map.19 = (f32[16,128,128]{2,1,0:T(8,128)S(1)}, f32[8,32,128]{2,1,0:T(8,128)S(1)}) custom-call(f32[128,128]{1,0:T(8,128)S(1)} %get-tuple-element.34.f_ref, f32[16,128,128]{2,1,0:T(8,128)S(1)} %get-tuple-element.33.g_ref), custom_call_target="tpu_custom_call" | custom-call | tf_op jit(solution)/shard_map/pallas_call | solution.py:398
  20.1 1.9 %collective-permute-start = (f32[8,32,128]{2,1,0:T(8,128)S(1)}, f32[8,32,128]{2,1,0:T(8,128)S(1)}, u32[]{:S(2)}, u32[]{:S(2)}) collective-permute-start(f32[8,32,128]{2,1,0:T(8,128)S(1)} %get-tuple-element.38), channel_id=1, source_target_pairs={{0,16},{16,0},{32,48},{48,32},{64,80},{80,64},{96,112},{112,96},{1... | collective-permute-start | bytes 393224 | tf_op jit(solution)/shard_map/ppermute | solution.py:432
  22.0 5.9 %collective-permute-start.1 = (f32[8,32,128]{2,1,0:T(8,128)S(1)}, f32[8,32,128]{2,1,0:T(8,128)S(1)}, u32[]{:S(2)}, u32[]{:S(2)}) collective-permute-start(f32[8,32,128]{2,1,0:T(8,128)S(1)} %get-tuple-element.40), channel_id=1, source_target_pairs={{16,32},{48,64},{80,96},{112,128},{144,160},{176,192},{208,224},{2... | collective-permute-start | bytes 393224 | tf_op jit(solution)/shard_map/ppermute | solution.py:430
  28.0 0.9 %shard_map.20 = (f32[16,128,128]{2,1,0:T(8,128)S(1)}, f32[16,128]{1,0:T(8,128)S(1)}) custom-call(f32[16,128,128]{2,1,0:T(8,128)S(1)} %get-tuple-element.35.l_ref, bf16[48,2048]{1,0:T(8,128)(2,1)S(1)} %get-tuple-element.36.w_ref.refs_2_), custom_call_target="tpu_custom_call" | custom-call | tf_op jit(solution)/shard_map/pallas_call | solution.py:398
  28.9 0.0 collective-permute-done.refs_1_
  28.9 0.4 shard_map.21
  29.2 2.7 %collective-permute-done.1.refs_1_ = f32[8,32,128]{2,1,0:T(8,128)S(1)} collective-permute-done((f32[8,32,128]{2,1,0:T(8,128)S(1)}, f32[8,32,128]{2,1,0:T(8,128)S(1)}, u32[]{:S(2)}, u32[]{:S(2)}) %collective-permute-start.1) | collective-permute-done | bytes 131104 | tf_op jit(solution)/shard_map/ppermute | solution.py:430
  31.9 0.3 shard_map.22
  32.3 0.1 broadcast_in_dim.7
  32.3 11.6 %all_to_all.16.a_ref = f32[16,16,128]{2,1,0:T(8,128)S(1)} all-to-all(f32[16,16,128]{2,1,0:T(8,128)S(1)} %broadcast_in_dim.7), channel_id=1, replica_groups=mesh['space'=48,'vel'=16] {'vel'}, dimensions={0} | all-to-all | bytes 262144 | tf_op jit(solution)/shard_map/all_to_all | solution.py:428
  44.0 0.3 shard_map.23
  44.3 1.2 %shard_map.24 = (f32[16,128,128]{2,1,0:T(8,128)S(1)}, f32[8,32,128]{2,1,0:T(8,128)S(1)}) custom-call(f32[128,128]{1,0:T(8,128)S(1)} %get-tuple-element.43.f_ref, f32[16,128,128]{2,1,0:T(8,128)S(1)} %get-tuple-element.42.g_ref, f32[8,32,128]{2,1,0:T(8,128)S(1)} %get-tuple-element.44.refs_0_, f32[8,32,128]{2,1,0:T(8,128)S(1)} %get-tuple-element.45.refs_1_), custom_call_target="tpu_custom_call" | custom-call | tf_op jit(solution)/shard_map/pallas_call | solution.py:398
  45.6 1.9 %collective-permute-start.2 = (f32[8,32,128]{2,1,0:T(8,128)S(1)}, f32[8,32,128]{2,1,0:T(8,128)S(1)}, u32[]{:S(2)}, u32[]{:S(2)}) collective-permute-start(f32[8,32,128]{2,1,0:T(8,128)S(1)} %get-tuple-element.48), channel_id=1, source_target_pairs={{0,16},{16,0},{32,48},{48,32},{64,80},{80,64},{96,112},{112,96},{1... | collective-permute-start | bytes 393224 | tf_op jit(solution)/shard_map/ppermute | solution.py:432
  47.5 4.6 %collective-permute-start.3 = (f32[8,32,128]{2,1,0:T(8,128)S(1)}, f32[8,32,128]{2,1,0:T(8,128)S(1)}, u32[]{:S(2)}, u32[]{:S(2)}) collective-permute-start(f32[8,32,128]{2,1,0:T(8,128)S(1)} %get-tuple-element.50), channel_id=1, source_target_pairs={{16,32},{48,64},{80,96},{112,128},{144,160},{176,192},{208,224},{2... | collective-permute-start | bytes 393224 | tf_op jit(solution)/shard_map/ppermute | solution.py:430
  52.1 0.9 %shard_map.25 = (f32[16,128,128]{2,1,0:T(8,128)S(1)}, f32[16,128]{1,0:T(8,128)S(1)}) custom-call(f32[16,128,128]{2,1,0:T(8,128)S(1)} %get-tuple-element.46.l_ref, bf16[48,2048]{1,0:T(8,128)(2,1)S(1)} %get-tuple-element.36.w_ref.refs_2_), custom_call_target="tpu_custom_call" | custom-call | tf_op jit(solution)/shard_map/pallas_call | solution.py:398
  53.0 0.0 collective-permute-done.2.refs_1_
  53.0 0.4 shard_map.26
  53.4 4.0 %collective-permute-done.3.refs_1_ = f32[8,32,128]{2,1,0:T(8,128)S(1)} collective-permute-done((f32[8,32,128]{2,1,0:T(8,128)S(1)}, f32[8,32,128]{2,1,0:T(8,128)S(1)}, u32[]{:S(2)}, u32[]{:S(2)}) %collective-permute-start.3) | collective-permute-done | bytes 131104 | tf_op jit(solution)/shard_map/ppermute | solution.py:430
  57.4 0.3 shard_map.27
  57.7 0.1 broadcast_in_dim.8
  57.8 11.6 %all_to_all.17.a_ref = f32[16,16,128]{2,1,0:T(8,128)S(1)} all-to-all(f32[16,16,128]{2,1,0:T(8,128)S(1)} %broadcast_in_dim.8), channel_id=1, replica_groups=mesh['space'=48,'vel'=16] {'vel'}, dimensions={0} | all-to-all | bytes 262144 | tf_op jit(solution)/shard_map/all_to_all | solution.py:428
  69.4 0.3 shard_map.28
  69.8 1.2 %shard_map.29 = (f32[16,128,128]{2,1,0:T(8,128)S(1)}, f32[8,32,128]{2,1,0:T(8,128)S(1)}) custom-call(f32[128,128]{1,0:T(8,128)S(1)} %get-tuple-element.53.f_ref, f32[16,128,128]{2,1,0:T(8,128)S(1)} %get-tuple-element.52.g_ref, f32[8,32,128]{2,1,0:T(8,128)S(1)} %get-tuple-element.54.refs_0_, f32[8,32,128]{2,1,0:T(8,128)S(1)} %get-tuple-element.55.refs_1_), custom_call_target="tpu_custom_call" | custom-call | tf_op jit(solution)/shard_map/pallas_call | solution.py:398
  71.0 1.9 %collective-permute-start.4 = (f32[8,32,128]{2,1,0:T(8,128)S(1)}, f32[8,32,128]{2,1,0:T(8,128)S(1)}, u32[]{:S(2)}, u32[]{:S(2)}) collective-permute-start(f32[8,32,128]{2,1,0:T(8,128)S(1)} %get-tuple-element.57), channel_id=1, source_target_pairs={{0,16},{16,0},{32,48},{48,32},{64,80},{80,64},{96,112},{112,96},{1... | collective-permute-start | bytes 393224 | tf_op jit(solution)/shard_map/ppermute | solution.py:432
  73.0 3.5 %collective-permute-start.5 = (f32[8,32,128]{2,1,0:T(8,128)S(1)}, f32[8,32,128]{2,1,0:T(8,128)S(1)}, u32[]{:S(2)}, u32[]{:S(2)}) collective-permute-start(f32[8,32,128]{2,1,0:T(8,128)S(1)} %get-tuple-element.58), channel_id=1, source_target_pairs={{16,32},{48,64},{80,96},{112,128},{144,160},{176,192},{208,224},{2... | collective-permute-start | bytes 393224 | tf_op jit(solution)/shard_map/ppermute | solution.py:430
  76.5 1.0 %shard_map.30.s_ref = f32[8,264,128]{2,1,0:T(8,128)S(1)} custom-call(f32[16,128,128]{2,1,0:T(8,128)S(1)} %get-tuple-element.56.l_ref), custom_call_target="tpu_custom_call" | custom-call | tf_op jit(solution)/shard_map/pallas_call | solution.py:398
  77.4 0.0 collective-permute-done.4.ra_ref
  77.4 5.4 %collective-permute-done.5.rb_ref = f32[8,32,128]{2,1,0:T(8,128)S(1)} collective-permute-done((f32[8,32,128]{2,1,0:T(8,128)S(1)}, f32[8,32,128]{2,1,0:T(8,128)S(1)}, u32[]{:S(2)}, u32[]{:S(2)}) %collective-permute-start.5) | collective-permute-done | bytes 131104 | tf_op jit(solution)/shard_map/ppermute | solution.py:430
  82.9 1.0 %shard_map.31 = f32[8,256,128]{2,1,0:T(8,128)} custom-call(f32[8,264,128]{2,1,0:T(8,128)S(1)} %shard_map.30.s_ref, f32[8,32,128]{2,1,0:T(8,128)S(1)} %collective-permute-done.4.ra_ref, f32[8,32,128]{2,1,0:T(8,128)S(1)} %collective-permute-done.5.rb_ref), custom_call_target="tpu_custom_call" | custom-call | tf_op jit(solution)/shard_map/pallas_call | solution.py:398
  (1 shorter events, 0.0 us)
Async XLA Ops:
  20.1 8.8 %collective-permute-start = (f32[8,32,128]{2,1,0:T(8,128)S(1)}, f32[8,32,128]{2,1,0:T(8,128)S(1)}, u32[]{:S(2)}, u32[]{:S(2)}) collective-permute-start(f32[8,32,128]{2,1,0:T(8,128)S(1)} %get-tuple-element.38), channel_id=1, source_target_pairs={{0,16},{16,0},{32,48},{48,32},{64,80},{80,64},{96,112},{112,96},{1... | collective-permute-start | bytes 393224 | tf_op jit(solution)/shard_map/ppermute | solution.py:432
  22.0 9.9 %collective-permute-start.1 = (f32[8,32,128]{2,1,0:T(8,128)S(1)}, f32[8,32,128]{2,1,0:T(8,128)S(1)}, u32[]{:S(2)}, u32[]{:S(2)}) collective-permute-start(f32[8,32,128]{2,1,0:T(8,128)S(1)} %get-tuple-element.40), channel_id=1, source_target_pairs={{16,32},{48,64},{80,96},{112,128},{144,160},{176,192},{208,224},{2... | collective-permute-start | bytes 393224 | tf_op jit(solution)/shard_map/ppermute | solution.py:430
  45.6 7.5 %collective-permute-start.2 = (f32[8,32,128]{2,1,0:T(8,128)S(1)}, f32[8,32,128]{2,1,0:T(8,128)S(1)}, u32[]{:S(2)}, u32[]{:S(2)}) collective-permute-start(f32[8,32,128]{2,1,0:T(8,128)S(1)} %get-tuple-element.48), channel_id=1, source_target_pairs={{0,16},{16,0},{32,48},{48,32},{64,80},{80,64},{96,112},{112,96},{1... | collective-permute-start | bytes 393224 | tf_op jit(solution)/shard_map/ppermute | solution.py:432
  47.5 9.9 %collective-permute-start.3 = (f32[8,32,128]{2,1,0:T(8,128)S(1)}, f32[8,32,128]{2,1,0:T(8,128)S(1)}, u32[]{:S(2)}, u32[]{:S(2)}) collective-permute-start(f32[8,32,128]{2,1,0:T(8,128)S(1)} %get-tuple-element.50), channel_id=1, source_target_pairs={{16,32},{48,64},{80,96},{112,128},{144,160},{176,192},{208,224},{2... | collective-permute-start | bytes 393224 | tf_op jit(solution)/shard_map/ppermute | solution.py:430
  71.0 6.4 %collective-permute-start.4 = (f32[8,32,128]{2,1,0:T(8,128)S(1)}, f32[8,32,128]{2,1,0:T(8,128)S(1)}, u32[]{:S(2)}, u32[]{:S(2)}) collective-permute-start(f32[8,32,128]{2,1,0:T(8,128)S(1)} %get-tuple-element.57), channel_id=1, source_target_pairs={{0,16},{16,0},{32,48},{48,32},{64,80},{80,64},{96,112},{112,96},{1... | collective-permute-start | bytes 393224 | tf_op jit(solution)/shard_map/ppermute | solution.py:432
  73.0 9.9 %collective-permute-start.5 = (f32[8,32,128]{2,1,0:T(8,128)S(1)}, f32[8,32,128]{2,1,0:T(8,128)S(1)}, u32[]{:S(2)}, u32[]{:S(2)}) collective-permute-start(f32[8,32,128]{2,1,0:T(8,128)S(1)} %get-tuple-element.58), channel_id=1, source_target_pairs={{16,32},{48,64},{80,96},{112,128},{144,160},{176,192},{208,224},{2... | collective-permute-start | bytes 393224 | tf_op jit(solution)/shard_map/ppermute | solution.py:430

commit v5 on v4

--- a/solution.py
+++ b/solution.py
@@ -15,7 +15,7 @@
 LAM = 1.9 / ((NV - 1) * SPEED_LIMIT / NV)
 QUAD = SPACING**3 / (2.0 * math.pi) ** 1.5
 LOG2E = math.log2(math.e)
-LAYERS, CELLS = 8, 128
+LAYERS, NYZ, CELLS = 8, 16, 128
 VMEM = pl.BlockSpec(memory_space=pltpu.VMEM)
 TILE = (8, 128)
 
@@ -120,10 +120,12 @@
     for k in range(8):
         copies[k].wait()
         for yz in (2 * k, 2 * k + 1):
-            for block in range(8):
-                for half in range(2):
-                    g_ref[half * 8 + block, pl.ds(yz * 8, 8), :] = d_ref[:, yz * 16 + block * 2 + half, :]
-    m_ref[...] = weighed(w_ref, wide(g_ref, slice(None)))
+            for group in range(2):
+                turned = jnp.swapaxes(d_ref[:, pl.ds(yz * 16 + group * 8, 8), :], 0, 1)
+                for k in range(8):
+                    block, half = group * 4 + k // 2, k % 2
+                    g_ref[half * 8 + block, pl.ds(yz * 8, 8), :] = turned[k]
+    m_ref[...] = jnp.broadcast_to(weighed(w_ref, wide(g_ref, slice(None)))[None], m_ref.shape)
 
 
 def cell_fields(m):
@@ -229,8 +231,7 @@
     pl.when(jnp.logical_not(even))(lambda: message(1))
 
 
-def inner_kernel(f_ref, g_ref, *refs):
-    sides, (l_ref, ma_ref) = refs[:-2], refs[-2:]
+def inner_kernel(f_ref, g_ref, sides, l_ref, ma_ref, on_even):
     xabs = xabs_here()
     own, near, far = shares(xabs)
     zero = jnp.zeros(TILE, jnp.float32)
@@ -269,8 +270,18 @@
         lax.fori_loop(0, 4, per_y, 0)
 
     even = even_here()
-    pl.when(even)(lambda: slab(1))
-    pl.when(jnp.logical_not(even))(lambda: slab(0))
+    if on_even:
+        pl.when(even)(lambda: slab(1))
+    else:
+        pl.when(jnp.logical_not(even))(lambda: slab(0))
+
+
+def odd_inner_kernel(f_ref, g_ref, *refs):
+    inner_kernel(f_ref, g_ref, refs[:-2], *refs[-2:], False)
+
+
+def even_inner_kernel(_l, _ma, f_ref, g_ref, *refs):
+    inner_kernel(f_ref, g_ref, refs[:-2], *refs[-2:], True)
 
 
 def sweep_cells(l_ref, store):
@@ -295,11 +306,15 @@
     m_ref[...] = weighed(w_ref, wide(g_ref, slice(None)))
 
 
-def last_sweep_kernel(l_ref, o_ref):
+def last_sweep_kernel(l_ref, o_ref, g_ref):
     def store(yz, half, block, value):
-        o_ref[:, yz * 16 + block * 2 + half, :] = value
+        g_ref[half * 8 + block, pl.ds(yz * 8, 8), :] = value
 
     sweep_cells(l_ref, store)
+    for yz in range(NYZ):
+        for group in range(2):
+            rows = [g_ref[k % 2 * 8 + group * 4 + k // 2, pl.ds(yz * 8, 8), :] for k in range(8)]
+            o_ref[:, pl.ds(yz * 16 + group * 8, 8), :] = jnp.swapaxes(jnp.stack(rows), 0, 1)
 
 
 def sweep_edges(ra_ref, rb_ref, x_refs):
@@ -346,7 +361,8 @@
     cell = lax.broadcasted_iota(jnp.int32, (32, CELLS), 1)
     spread = (source // 2 * 8 + source % 2 + 6 * (1 - half) == cell).astype(jnp.bfloat16)
     thirds = jnp.dot(jnp.concatenate(split(sums)), spread, preferred_element_type=jnp.float32)
-    m_ref[...] = mi_ref[...] + ((thirds[32:48, :] + thirds[16:32, :]) + thirds[0:16, :])
+    total = mi_ref[...] + ((thirds[32:48, :] + thirds[16:32, :]) + thirds[0:16, :])
+    m_ref[...] = total if len(m_ref.shape) == 2 else jnp.broadcast_to(total[None], m_ref.shape)
 
 
 def chip_edge_kernel(*refs):
@@ -358,7 +374,7 @@
 
 
 def last_kernel(s_ref, ra_ref, rb_ref, o_hbm, x0_ref, x1_ref, e_ref, sems):
-    inside = pltpu.make_async_copy(s_ref.at[pl.ds(2, 4), pl.ds(0, 256)], o_hbm.at[pl.ds(2, 4)], sems.at[4])
+    inside = pltpu.make_async_copy(s_ref.at[pl.ds(2, 4)], o_hbm.at[pl.ds(2, 4)], sems.at[4])
     inside.start()
     x_refs = (x0_ref, x1_ref)
     sweep_edges(ra_ref, rb_ref, x_refs)
@@ -367,7 +383,7 @@
         for layer in range(2):
             at = layer if half else 2 + layer
             outer = layer if half else 6 + layer
-            e_ref[at] = s_ref[outer, 0:256, :]
+            e_ref[at] = s_ref[outer]
             for y in range(4):
                 for block in range(8):
                     rows = pl.ds(y * 64 + block * 2 + half, 4, stride=16)
@@ -382,7 +398,7 @@
 F32, BF16 = jnp.float32, jnp.bfloat16
 HBM = pl.BlockSpec(memory_space=pltpu.HBM)
 GRID, MESSAGE, STORED = (16, CELLS, 128), (8, 32, 128), (LAYERS, 256, 128)
-PADDED = (LAYERS, 264, 128)
+EVERYWHERE = (16, 16, CELLS)
 EDGES = [pltpu.VMEM(MESSAGE, F32), pltpu.VMEM(MESSAGE, F32)]
 
 
@@ -410,7 +426,6 @@
 
 def local(distribution):
     layers, breadth, height, halves, _ = distribution.shape
-    vel_count = lax.axis_size("vel")
     space_count = lax.axis_size("space")
     stored = distribution.reshape(layers, breadth, height, halves, 8, 128).transpose(0, 1, 2, 4, 3, 5)
     pairs_a = [(i, i ^ 1) for i in range(space_count)]
@@ -418,17 +433,18 @@
     pairs_b = pairs_b + [(j, i) for i, j in pairs_b]
     g, weights, partial_moments = call(
         first_kernel,
-        [(GRID, F32), ((48, 2048), BF16), ((16, CELLS), F32)],
-        [pltpu.VMEM(PADDED, F32), pltpu.SemaphoreType.DMA((8,))],
+        [(GRID, F32), ((48, 2048), BF16), (EVERYWHERE, F32)],
+        [pltpu.VMEM(STORED, F32), pltpu.SemaphoreType.DMA((8,))],
         hbm_in=True,
     )(stored.reshape(STORED))
     sides = ()
     for step in range(STEPS):
-        everywhere = jnp.broadcast_to(partial_moments[None], (vel_count, 16, CELLS))
-        gathered = lax.all_to_all(everywhere, "vel", 0, 0)
+        gathered = lax.all_to_all(partial_moments, "vel", 0, 0)
         fields, msg_b = call(outer_kernel, [((128, 128), F32), (MESSAGE, F32)])(gathered, g)
+        inner_outs = [(GRID, F32), (MESSAGE, F32)]
+        begun = call(odd_inner_kernel, inner_outs)(fields, g, *sides)
         got_b = lax.ppermute(msg_b, "space", pairs_b)
-        moved, msg_a = call(inner_kernel, [(GRID, F32), (MESSAGE, F32)])(fields, g, *sides)
+        moved, msg_a = call(even_inner_kernel, inner_outs, input_output_aliases={0: 0, 1: 1})(*begun, fields, g, *sides)
         got_a = lax.ppermute(msg_a, "space", pairs_a)
         if step + 1 < STEPS:
             g, inside = call(sweep_kernel, [(GRID, F32), ((16, CELLS), F32)])(
@@ -436,10 +452,12 @@
             )
             outs = [(MESSAGE, F32), ((16, CELLS), F32)]
             near, inside = call(chip_edge_kernel, outs)(inside, got_a, weights)
-            distant, partial_moments = call(far_edge_kernel, outs)(inside, got_b, weights)
+            distant, partial_moments = call(far_edge_kernel, [(MESSAGE, F32), (EVERYWHERE, F32)])(
+                inside, got_b, weights
+            )
             sides = (near, distant)
         else:
-            (swept,) = call(last_sweep_kernel, [(PADDED, F32)])(moved)
+            (swept,) = call(last_sweep_kernel, [(STORED, F32)], [pltpu.VMEM(GRID, F32)])(moved)
             (out,) = call(
                 last_kernel,
                 [(STORED, F32)],

time: 84.3 us -> 81.6 us (0.968)
  the two profiles are of different devices: /device:TPU:512 before, /device:TPU:199 now
where the time goes in v5:
time: 81.6 us; the launch traced here: 81.3 us
  blocking collectives  35.3 us (43%)
  starting transfers between devices  29.5 us (36%)
  Pallas kernels  11.5 us (14%)
  waiting for transfers between devices  4.83 us (6%)
    all_to_all x3, blocking collectives, local(): gathered = lax.all_to_all(partial_moments, 'vel', 0, 0)  35.3 us
    ppermute x3, starting transfers between devices, local(): got_b = lax.ppermute(msg_b, 'space', pairs_b)  21.6 us
    pallas_call x18, Pallas kernels, run(): pl.pallas_call(kernel, out_shape=shapes, in_specs=[HBM if hbm_in else VME...  11.5 us
    ppermute x3, starting transfers between devices, local(): got_a = lax.ppermute(msg_a, 'space', pairs_a)  7.84 us
    ppermute x3, waiting for transfers between devices, local(): got_b = lax.ppermute(msg_b, 'space', pairs_b)  4.12 us
  transfers between devices with their start and end apart: 6, of which 3 were waited for; matrix products, arithmetic and copies ran while one was open for 0% of the time, Pallas kernels for 5%

profile of v5, /device:TPU:199, one launch (start us, length us, event | category | flops | bytes accessed | tf_op | source)
XLA Modules:
  0.0 81.3 jit_solution(7570395745074632129)
XLA Ops:
  0.0 1.9 %shard_map.17 = (f32[16,128,128]{2,1,0:T(8,128)S(1)}, bf16[48,2048]{1,0:T(8,128)(2,1)S(1)}, f32[16,16,128]{2,1,0:T(8,128)S(1)}) custom-call(f32[8,256,128]{2,1,0:T(8,128)} %bitcast.10), custom_call_target="tpu_custom_call" | custom-call | tf_op jit(solution)/shard_map/pallas_call | solution.py:414
  1.9 14.5 %all_to_all.15.a_ref = f32[16,16,128]{2,1,0:T(8,128)S(1)} all-to-all(f32[16,16,128]{2,1,0:T(8,128)S(1)} %get-tuple-element.38), channel_id=1, replica_groups=mesh['space'=48,'vel'=16] {'vel'}, dimensions={0} | all-to-all | bytes 262144 | tf_op jit(solution)/shard_map/all_to_all | solution.py:442
  16.4 0.3 shard_map.18
  16.8 1.1 %shard_map.19 = (f32[16,128,128]{2,1,0:T(8,128)S(1)}, f32[8,32,128]{2,1,0:T(8,128)S(1)}) custom-call(f32[128,128]{1,0:T(8,128)S(1)} %get-tuple-element.40.f_ref, f32[16,128,128]{2,1,0:T(8,128)S(1)} %get-tuple-element.39.g_ref), custom_call_target="tpu_custom_call" | custom-call | tf_op jit(solution)/shard_map/pallas_call | solution.py:414
  17.9 4.0 %collective-permute-start = (f32[8,32,128]{2,1,0:T(8,128)S(1)}, f32[8,32,128]{2,1,0:T(8,128)S(1)}, u32[]{:S(2)}, u32[]{:S(2)}) collective-permute-start(f32[8,32,128]{2,1,0:T(8,128)S(1)} %get-tuple-element.46), channel_id=1, source_target_pairs={{0,16},{16,0},{32,48},{48,32},{64,80},{80,64},{96,112},{112,96},{1... | collective-permute-start | bytes 393224 | tf_op jit(solution)/shard_map/ppermute | solution.py:448
  22.0 5.9 %collective-permute-start.1 = (f32[8,32,128]{2,1,0:T(8,128)S(1)}, f32[8,32,128]{2,1,0:T(8,128)S(1)}, u32[]{:S(2)}, u32[]{:S(2)}) collective-permute-start(f32[8,32,128]{2,1,0:T(8,128)S(1)} %get-tuple-element.48), channel_id=1, source_target_pairs={{16,32},{48,64},{80,96},{112,128},{144,160},{176,192},{208,224},{2... | collective-permute-start | bytes 393224 | tf_op jit(solution)/shard_map/ppermute | solution.py:446
  27.9 0.9 %shard_map.21 = (f32[16,128,128]{2,1,0:T(8,128)S(1)}, f32[16,128]{1,0:T(8,128)S(1)}) custom-call(f32[16,128,128]{2,1,0:T(8,128)S(1)} %get-tuple-element.43.l_ref, bf16[48,2048]{1,0:T(8,128)(2,1)S(1)} %get-tuple-element.44.w_ref.refs_2_), custom_call_target="tpu_custom_call" | custom-call | tf_op jit(solution)/shard_map/pallas_call | solution.py:414
  28.8 0.0 collective-permute-done.refs_1_
  28.8 0.4 shard_map.22
  29.1 2.7 %collective-permute-done.1.refs_1_ = f32[8,32,128]{2,1,0:T(8,128)S(1)} collective-permute-done((f32[8,32,128]{2,1,0:T(8,128)S(1)}, f32[8,32,128]{2,1,0:T(8,128)S(1)}, u32[]{:S(2)}, u32[]{:S(2)}) %collective-permute-start.1) | collective-permute-done | bytes 131104 | tf_op jit(solution)/shard_map/ppermute | solution.py:446
  31.9 0.4 shard_map.23
  32.3 10.2 %all_to_all.16.a_ref = f32[16,16,128]{2,1,0:T(8,128)S(1)} all-to-all(f32[16,16,128]{2,1,0:T(8,128)S(1)} %get-tuple-element.49), channel_id=1, replica_groups=mesh['space'=48,'vel'=16] {'vel'}, dimensions={0} | all-to-all | bytes 262144 | tf_op jit(solution)/shard_map/all_to_all | solution.py:442
  42.5 0.3 shard_map.24
  42.8 1.2 %shard_map.25 = (f32[16,128,128]{2,1,0:T(8,128)S(1)}, f32[8,32,128]{2,1,0:T(8,128)S(1)}) custom-call(f32[128,128]{1,0:T(8,128)S(1)} %get-tuple-element.51.f_ref, f32[16,128,128]{2,1,0:T(8,128)S(1)} %get-tuple-element.50.g_ref, f32[8,32,128]{2,1,0:T(8,128)S(1)} %get-tuple-element.52.refs_0_, f32[8,32,128]{2,1,0:T(8,128)S(1)} %get-tuple-element.53.refs_1_), custom_call_target="tpu_custom_call" | custom-call | tf_op jit(solution)/shard_map/pallas_call | solution.py:414
  44.1 1.9 %collective-permute-start.2 = (f32[8,32,128]{2,1,0:T(8,128)S(1)}, f32[8,32,128]{2,1,0:T(8,128)S(1)}, u32[]{:S(2)}, u32[]{:S(2)}) collective-permute-start(f32[8,32,128]{2,1,0:T(8,128)S(1)} %get-tuple-element.58), channel_id=1, source_target_pairs={{0,16},{16,0},{32,48},{48,32},{64,80},{80,64},{96,112},{112,96},{1... | collective-permute-start | bytes 393224 | tf_op jit(solution)/shard_map/ppermute | solution.py:448
  46.0 7.4 %collective-permute-start.3 = (f32[8,32,128]{2,1,0:T(8,128)S(1)}, f32[8,32,128]{2,1,0:T(8,128)S(1)}, u32[]{:S(2)}, u32[]{:S(2)}) collective-permute-start(f32[8,32,128]{2,1,0:T(8,128)S(1)} %get-tuple-element.60), channel_id=1, source_target_pairs={{16,32},{48,64},{80,96},{112,128},{144,160},{176,192},{208,224},{2... | collective-permute-start | bytes 393224 | tf_op jit(solution)/shard_map/ppermute | solution.py:446
  53.4 0.9 %shard_map.27 = (f32[16,128,128]{2,1,0:T(8,128)S(1)}, f32[16,128]{1,0:T(8,128)S(1)}) custom-call(f32[16,128,128]{2,1,0:T(8,128)S(1)} %get-tuple-element.56.l_ref, bf16[48,2048]{1,0:T(8,128)(2,1)S(1)} %get-tuple-element.44.w_ref.refs_2_), custom_call_target="tpu_custom_call" | custom-call | tf_op jit(solution)/shard_map/pallas_call | solution.py:414
  54.3 0.0 collective-permute-done.2.refs_1_
  54.3 0.4 shard_map.28
  54.7 1.4 %collective-permute-done.3.refs_1_ = f32[8,32,128]{2,1,0:T(8,128)S(1)} collective-permute-done((f32[8,32,128]{2,1,0:T(8,128)S(1)}, f32[8,32,128]{2,1,0:T(8,128)S(1)}, u32[]{:S(2)}, u32[]{:S(2)}) %collective-permute-start.3) | collective-permute-done | bytes 131104 | tf_op jit(solution)/shard_map/ppermute | solution.py:446
  56.1 0.4 shard_map.29
  56.5 10.6 %all_to_all.17.a_ref = f32[16,16,128]{2,1,0:T(8,128)S(1)} all-to-all(f32[16,16,128]{2,1,0:T(8,128)S(1)} %get-tuple-element.61), channel_id=1, replica_groups=mesh['space'=48,'vel'=16] {'vel'}, dimensions={0} | all-to-all | bytes 262144 | tf_op jit(solution)/shard_map/all_to_all | solution.py:442
  67.1 0.3 shard_map.30
  67.4 8.3 %collective-permute-start.5 = (f32[8,32,128]{2,1,0:T(8,128)S(1)}, f32[8,32,128]{2,1,0:T(8,128)S(1)}, u32[]{:S(2)}, u32[]{:S(2)}) collective-permute-start(f32[8,32,128]{2,1,0:T(8,128)S(1)} %get-tuple-element.70), channel_id=1, source_target_pairs={{16,32},{48,64},{80,96},{112,128},{144,160},{176,192},{208,224},{2... | collective-permute-start | bytes 393224 | tf_op jit(solution)/shard_map/ppermute | solution.py:446
  75.7 1.2 %shard_map.31 = (f32[16,128,128]{2,1,0:T(8,128)S(1)}, f32[8,32,128]{2,1,0:T(8,128)S(1)}) custom-call(f32[128,128]{1,0:T(8,128)S(1)} %get-tuple-element.63.f_ref, f32[16,128,128]{2,1,0:T(8,128)S(1)} %get-tuple-element.62.g_ref, f32[8,32,128]{2,1,0:T(8,128)S(1)} %get-tuple-element.64.refs_0_, f32[8,32,128]{2,1,0:T(8,128)S(1)} %get-tuple-element.65.refs_1_), custom_call_target="tpu_custom_call" | custom-call | tf_op jit(solution)/shard_map/pallas_call | solution.py:414
  77.0 1.9 %collective-permute-start.4 = (f32[8,32,128]{2,1,0:T(8,128)S(1)}, f32[8,32,128]{2,1,0:T(8,128)S(1)}, u32[]{:S(2)}, u32[]{:S(2)}) collective-permute-start(f32[8,32,128]{2,1,0:T(8,128)S(1)} %get-tuple-element.69), channel_id=1, source_target_pairs={{0,16},{16,0},{32,48},{48,32},{64,80},{80,64},{96,112},{112,96},{1... | collective-permute-start | bytes 393224 | tf_op jit(solution)/shard_map/ppermute | solution.py:448
  78.9 0.6 shard_map.33.s_ref
  79.5 0.0 collective-permute-done.5.rb_ref
  79.5 0.7 collective-permute-done.4.ra_ref
  80.2 1.0 %shard_map.34 = f32[8,256,128]{2,1,0:T(8,128)} custom-call(f32[8,256,128]{2,1,0:T(8,128)S(1)} %shard_map.33.s_ref, f32[8,32,128]{2,1,0:T(8,128)S(1)} %collective-permute-done.4.ra_ref, f32[8,32,128]{2,1,0:T(8,128)S(1)} %collective-permute-done.5.rb_ref), custom_call_target="tpu_custom_call" | custom-call | tf_op jit(solution)/shard_map/pallas_call | solution.py:414
  (3 shorter events, 0.1 us)
Async XLA Ops:
  17.9 10.8 %collective-permute-start = (f32[8,32,128]{2,1,0:T(8,128)S(1)}, f32[8,32,128]{2,1,0:T(8,128)S(1)}, u32[]{:S(2)}, u32[]{:S(2)}) collective-permute-start(f32[8,32,128]{2,1,0:T(8,128)S(1)} %get-tuple-element.46), channel_id=1, source_target_pairs={{0,16},{16,0},{32,48},{48,32},{64,80},{80,64},{96,112},{112,96},{1... | collective-permute-start | bytes 393224 | tf_op jit(solution)/shard_map/ppermute | solution.py:448
  22.0 9.9 %collective-permute-start.1 = (f32[8,32,128]{2,1,0:T(8,128)S(1)}, f32[8,32,128]{2,1,0:T(8,128)S(1)}, u32[]{:S(2)}, u32[]{:S(2)}) collective-permute-start(f32[8,32,128]{2,1,0:T(8,128)S(1)} %get-tuple-element.48), channel_id=1, source_target_pairs={{16,32},{48,64},{80,96},{112,128},{144,160},{176,192},{208,224},{2... | collective-permute-start | bytes 393224 | tf_op jit(solution)/shard_map/ppermute | solution.py:446
  44.1 10.2 %collective-permute-start.2 = (f32[8,32,128]{2,1,0:T(8,128)S(1)}, f32[8,32,128]{2,1,0:T(8,128)S(1)}, u32[]{:S(2)}, u32[]{:S(2)}) collective-permute-start(f32[8,32,128]{2,1,0:T(8,128)S(1)} %get-tuple-element.58), channel_id=1, source_target_pairs={{0,16},{16,0},{32,48},{48,32},{64,80},{80,64},{96,112},{112,96},{1... | collective-permute-start | bytes 393224 | tf_op jit(solution)/shard_map/ppermute | solution.py:448
  46.0 10.0 %collective-permute-start.3 = (f32[8,32,128]{2,1,0:T(8,128)S(1)}, f32[8,32,128]{2,1,0:T(8,128)S(1)}, u32[]{:S(2)}, u32[]{:S(2)}) collective-permute-start(f32[8,32,128]{2,1,0:T(8,128)S(1)} %get-tuple-element.60), channel_id=1, source_target_pairs={{16,32},{48,64},{80,96},{112,128},{144,160},{176,192},{208,224},{2... | collective-permute-start | bytes 393224 | tf_op jit(solution)/shard_map/ppermute | solution.py:446
  67.4 12.1 %collective-permute-start.5 = (f32[8,32,128]{2,1,0:T(8,128)S(1)}, f32[8,32,128]{2,1,0:T(8,128)S(1)}, u32[]{:S(2)}, u32[]{:S(2)}) collective-permute-start(f32[8,32,128]{2,1,0:T(8,128)S(1)} %get-tuple-element.70), channel_id=1, source_target_pairs={{16,32},{48,64},{80,96},{112,128},{144,160},{176,192},{208,224},{2... | collective-permute-start | bytes 393224 | tf_op jit(solution)/shard_map/ppermute | solution.py:446
  77.0 3.2 %collective-permute-start.4 = (f32[8,32,128]{2,1,0:T(8,128)S(1)}, f32[8,32,128]{2,1,0:T(8,128)S(1)}, u32[]{:S(2)}, u32[]{:S(2)}) collective-permute-start(f32[8,32,128]{2,1,0:T(8,128)S(1)} %get-tuple-element.69), channel_id=1, source_target_pairs={{0,16},{16,0},{32,48},{48,32},{64,80},{80,64},{96,112},{112,96},{1... | collective-permute-start | bytes 393224 | tf_op jit(solution)/shard_map/ppermute | solution.py:448

commit v6 on v5

--- a/solution.py
+++ b/solution.py
@@ -231,7 +231,8 @@
     pl.when(jnp.logical_not(even))(lambda: message(1))
 
 
-def inner_kernel(f_ref, g_ref, sides, l_ref, ma_ref, on_even):
+def inner_kernel(f_ref, g_ref, *refs):
+    sides, (l_ref, ma_ref) = refs[:-2], refs[-2:]
     xabs = xabs_here()
     own, near, far = shares(xabs)
     zero = jnp.zeros(TILE, jnp.float32)
@@ -270,18 +271,8 @@
         lax.fori_loop(0, 4, per_y, 0)
 
     even = even_here()
-    if on_even:
-        pl.when(even)(lambda: slab(1))
-    else:
-        pl.when(jnp.logical_not(even))(lambda: slab(0))
-
-
-def odd_inner_kernel(f_ref, g_ref, *refs):
-    inner_kernel(f_ref, g_ref, refs[:-2], *refs[-2:], False)
-
-
-def even_inner_kernel(_l, _ma, f_ref, g_ref, *refs):
-    inner_kernel(f_ref, g_ref, refs[:-2], *refs[-2:], True)
+    pl.when(even)(lambda: slab(1))
+    pl.when(jnp.logical_not(even))(lambda: slab(0))
 
 
 def sweep_cells(l_ref, store):
@@ -441,10 +432,8 @@
     for step in range(STEPS):
         gathered = lax.all_to_all(partial_moments, "vel", 0, 0)
         fields, msg_b = call(outer_kernel, [((128, 128), F32), (MESSAGE, F32)])(gathered, g)
-        inner_outs = [(GRID, F32), (MESSAGE, F32)]
-        begun = call(odd_inner_kernel, inner_outs)(fields, g, *sides)
         got_b = lax.ppermute(msg_b, "space", pairs_b)
-        moved, msg_a = call(even_inner_kernel, inner_outs, input_output_aliases={0: 0, 1: 1})(*begun, fields, g, *sides)
+        moved, msg_a = call(inner_kernel, [(GRID, F32), (MESSAGE, F32)])(fields, g, *sides)
         got_a = lax.ppermute(msg_a, "space", pairs_a)
         if step + 1 < STEPS:
             g, inside = call(sweep_kernel, [(GRID, F32), ((16, CELLS), F32)])(

time: 81.6 us -> 84.1 us (1.031)
  the two profiles are of different devices: /device:TPU:199 before, /device:TPU:512 now
where the time goes in v6:
time: 84.1 us; the launch traced here: 83.7 us
  blocking collectives  39.8 us (47%)
  starting transfers between devices  19.8 us (24%)
  waiting for transfers between devices  12.6 us (15%)
  Pallas kernels  11.4 us (14%)
    all_to_all x3, blocking collectives, local(): gathered = lax.all_to_all(partial_moments, 'vel', 0, 0)  39.8 us
    ppermute x3, starting transfers between devices, local(): got_b = lax.ppermute(msg_b, 'space', pairs_b)  14.1 us
    ppermute x3, waiting for transfers between devices, local(): got_b = lax.ppermute(msg_b, 'space', pairs_b)  12.5 us
    pallas_call x15, Pallas kernels, run(): pl.pallas_call(kernel, out_shape=shapes, in_specs=[HBM if hbm_in else VME...  11.4 us
    ppermute x3, starting transfers between devices, local(): got_a = lax.ppermute(msg_a, 'space', pairs_a)  5.76 us
  transfers between devices with their start and end apart: 6, of which 3 were waited for; matrix products, arithmetic and copies ran while one was open for 0% of the time, Pallas kernels for 4%

profile of v6, /device:TPU:512, one launch (start us, length us, event | category | flops | bytes accessed | tf_op | source)
XLA Modules:
  0.0 83.7 jit_solution(11274481958164699364)
XLA Ops:
  0.0 1.9 %shard_map.17 = (f32[16,128,128]{2,1,0:T(8,128)S(1)}, bf16[48,2048]{1,0:T(8,128)(2,1)S(1)}, f32[16,16,128]{2,1,0:T(8,128)S(1)}) custom-call(f32[8,256,128]{2,1,0:T(8,128)} %bitcast.10), custom_call_target="tpu_custom_call" | custom-call | tf_op jit(solution)/shard_map/pallas_call | solution.py:405
  1.9 16.5 %all_to_all.15.a_ref = f32[16,16,128]{2,1,0:T(8,128)S(1)} all-to-all(f32[16,16,128]{2,1,0:T(8,128)S(1)} %get-tuple-element.32), channel_id=1, replica_groups=mesh['space'=48,'vel'=16] {'vel'}, dimensions={0} | all-to-all | bytes 262144 | tf_op jit(solution)/shard_map/all_to_all | solution.py:433
  18.4 0.3 shard_map.18
  18.8 1.1 %shard_map.19 = (f32[16,128,128]{2,1,0:T(8,128)S(1)}, f32[8,32,128]{2,1,0:T(8,128)S(1)}) custom-call(f32[128,128]{1,0:T(8,128)S(1)} %get-tuple-element.34.f_ref, f32[16,128,128]{2,1,0:T(8,128)S(1)} %get-tuple-element.33.g_ref), custom_call_target="tpu_custom_call" | custom-call | tf_op jit(solution)/shard_map/pallas_call | solution.py:405
  19.9 1.9 %collective-permute-start = (f32[8,32,128]{2,1,0:T(8,128)S(1)}, f32[8,32,128]{2,1,0:T(8,128)S(1)}, u32[]{:S(2)}, u32[]{:S(2)}) collective-permute-start(f32[8,32,128]{2,1,0:T(8,128)S(1)} %get-tuple-element.38), channel_id=1, source_target_pairs={{0,16},{16,0},{32,48},{48,32},{64,80},{80,64},{96,112},{112,96},{1... | collective-permute-start | bytes 393224 | tf_op jit(solution)/shard_map/ppermute | solution.py:437
  21.8 5.9 %collective-permute-start.1 = (f32[8,32,128]{2,1,0:T(8,128)S(1)}, f32[8,32,128]{2,1,0:T(8,128)S(1)}, u32[]{:S(2)}, u32[]{:S(2)}) collective-permute-start(f32[8,32,128]{2,1,0:T(8,128)S(1)} %get-tuple-element.40), channel_id=1, source_target_pairs={{16,32},{48,64},{80,96},{112,128},{144,160},{176,192},{208,224},{2... | collective-permute-start | bytes 393224 | tf_op jit(solution)/shard_map/ppermute | solution.py:435
  27.8 0.9 %shard_map.20 = (f32[16,128,128]{2,1,0:T(8,128)S(1)}, f32[16,128]{1,0:T(8,128)S(1)}) custom-call(f32[16,128,128]{2,1,0:T(8,128)S(1)} %get-tuple-element.35.l_ref, bf16[48,2048]{1,0:T(8,128)(2,1)S(1)} %get-tuple-element.36.w_ref.refs_2_), custom_call_target="tpu_custom_call" | custom-call | tf_op jit(solution)/shard_map/pallas_call | solution.py:405
  28.7 0.0 collective-permute-done.refs_1_
  28.7 0.4 shard_map.21
  29.0 2.7 %collective-permute-done.1.refs_1_ = f32[8,32,128]{2,1,0:T(8,128)S(1)} collective-permute-done((f32[8,32,128]{2,1,0:T(8,128)S(1)}, f32[8,32,128]{2,1,0:T(8,128)S(1)}, u32[]{:S(2)}, u32[]{:S(2)}) %collective-permute-start.1) | collective-permute-done | bytes 131104 | tf_op jit(solution)/shard_map/ppermute | solution.py:435
  31.7 0.4 shard_map.22
  32.2 11.6 %all_to_all.16.a_ref = f32[16,16,128]{2,1,0:T(8,128)S(1)} all-to-all(f32[16,16,128]{2,1,0:T(8,128)S(1)} %get-tuple-element.41), channel_id=1, replica_groups=mesh['space'=48,'vel'=16] {'vel'}, dimensions={0} | all-to-all | bytes 262144 | tf_op jit(solution)/shard_map/all_to_all | solution.py:433
  43.8 0.3 shard_map.23
  44.1 1.2 %shard_map.24 = (f32[16,128,128]{2,1,0:T(8,128)S(1)}, f32[8,32,128]{2,1,0:T(8,128)S(1)}) custom-call(f32[128,128]{1,0:T(8,128)S(1)} %get-tuple-element.43.f_ref, f32[16,128,128]{2,1,0:T(8,128)S(1)} %get-tuple-element.42.g_ref, f32[8,32,128]{2,1,0:T(8,128)S(1)} %get-tuple-element.44.refs_0_, f32[8,32,128]{2,1,0:T(8,128)S(1)} %get-tuple-element.45.refs_1_), custom_call_target="tpu_custom_call" | custom-call | tf_op jit(solution)/shard_map/pallas_call | solution.py:405
  45.4 1.9 %collective-permute-start.2 = (f32[8,32,128]{2,1,0:T(8,128)S(1)}, f32[8,32,128]{2,1,0:T(8,128)S(1)}, u32[]{:S(2)}, u32[]{:S(2)}) collective-permute-start(f32[8,32,128]{2,1,0:T(8,128)S(1)} %get-tuple-element.48), channel_id=1, source_target_pairs={{0,16},{16,0},{32,48},{48,32},{64,80},{80,64},{96,112},{112,96},{1... | collective-permute-start | bytes 393224 | tf_op jit(solution)/shard_map/ppermute | solution.py:437
  47.3 4.6 %collective-permute-start.3 = (f32[8,32,128]{2,1,0:T(8,128)S(1)}, f32[8,32,128]{2,1,0:T(8,128)S(1)}, u32[]{:S(2)}, u32[]{:S(2)}) collective-permute-start(f32[8,32,128]{2,1,0:T(8,128)S(1)} %get-tuple-element.50), channel_id=1, source_target_pairs={{16,32},{48,64},{80,96},{112,128},{144,160},{176,192},{208,224},{2... | collective-permute-start | bytes 393224 | tf_op jit(solution)/shard_map/ppermute | solution.py:435
  51.9 0.9 %shard_map.25 = (f32[16,128,128]{2,1,0:T(8,128)S(1)}, f32[16,128]{1,0:T(8,128)S(1)}) custom-call(f32[16,128,128]{2,1,0:T(8,128)S(1)} %get-tuple-element.46.l_ref, bf16[48,2048]{1,0:T(8,128)(2,1)S(1)} %get-tuple-element.36.w_ref.refs_2_), custom_call_target="tpu_custom_call" | custom-call | tf_op jit(solution)/shard_map/pallas_call | solution.py:405
  52.8 0.0 collective-permute-done.2.refs_1_
  52.8 0.4 shard_map.26
  53.2 4.0 %collective-permute-done.3.refs_1_ = f32[8,32,128]{2,1,0:T(8,128)S(1)} collective-permute-done((f32[8,32,128]{2,1,0:T(8,128)S(1)}, f32[8,32,128]{2,1,0:T(8,128)S(1)}, u32[]{:S(2)}, u32[]{:S(2)}) %collective-permute-start.3) | collective-permute-done | bytes 131104 | tf_op jit(solution)/shard_map/ppermute | solution.py:435
  57.2 0.4 shard_map.27
  57.6 11.6 %all_to_all.17.a_ref = f32[16,16,128]{2,1,0:T(8,128)S(1)} all-to-all(f32[16,16,128]{2,1,0:T(8,128)S(1)} %get-tuple-element.51), channel_id=1, replica_groups=mesh['space'=48,'vel'=16] {'vel'}, dimensions={0} | all-to-all | bytes 262144 | tf_op jit(solution)/shard_map/all_to_all | solution.py:433
  69.2 0.3 shard_map.28
  69.6 1.2 %shard_map.29 = (f32[16,128,128]{2,1,0:T(8,128)S(1)}, f32[8,32,128]{2,1,0:T(8,128)S(1)}) custom-call(f32[128,128]{1,0:T(8,128)S(1)} %get-tuple-element.53.f_ref, f32[16,128,128]{2,1,0:T(8,128)S(1)} %get-tuple-element.52.g_ref, f32[8,32,128]{2,1,0:T(8,128)S(1)} %get-tuple-element.54.refs_0_, f32[8,32,128]{2,1,0:T(8,128)S(1)} %get-tuple-element.55.refs_1_), custom_call_target="tpu_custom_call" | custom-call | tf_op jit(solution)/shard_map/pallas_call | solution.py:405
  70.8 1.9 %collective-permute-start.4 = (f32[8,32,128]{2,1,0:T(8,128)S(1)}, f32[8,32,128]{2,1,0:T(8,128)S(1)}, u32[]{:S(2)}, u32[]{:S(2)}) collective-permute-start(f32[8,32,128]{2,1,0:T(8,128)S(1)} %get-tuple-element.57), channel_id=1, source_target_pairs={{0,16},{16,0},{32,48},{48,32},{64,80},{80,64},{96,112},{112,96},{1... | collective-permute-start | bytes 393224 | tf_op jit(solution)/shard_map/ppermute | solution.py:437
  72.7 3.5 %collective-permute-start.5 = (f32[8,32,128]{2,1,0:T(8,128)S(1)}, f32[8,32,128]{2,1,0:T(8,128)S(1)}, u32[]{:S(2)}, u32[]{:S(2)}) collective-permute-start(f32[8,32,128]{2,1,0:T(8,128)S(1)} %get-tuple-element.58), channel_id=1, source_target_pairs={{16,32},{48,64},{80,96},{112,128},{144,160},{176,192},{208,224},{2... | collective-permute-start | bytes 393224 | tf_op jit(solution)/shard_map/ppermute | solution.py:435
  76.2 0.6 shard_map.30.s_ref
  76.8 0.0 collective-permute-done.4.ra_ref
  76.8 5.8 %collective-permute-done.5.rb_ref = f32[8,32,128]{2,1,0:T(8,128)S(1)} collective-permute-done((f32[8,32,128]{2,1,0:T(8,128)S(1)}, f32[8,32,128]{2,1,0:T(8,128)S(1)}, u32[]{:S(2)}, u32[]{:S(2)}) %collective-permute-start.5) | collective-permute-done | bytes 131104 | tf_op jit(solution)/shard_map/ppermute | solution.py:435
  82.6 1.0 %shard_map.31 = f32[8,256,128]{2,1,0:T(8,128)} custom-call(f32[8,256,128]{2,1,0:T(8,128)S(1)} %shard_map.30.s_ref, f32[8,32,128]{2,1,0:T(8,128)S(1)} %collective-permute-done.4.ra_ref, f32[8,32,128]{2,1,0:T(8,128)S(1)} %collective-permute-done.5.rb_ref), custom_call_target="tpu_custom_call" | custom-call | tf_op jit(solution)/shard_map/pallas_call | solution.py:405
Async XLA Ops:
  19.9 8.8 %collective-permute-start = (f32[8,32,128]{2,1,0:T(8,128)S(1)}, f32[8,32,128]{2,1,0:T(8,128)S(1)}, u32[]{:S(2)}, u32[]{:S(2)}) collective-permute-start(f32[8,32,128]{2,1,0:T(8,128)S(1)} %get-tuple-element.38), channel_id=1, source_target_pairs={{0,16},{16,0},{32,48},{48,32},{64,80},{80,64},{96,112},{112,96},{1... | collective-permute-start | bytes 393224 | tf_op jit(solution)/shard_map/ppermute | solution.py:437
  21.8 9.9 %collective-permute-start.1 = (f32[8,32,128]{2,1,0:T(8,128)S(1)}, f32[8,32,128]{2,1,0:T(8,128)S(1)}, u32[]{:S(2)}, u32[]{:S(2)}) collective-permute-start(f32[8,32,128]{2,1,0:T(8,128)S(1)} %get-tuple-element.40), channel_id=1, source_target_pairs={{16,32},{48,64},{80,96},{112,128},{144,160},{176,192},{208,224},{2... | collective-permute-start | bytes 393224 | tf_op jit(solution)/shard_map/ppermute | solution.py:435
  45.4 7.4 %collective-permute-start.2 = (f32[8,32,128]{2,1,0:T(8,128)S(1)}, f32[8,32,128]{2,1,0:T(8,128)S(1)}, u32[]{:S(2)}, u32[]{:S(2)}) collective-permute-start(f32[8,32,128]{2,1,0:T(8,128)S(1)} %get-tuple-element.48), channel_id=1, source_target_pairs={{0,16},{16,0},{32,48},{48,32},{64,80},{80,64},{96,112},{112,96},{1... | collective-permute-start | bytes 393224 | tf_op jit(solution)/shard_map/ppermute | solution.py:437
  47.3 9.9 %collective-permute-start.3 = (f32[8,32,128]{2,1,0:T(8,128)S(1)}, f32[8,32,128]{2,1,0:T(8,128)S(1)}, u32[]{:S(2)}, u32[]{:S(2)}) collective-permute-start(f32[8,32,128]{2,1,0:T(8,128)S(1)} %get-tuple-element.50), channel_id=1, source_target_pairs={{16,32},{48,64},{80,96},{112,128},{144,160},{176,192},{208,224},{2... | collective-permute-start | bytes 393224 | tf_op jit(solution)/shard_map/ppermute | solution.py:435
  70.8 6.0 %collective-permute-start.4 = (f32[8,32,128]{2,1,0:T(8,128)S(1)}, f32[8,32,128]{2,1,0:T(8,128)S(1)}, u32[]{:S(2)}, u32[]{:S(2)}) collective-permute-start(f32[8,32,128]{2,1,0:T(8,128)S(1)} %get-tuple-element.57), channel_id=1, source_target_pairs={{0,16},{16,0},{32,48},{48,32},{64,80},{80,64},{96,112},{112,96},{1... | collective-permute-start | bytes 393224 | tf_op jit(solution)/shard_map/ppermute | solution.py:437
  72.7 9.9 %collective-permute-start.5 = (f32[8,32,128]{2,1,0:T(8,128)S(1)}, f32[8,32,128]{2,1,0:T(8,128)S(1)}, u32[]{:S(2)}, u32[]{:S(2)}) collective-permute-start(f32[8,32,128]{2,1,0:T(8,128)S(1)} %get-tuple-element.58), channel_id=1, source_target_pairs={{16,32},{48,64},{80,96},{112,128},{144,160},{176,192},{208,224},{2... | collective-permute-start | bytes 393224 | tf_op jit(solution)/shard_map/ppermute | solution.py:435

commit v7 on v6

--- a/solution.py
+++ b/solution.py
@@ -81,6 +81,11 @@
             piece = product[j * n : (j + 1) * n, :]
             total = piece if total is None else total + piece
     return total
+
+
+def in_a_row(m_ref, moments):
+    for k in range(13):
+        m_ref[:, k * CELLS : (k + 1) * CELLS] = moments[k : k + 1, :]
 
 
 def xabs_here():
@@ -125,7 +130,7 @@
                 for k in range(8):
                     block, half = group * 4 + k // 2, k % 2
                     g_ref[half * 8 + block, pl.ds(yz * 8, 8), :] = turned[k]
-    m_ref[...] = jnp.broadcast_to(weighed(w_ref, wide(g_ref, slice(None)))[None], m_ref.shape)
+    in_a_row(m_ref, weighed(w_ref, wide(g_ref, slice(None))))
 
 
 def cell_fields(m):
@@ -200,7 +205,7 @@
     total = a_ref[0]
     for peer in range(1, a_ref.shape[0]):
         total = total + a_ref[peer]
-    fields = cell_fields([total[k : k + 1, :] for k in range(13)])
+    fields = cell_fields([total[:, k * CELLS : (k + 1) * CELLS] for k in range(13)])
     for k, value in enumerate(fields):
         f_ref[k : k + 1, :] = value
     f_ref[...] = jnp.transpose(f_ref[...])
@@ -353,7 +358,10 @@
     spread = (source // 2 * 8 + source % 2 + 6 * (1 - half) == cell).astype(jnp.bfloat16)
     thirds = jnp.dot(jnp.concatenate(split(sums)), spread, preferred_element_type=jnp.float32)
     total = mi_ref[...] + ((thirds[32:48, :] + thirds[16:32, :]) + thirds[0:16, :])
-    m_ref[...] = total if len(m_ref.shape) == 2 else jnp.broadcast_to(total[None], m_ref.shape)
+    if m_ref.shape == total.shape:
+        m_ref[...] = total
+    else:
+        in_a_row(m_ref, total)
 
 
 def chip_edge_kernel(*refs):
@@ -389,7 +397,7 @@
 F32, BF16 = jnp.float32, jnp.bfloat16
 HBM = pl.BlockSpec(memory_space=pltpu.HBM)
 GRID, MESSAGE, STORED = (16, CELLS, 128), (8, 32, 128), (LAYERS, 256, 128)
-EVERYWHERE = (16, 16, CELLS)
+ROW = (1, 13 * CELLS)
 EDGES = [pltpu.VMEM(MESSAGE, F32), pltpu.VMEM(MESSAGE, F32)]
 
 
@@ -424,13 +432,14 @@
     pairs_b = pairs_b + [(j, i) for i, j in pairs_b]
     g, weights, partial_moments = call(
         first_kernel,
-        [(GRID, F32), ((48, 2048), BF16), (EVERYWHERE, F32)],
+        [(GRID, F32), ((48, 2048), BF16), (ROW, F32)],
         [pltpu.VMEM(STORED, F32), pltpu.SemaphoreType.DMA((8,))],
         hbm_in=True,
     )(stored.reshape(STORED))
     sides = ()
     for step in range(STEPS):
-        gathered = lax.all_to_all(partial_moments, "vel", 0, 0)
+        everywhere = jnp.broadcast_to(partial_moments[None], (lax.axis_size("vel"),) + ROW)
+        gathered = lax.all_to_all(everywhere, "vel", 0, 0)
         fields, msg_b = call(outer_kernel, [((128, 128), F32), (MESSAGE, F32)])(gathered, g)
         got_b = lax.ppermute(msg_b, "space", pairs_b)
         moved, msg_a = call(inner_kernel, [(GRID, F32), (MESSAGE, F32)])(fields, g, *sides)
@@ -441,9 +450,7 @@
             )
             outs = [(MESSAGE, F32), ((16, CELLS), F32)]
             near, inside = call(chip_edge_kernel, outs)(inside, got_a, weights)
-            distant, partial_moments = call(far_edge_kernel, [(MESSAGE, F32), (EVERYWHERE, F32)])(
-                inside, got_b, weights
-            )
+            distant, partial_moments = call(far_edge_kernel, [(MESSAGE, F32), (ROW, F32)])(inside, got_b, weights)
             sides = (near, distant)
         else:
             (swept,) = call(last_sweep_kernel, [(STORED, F32)], [pltpu.VMEM(GRID, F32)])(moved)

time: 84.1 us -> 83.8 us (level)
  no operation moved by 1% of the time
where the time goes in v7:
time: 83.8 us; the launch traced here: 83.4 us
  blocking collectives  39.2 us (47%)
  starting transfers between devices  19.7 us (24%)
  waiting for transfers between devices  12.6 us (15%)
  Pallas kernels  11.4 us (14%)
    all_to_all x3, blocking collectives, local(): gathered = lax.all_to_all(everywhere, 'vel', 0, 0)  39.2 us
    ppermute x3, starting transfers between devices, local(): got_b = lax.ppermute(msg_b, 'space', pairs_b)  14 us
    ppermute x3, waiting for transfers between devices, local(): got_b = lax.ppermute(msg_b, 'space', pairs_b)  12.6 us
    pallas_call x15, Pallas kernels, run(): pl.pallas_call(kernel, out_shape=shapes, in_specs=[HBM if hbm_in else VME...  11.4 us
    ppermute x3, starting transfers between devices, local(): got_a = lax.ppermute(msg_a, 'space', pairs_a)  5.76 us
  transfers between devices with their start and end apart: 6, of which 3 were waited for; matrix products, arithmetic and copies ran while one was open for 0% of the time, Pallas kernels for 4%

profile of v7, /device:TPU:512, one launch (start us, length us, event | category | flops | bytes accessed | tf_op | source)
XLA Modules:
  0.0 83.4 jit_solution(17166993437456195855)
XLA Ops:
  0.0 1.9 %shard_map.17 = (f32[16,128,128]{2,1,0:T(8,128)S(1)}, bf16[48,2048]{1,0:T(8,128)(2,1)S(1)}, f32[1,1664]{1,0:T(1,128)S(1)}) custom-call(f32[8,256,128]{2,1,0:T(8,128)} %bitcast.10), custom_call_target="tpu_custom_call" | custom-call | tf_op jit(solution)/shard_map/pallas_call | solution.py:413
  1.9 0.1 broadcast_in_dim.25
  2.0 16.5 %all_to_all.15.a_ref = f32[16,1,1664]{2,1,0:T(1,128)S(1)} all-to-all(f32[16,1,1664]{2,1,0:T(1,128)S(1)} %broadcast_in_dim.25), channel_id=1, replica_groups=mesh['space'=48,'vel'=16] {'vel'}, dimensions={0} | all-to-all | bytes 212992 | tf_op jit(solution)/shard_map/all_to_all | solution.py:442
  18.5 0.3 shard_map.18
  18.9 1.1 %shard_map.19 = (f32[16,128,128]{2,1,0:T(8,128)S(1)}, f32[8,32,128]{2,1,0:T(8,128)S(1)}) custom-call(f32[128,128]{1,0:T(8,128)S(1)} %get-tuple-element.34.f_ref, f32[16,128,128]{2,1,0:T(8,128)S(1)} %get-tuple-element.33.g_ref), custom_call_target="tpu_custom_call" | custom-call | tf_op jit(solution)/shard_map/pallas_call | solution.py:413
  20.0 1.9 %collective-permute-start = (f32[8,32,128]{2,1,0:T(8,128)S(1)}, f32[8,32,128]{2,1,0:T(8,128)S(1)}, u32[]{:S(2)}, u32[]{:S(2)}) collective-permute-start(f32[8,32,128]{2,1,0:T(8,128)S(1)} %get-tuple-element.38), channel_id=1, source_target_pairs={{0,16},{16,0},{32,48},{48,32},{64,80},{80,64},{96,112},{112,96},{1... | collective-permute-start | bytes 393224 | tf_op jit(solution)/shard_map/ppermute | solution.py:446
  21.9 5.9 %collective-permute-start.1 = (f32[8,32,128]{2,1,0:T(8,128)S(1)}, f32[8,32,128]{2,1,0:T(8,128)S(1)}, u32[]{:S(2)}, u32[]{:S(2)}) collective-permute-start(f32[8,32,128]{2,1,0:T(8,128)S(1)} %get-tuple-element.40), channel_id=1, source_target_pairs={{16,32},{48,64},{80,96},{112,128},{144,160},{176,192},{208,224},{2... | collective-permute-start | bytes 393224 | tf_op jit(solution)/shard_map/ppermute | solution.py:444
  27.9 0.9 %shard_map.20 = (f32[16,128,128]{2,1,0:T(8,128)S(1)}, f32[16,128]{1,0:T(8,128)S(1)}) custom-call(f32[16,128,128]{2,1,0:T(8,128)S(1)} %get-tuple-element.35.l_ref, bf16[48,2048]{1,0:T(8,128)(2,1)S(1)} %get-tuple-element.36.w_ref.refs_2_), custom_call_target="tpu_custom_call" | custom-call | tf_op jit(solution)/shard_map/pallas_call | solution.py:413
  28.7 0.0 collective-permute-done.refs_1_
  28.7 0.4 shard_map.21
  29.1 2.7 %collective-permute-done.1.refs_1_ = f32[8,32,128]{2,1,0:T(8,128)S(1)} collective-permute-done((f32[8,32,128]{2,1,0:T(8,128)S(1)}, f32[8,32,128]{2,1,0:T(8,128)S(1)}, u32[]{:S(2)}, u32[]{:S(2)}) %collective-permute-start.1) | collective-permute-done | bytes 131104 | tf_op jit(solution)/shard_map/ppermute | solution.py:444
  31.8 0.4 shard_map.22
  32.3 0.1 broadcast_in_dim.27
  32.3 11.4 %all_to_all.16.a_ref = f32[16,1,1664]{2,1,0:T(1,128)S(1)} all-to-all(f32[16,1,1664]{2,1,0:T(1,128)S(1)} %broadcast_in_dim.27), channel_id=1, replica_groups=mesh['space'=48,'vel'=16] {'vel'}, dimensions={0} | all-to-all | bytes 212992 | tf_op jit(solution)/shard_map/all_to_all | solution.py:442
  43.7 0.3 shard_map.23
  44.0 1.2 %shard_map.24 = (f32[16,128,128]{2,1,0:T(8,128)S(1)}, f32[8,32,128]{2,1,0:T(8,128)S(1)}) custom-call(f32[128,128]{1,0:T(8,128)S(1)} %get-tuple-element.43.f_ref, f32[16,128,128]{2,1,0:T(8,128)S(1)} %get-tuple-element.42.g_ref, f32[8,32,128]{2,1,0:T(8,128)S(1)} %get-tuple-element.44.refs_0_, f32[8,32,128]{2,1,0:T(8,128)S(1)} %get-tuple-element.45.refs_1_), custom_call_target="tpu_custom_call" | custom-call | tf_op jit(solution)/shard_map/pallas_call | solution.py:413
  45.3 1.9 %collective-permute-start.2 = (f32[8,32,128]{2,1,0:T(8,128)S(1)}, f32[8,32,128]{2,1,0:T(8,128)S(1)}, u32[]{:S(2)}, u32[]{:S(2)}) collective-permute-start(f32[8,32,128]{2,1,0:T(8,128)S(1)} %get-tuple-element.48), channel_id=1, source_target_pairs={{0,16},{16,0},{32,48},{48,32},{64,80},{80,64},{96,112},{112,96},{1... | collective-permute-start | bytes 393224 | tf_op jit(solution)/shard_map/ppermute | solution.py:446
  47.2 4.6 %collective-permute-start.3 = (f32[8,32,128]{2,1,0:T(8,128)S(1)}, f32[8,32,128]{2,1,0:T(8,128)S(1)}, u32[]{:S(2)}, u32[]{:S(2)}) collective-permute-start(f32[8,32,128]{2,1,0:T(8,128)S(1)} %get-tuple-element.50), channel_id=1, source_target_pairs={{16,32},{48,64},{80,96},{112,128},{144,160},{176,192},{208,224},{2... | collective-permute-start | bytes 393224 | tf_op jit(solution)/shard_map/ppermute | solution.py:444
  51.8 0.9 %shard_map.25 = (f32[16,128,128]{2,1,0:T(8,128)S(1)}, f32[16,128]{1,0:T(8,128)S(1)}) custom-call(f32[16,128,128]{2,1,0:T(8,128)S(1)} %get-tuple-element.46.l_ref, bf16[48,2048]{1,0:T(8,128)(2,1)S(1)} %get-tuple-element.36.w_ref.refs_2_), custom_call_target="tpu_custom_call" | custom-call | tf_op jit(solution)/shard_map/pallas_call | solution.py:413
  52.7 0.0 collective-permute-done.2.refs_1_
  52.7 0.4 shard_map.26
  53.1 4.0 %collective-permute-done.3.refs_1_ = f32[8,32,128]{2,1,0:T(8,128)S(1)} collective-permute-done((f32[8,32,128]{2,1,0:T(8,128)S(1)}, f32[8,32,128]{2,1,0:T(8,128)S(1)}, u32[]{:S(2)}, u32[]{:S(2)}) %collective-permute-start.3) | collective-permute-done | bytes 131104 | tf_op jit(solution)/shard_map/ppermute | solution.py:444
  57.1 0.4 shard_map.27
  57.5 0.1 broadcast_in_dim.29
  57.6 11.4 %all_to_all.17.a_ref = f32[16,1,1664]{2,1,0:T(1,128)S(1)} all-to-all(f32[16,1,1664]{2,1,0:T(1,128)S(1)} %broadcast_in_dim.29), channel_id=1, replica_groups=mesh['space'=48,'vel'=16] {'vel'}, dimensions={0} | all-to-all | bytes 212992 | tf_op jit(solution)/shard_map/all_to_all | solution.py:442
  69.0 0.3 shard_map.28
  69.3 1.2 %shard_map.29 = (f32[16,128,128]{2,1,0:T(8,128)S(1)}, f32[8,32,128]{2,1,0:T(8,128)S(1)}) custom-call(f32[128,128]{1,0:T(8,128)S(1)} %get-tuple-element.53.f_ref, f32[16,128,128]{2,1,0:T(8,128)S(1)} %get-tuple-element.52.g_ref, f32[8,32,128]{2,1,0:T(8,128)S(1)} %get-tuple-element.54.refs_0_, f32[8,32,128]{2,1,0:T(8,128)S(1)} %get-tuple-element.55.refs_1_), custom_call_target="tpu_custom_call" | custom-call | tf_op jit(solution)/shard_map/pallas_call | solution.py:413
  70.5 1.9 %collective-permute-start.4 = (f32[8,32,128]{2,1,0:T(8,128)S(1)}, f32[8,32,128]{2,1,0:T(8,128)S(1)}, u32[]{:S(2)}, u32[]{:S(2)}) collective-permute-start(f32[8,32,128]{2,1,0:T(8,128)S(1)} %get-tuple-element.57), channel_id=1, source_target_pairs={{0,16},{16,0},{32,48},{48,32},{64,80},{80,64},{96,112},{112,96},{1... | collective-permute-start | bytes 393224 | tf_op jit(solution)/shard_map/ppermute | solution.py:446
  72.5 3.4 %collective-permute-start.5 = (f32[8,32,128]{2,1,0:T(8,128)S(1)}, f32[8,32,128]{2,1,0:T(8,128)S(1)}, u32[]{:S(2)}, u32[]{:S(2)}) collective-permute-start(f32[8,32,128]{2,1,0:T(8,128)S(1)} %get-tuple-element.58), channel_id=1, source_target_pairs={{16,32},{48,64},{80,96},{112,128},{144,160},{176,192},{208,224},{2... | collective-permute-start | bytes 393224 | tf_op jit(solution)/shard_map/ppermute | solution.py:444
  75.9 0.6 shard_map.30.s_ref
  76.5 0.0 collective-permute-done.4.ra_ref
  76.5 5.9 %collective-permute-done.5.rb_ref = f32[8,32,128]{2,1,0:T(8,128)S(1)} collective-permute-done((f32[8,32,128]{2,1,0:T(8,128)S(1)}, f32[8,32,128]{2,1,0:T(8,128)S(1)}, u32[]{:S(2)}, u32[]{:S(2)}) %collective-permute-start.5) | collective-permute-done | bytes 131104 | tf_op jit(solution)/shard_map/ppermute | solution.py:444
  82.4 1.0 %shard_map.31 = f32[8,256,128]{2,1,0:T(8,128)} custom-call(f32[8,256,128]{2,1,0:T(8,128)S(1)} %shard_map.30.s_ref, f32[8,32,128]{2,1,0:T(8,128)S(1)} %collective-permute-done.4.ra_ref, f32[8,32,128]{2,1,0:T(8,128)S(1)} %collective-permute-done.5.rb_ref), custom_call_target="tpu_custom_call" | custom-call | tf_op jit(solution)/shard_map/pallas_call | solution.py:413
  (3 shorter events, 0.1 us)
Async XLA Ops:
  20.0 8.8 %collective-permute-start = (f32[8,32,128]{2,1,0:T(8,128)S(1)}, f32[8,32,128]{2,1,0:T(8,128)S(1)}, u32[]{:S(2)}, u32[]{:S(2)}) collective-permute-start(f32[8,32,128]{2,1,0:T(8,128)S(1)} %get-tuple-element.38), channel_id=1, source_target_pairs={{0,16},{16,0},{32,48},{48,32},{64,80},{80,64},{96,112},{112,96},{1... | collective-permute-start | bytes 393224 | tf_op jit(solution)/shard_map/ppermute | solution.py:446
  21.9 9.9 %collective-permute-start.1 = (f32[8,32,128]{2,1,0:T(8,128)S(1)}, f32[8,32,128]{2,1,0:T(8,128)S(1)}, u32[]{:S(2)}, u32[]{:S(2)}) collective-permute-start(f32[8,32,128]{2,1,0:T(8,128)S(1)} %get-tuple-element.40), channel_id=1, source_target_pairs={{16,32},{48,64},{80,96},{112,128},{144,160},{176,192},{208,224},{2... | collective-permute-start | bytes 393224 | tf_op jit(solution)/shard_map/ppermute | solution.py:444
  45.3 7.5 %collective-permute-start.2 = (f32[8,32,128]{2,1,0:T(8,128)S(1)}, f32[8,32,128]{2,1,0:T(8,128)S(1)}, u32[]{:S(2)}, u32[]{:S(2)}) collective-permute-start(f32[8,32,128]{2,1,0:T(8,128)S(1)} %get-tuple-element.48), channel_id=1, source_target_pairs={{0,16},{16,0},{32,48},{48,32},{64,80},{80,64},{96,112},{112,96},{1... | collective-permute-start | bytes 393224 | tf_op jit(solution)/shard_map/ppermute | solution.py:446
  47.2 9.9 %collective-permute-start.3 = (f32[8,32,128]{2,1,0:T(8,128)S(1)}, f32[8,32,128]{2,1,0:T(8,128)S(1)}, u32[]{:S(2)}, u32[]{:S(2)}) collective-permute-start(f32[8,32,128]{2,1,0:T(8,128)S(1)} %get-tuple-element.50), channel_id=1, source_target_pairs={{16,32},{48,64},{80,96},{112,128},{144,160},{176,192},{208,224},{2... | collective-permute-start | bytes 393224 | tf_op jit(solution)/shard_map/ppermute | solution.py:444
  70.5 5.9 %collective-permute-start.4 = (f32[8,32,128]{2,1,0:T(8,128)S(1)}, f32[8,32,128]{2,1,0:T(8,128)S(1)}, u32[]{:S(2)}, u32[]{:S(2)}) collective-permute-start(f32[8,32,128]{2,1,0:T(8,128)S(1)} %get-tuple-element.57), channel_id=1, source_target_pairs={{0,16},{16,0},{32,48},{48,32},{64,80},{80,64},{96,112},{112,96},{1... | collective-permute-start | bytes 393224 | tf_op jit(solution)/shard_map/ppermute | solution.py:446
  72.5 9.9 %collective-permute-start.5 = (f32[8,32,128]{2,1,0:T(8,128)S(1)}, f32[8,32,128]{2,1,0:T(8,128)S(1)}, u32[]{:S(2)}, u32[]{:S(2)}) collective-permute-start(f32[8,32,128]{2,1,0:T(8,128)S(1)} %get-tuple-element.58), channel_id=1, source_target_pairs={{16,32},{48,64},{80,96},{112,128},{144,160},{176,192},{208,224},{2... | collective-permute-start | bytes 393224 | tf_op jit(solution)/shard_map/ppermute | solution.py:444
